TPU v7x, 256 devices: a whole 4x4x8 slice. The times are simulated.
256 devices in a mesh: seq: 16 (over y, z_lo, core), head: 16 (over z_hi, x).
Axes of the slice: x: 4, y: 4, z: 8 (z_hi: 4, z_lo: 2; z = z_hi * 2 + z_lo), core: 2. Of those that a mesh axis runs over, the one named last changes fastest.
Arguments:
- query_latent: bfloat16 [4096, 128, 576], P('seq', 'head'), may hold values from -6 to 6
- key_latent: bfloat16 [2048, 576], P('seq'), may hold values from -6 to 6
- normalizer: float32 [4096, 128], P('seq', 'head'), may hold values from 7 to 9
- index_query: bfloat16 [4096, 64, 128], P('seq', 'head'), may hold values from -20 to 20
- index_key: bfloat16 [2048, 128], P('seq'), may hold values from -6.5 to 6.5
- index_weight: float32 [4096, 64], P('seq', 'head'), may hold values from 0.05 to 0.5
- kept: int32 [32, 16], P('seq'), may hold values from 0 to 1, as said below
Outputs:
- index_query_grad: bfloat16 [4096, 64, 128], P('seq', 'head')
- index_key_grad: float32 [2048, 128], P('seq')
Inputs may be any that keep to these rules, and one draw needn't show every extreme that they name: `kept`: every query tile keeps the key tile whose position matches its own block of 256 queries.
All inputs are finite; a program needn't handle non-finite values.
Results may differ from a plain program's by a relative error of at most 0.009.
Values may be sent and summed in bfloat16 or wider, within the bound.
No kernel may reach another device: no remote copies, remote signals or barrier semaphores. Data moves between devices by JAX's collectives and lax.ppermute only.
A program may use at most 64 MiB of HBM per device.

v0:
```python
import functools

import jax
import jax.numpy as jnp
from jax import lax
from jax.experimental import pallas as pl
from jax.experimental.pallas import tpu as pltpu
from jax.sharding import PartitionSpec as P


attn_scale = 192.0 ** (-0.5)
LOG2E = 1.4426950408889634
STEPS = (1, 3, 2)
GROUPS = ((0, 1), (2, 3))
f32 = jnp.float32
bf16 = jnp.bfloat16
VM = pl.BlockSpec(memory_space=pltpu.VMEM)
SM = pl.BlockSpec(memory_space=pltpu.SMEM)

ROW_X = [[zh * 4 + x for x in range(4)] for zh in range(4)]
ROW_ZH = [[zh * 4 + x for zh in range(4)] for x in range(4)]
YZX = [
    [(y * 4 + z * 2 + c) * 16 + zh * 4 + x for y in range(4) for z in range(2) for x in range(4)]
    for zh in range(4)
    for c in range(2)
]


def along_y(value, d):
    return lax.ppermute(value, "seq", [(i, (i + 4 * d) % 16) for i in range(16)])


def along_z(value):
    return lax.ppermute(value, "seq", [(i, i ^ 2) for i in range(16)])


def other_core(value):
    return lax.ppermute(value, "seq", [(i, i ^ 1) for i in range(16)])


def exchanged(value, axis, groups=None):
    return lax.all_to_all(value, axis, 0, 0, tiled=True, axis_index_groups=groups)


def sds(shape, dtype):
    return jax.ShapeDtypeStruct(shape, dtype)


def call(body, outs, specs, **more):
    return pl.pallas_call(
        body,
        out_shape=outs,
        in_specs=specs,
        out_specs=jax.tree.map(lambda _: VM, outs),
        **more,
    )


def query_body(q_ref, lse_ref, out_ref, wide):
    h = pl.program_id(0)
    width = q_ref.shape[1]
    value = lse_ref[pl.ds(h, 1), :] * (-1.0 / attn_scale)
    p0 = value.astype(bf16).astype(f32)
    p1 = (value - p0).astype(bf16).astype(f32)
    p2 = value - p0 - p1
    row = lax.broadcasted_iota(jnp.int32, (wide.shape[0] - width, wide.shape[1]), 0)
    more = jnp.where(row == 0, p0, jnp.where(row == 1, p1, jnp.where(row == 2, p2, 0.0)))
    wide[0:width, :] = q_ref[0]
    wide[width:, :] = more.astype(bf16)
    out_ref[0] = wide[...].T


def wide_queries(query, normalizer):
    heads, width, rows = query.shape
    return pl.pallas_call(
        query_body,
        grid=(heads,),
        out_shape=sds((heads, rows, 640), bf16),
        in_specs=[
            pl.BlockSpec((1, width, rows), lambda h: (h, 0, 0)),
            pl.BlockSpec((heads, rows), lambda h: (0, 0)),
        ],
        out_specs=pl.BlockSpec((1, rows, 640), lambda h: (h, 0, 0)),
        scratch_shapes=[pltpu.VMEM((640, rows), bf16)],
        name="wide_queries",
    )(query, normalizer)


def score_body(q_ref, *refs):
    k_refs, out_ref, keys = refs[:-2], refs[-2], refs[-1]
    k_refs = [ref for ref in k_refs if len(ref.shape) == 3]
    n = pl.program_id(0)
    heads, rows, _ = q_ref.shape
    width = k_refs[0].shape[1] - 128

    @pl.when(n == 0)
    def _():
        row = lax.broadcasted_iota(jnp.int32, (keys.shape[0] - width, 256), 0)
        keys[width:, :] = jnp.where(row < 3, 1.0, 0.0).astype(bf16)

    for i, ref in enumerate(k_refs):

        @pl.when(n == i)
        def _():
            for u in range(2):
                keys[0:width, u * 128 : u * 128 + 128] = ref[u, 128:, :]

    total = None
    for h in range(0, heads, 2):
        both = q_ref[h : h + 2].reshape(2 * rows, q_ref.shape[2])
        s = jnp.dot(both, keys[...], preferred_element_type=f32)
        p = jnp.exp2(s * (attn_scale * LOG2E))
        p = p[:rows] + p[rows:]
        total = p if total is None else total + p
    for x in range(4):
        for zh in range(4):
            at, begin = (x * 4 + zh) * 16, (zh * 4 + x) * 16
            out_ref[at : at + 16, :] = total[begin : begin + 16].astype(bf16)


def scores(query, pairs, into, begin):
    _, rows, wide = query.shape
    whole = lambda shape: pl.BlockSpec(shape, lambda n: (0,) * len(shape))
    more = () if into is None else (into,)
    return pl.pallas_call(
        score_body,
        grid=(len(pairs),),
        out_shape=sds((rows, 2048), bf16),
        in_specs=[whole(query.shape)]
        + [whole(p.shape) for p in pairs]
        + [pl.BlockSpec(memory_space=pl.ANY) for _ in more],
        out_specs=pl.BlockSpec((rows, 256), lambda n: (0, n + begin)),
        scratch_shapes=[pltpu.VMEM((wide, 256), bf16)],
        input_output_aliases={1 + len(pairs): 0} if more else {},
        name="scores",
    )(query, *pairs, *more)


def weight_column(q_ref, j):
    row = jnp.sum(q_ref[j, 64:80, :].astype(f32), axis=0, keepdims=True)[:, 0:64]
    eye = lax.broadcasted_iota(jnp.int32, (64, 64), 0) == lax.broadcasted_iota(jnp.int32, (64, 64), 1)
    return jnp.sum(jnp.where(eye, row, 0.0), axis=1, keepdims=True)


def slot_tile(at_ref, slot):
    k, v, u = slot // 4, slot // 2 % 2, slot % 2
    y = lax.rem(at_ref[1] + ((0,) + STEPS)[k], 4)
    z = at_ref[2] if u == 0 else 1 - at_ref[2]
    c = at_ref[3] if v == 0 else 1 - at_ref[3]
    return y * 4 + z * 2 + c


def allowed(at_ref, kept_ref):
    half = jnp.where(at_ref[0] >= 8, 1, 0)
    flags = [
        jnp.full((16, 128), kept_ref[half, slot_tile(at_ref, slot)], jnp.int32) for slot in range(16)
    ]
    return jnp.concatenate(flags, axis=1) > 0


KEY_SPEC = pl.BlockSpec((2, 128, 128), lambda i: (0, 0, 0))


def gather_keys(k_refs, keys):
    for slot in range(16):
        keys[slot * 128 : slot * 128 + 128, :] = k_refs[slot // 2][slot % 2]


NT = (((1,), (1,)), ((), ()))
TN = (((0,), (0,)), ((), ()))


def index_body(scale, at_ref, kept_ref, q_ref, *refs):
    k_refs, (prob_ref, z_ref, keys, acc) = refs[:8], refs[8:]
    gather_keys(k_refs, keys)
    acc[...] = jnp.zeros_like(acc)

    @pl.loop(0, 4)
    def _(g):
        rows = q_ref[pl.ds(4 * g, 4), 0:64, :].reshape(256, 128)
        z = lax.dot_general(rows, keys[...], NT, preferred_element_type=f32)
        z_ref[g] = z.astype(bf16)
        part = None
        for a in range(4):
            weight = weight_column(q_ref, 4 * g + a) * scale
            term = jnp.maximum(z[a * 64 : a * 64 + 64], 0.0) * weight
            part = term if part is None else part + term
        acc[...] += part

    pick = (
        lax.broadcasted_iota(jnp.int32, (16, 64), 1) // 4
        == lax.broadcasted_iota(jnp.int32, (16, 64), 0)
    ).astype(f32)
    logit = jnp.dot(pick, acc[...], precision=lax.Precision.HIGHEST, preferred_element_type=f32)
    keep = allowed(at_ref, kept_ref)
    top = jnp.max(jnp.where(keep, logit, -jnp.inf), axis=1, keepdims=True)
    expo = jnp.where(keep, jnp.exp(jnp.where(keep, logit, top) - top), 0.0)
    prob_ref[...] = expo / jnp.sum(expo, axis=1, keepdims=True)


def index_forward(at, kept, queries, keys, scale):
    return call(
        functools.partial(index_body, scale),
        (sds((16, 2048), f32), sds((4, 256, 2048), bf16)),
        [SM, SM, VM] + [KEY_SPEC] * 8,
        grid=(1,),
        scratch_shapes=[pltpu.VMEM((2048, 128), bf16), pltpu.VMEM((64, 2048), f32)],
        name="index_forward",
    )(at, kept, queries, *keys)


def fill_dz(g, wide, z_ref, q_ref, dz):
    for a in range(4):
        at = a * 64
        dz[at : at + 64, :] = jnp.where(
            z_ref[g, at : at + 64, :].astype(f32) > 0.0, wide * weight_column(q_ref, 4 * g + a), 0.0
        ).astype(bf16)


def repeated(grad):
    pick = (
        lax.broadcasted_iota(jnp.int32, (64, 16), 0) // 4
        == lax.broadcasted_iota(jnp.int32, (64, 16), 1)
    ).astype(f32)
    return jnp.dot(pick, grad, precision=lax.Precision.HIGHEST, preferred_element_type=f32)


def back_body(scale, at_ref, kept_ref, prob_ref, z_ref, q_ref, *refs):
    k_refs, refs = refs[:8], refs[8:]
    sums, (own_ref, send_ref, dq_ref, keys, grad, dz, dk, wide) = refs[:-8], refs[-8:]
    gather_keys(k_refs, keys)
    begin = 0
    for ref in sums:
        total = ref[0].astype(f32)
        for j in range(1, ref.shape[0]):
            total += ref[j].astype(f32)
        grad[:, begin : begin + ref.shape[2]] = total
        begin += ref.shape[2]
    head_sum = jnp.where(allowed(at_ref, kept_ref), grad[...], 0.0)
    wide[...] = repeated(prob_ref[...] - head_sum / jnp.sum(head_sum, axis=1, keepdims=True))
    dk[...] = jnp.zeros_like(dk)

    @pl.loop(0, 4)
    def _(g):
        fill_dz(g, wide[...], z_ref, q_ref, dz)
        rows = q_ref[pl.ds(4 * g, 4), 0:64, :].reshape(256, 128)
        dk[...] += lax.dot_general(rows, dz[...], TN, preferred_element_type=f32)
        dq = jnp.dot(dz[...], keys[...], preferred_element_type=f32) * scale
        dq_ref[pl.ds(4 * g, 4)] = dq.astype(bf16).reshape(4, 64, 128)

    for slot in range(16):
        tile = dk[:, slot * 128 : slot * 128 + 128] * scale
        place = lax.div(slot_tile(at_ref, slot), 2)
        if slot // 2 % 2 == 0:
            own_ref[place] = tile
        else:
            send_ref[place] = tile.astype(bf16)


def index_backward(at, kept, prob, z, queries, keys, sums, scale):
    return call(
        functools.partial(back_body, scale),
        (sds((8, 128, 128), f32), sds((8, 128, 128), bf16), sds((16, 64, 128), bf16)),
        [SM, SM] + [VM] * 3 + [KEY_SPEC] * 8 + [VM] * len(sums),
        grid=(1,),
        scratch_shapes=[
            pltpu.VMEM((2048, 128), bf16),
            pltpu.VMEM((16, 2048), f32),
            pltpu.VMEM((256, 2048), bf16),
            pltpu.VMEM((128, 2048), f32),
            pltpu.VMEM((64, 2048), f32),
        ],
        name="index_backward",
    )(at, kept, prob, z, queries, *keys, *sums)


def local(query_latent, key_latent, normalizer, index_query, index_key, index_weight, kept):
    index_scale = index_query.shape[2] ** (-0.5)
    head = lax.axis_index("head")
    seq = lax.axis_index("seq")
    at = jnp.stack([head, seq // 4, seq // 2 % 2, seq % 2]).astype(jnp.int32)

    tile = jnp.concatenate([index_key, key_latent.T], axis=0)
    other = along_z(tile)
    pairs = [jnp.stack([tile, other])]
    for d in STEPS:
        pairs.append(along_y(pairs[0], -d))
    keys = []
    for pair in pairs:
        keys += [pair, other_core(pair)]

    w0 = lax.reduce_precision(index_weight, 8, 7)
    w1 = lax.reduce_precision(index_weight - w0, 8, 7)
    w2 = index_weight - w0 - w1
    weight = jnp.stack([w.reshape(16, 64) for w in (w0, w1, w2)], axis=1).astype(bf16)
    weight = jnp.pad(weight, ((0, 0), (0, 13), (0, 64)))
    queries = jnp.concatenate([index_query.reshape(16, 64, 128), weight], axis=1)
    queries = exchanged(queries, "head")

    query = wide_queries(jnp.transpose(query_latent, (1, 2, 0)), normalizer.T)
    part, begin = None, 0
    for group in GROUPS:
        pieces = [p for k in group for p in keys[2 * k : 2 * k + 2]]
        part = scores(query, pieces, part, begin)
        begin += len(pieces)
    part = exchanged(part.reshape(4, 64, 2048), "head", ROW_X)
    part = jnp.sum(part.astype(f32), axis=0).astype(bf16)
    sums = exchanged(part.reshape(4, 16, 2048), "head", ROW_ZH)

    prob, z = index_forward(at, kept, queries, keys, index_scale)
    own, send, dq = index_backward(at, kept, prob, z, queries, keys, [sums], index_scale)

    got = other_core(send)
    dkey = (own + got.astype(f32)).astype(bf16)
    dkey = exchanged(dkey.reshape(32, 32, 128), ("seq", "head"), YZX)
    dkey = jnp.sum(dkey.astype(f32), axis=0).astype(bf16)
    dkey = jnp.broadcast_to(dkey, (16, 32, 128))
    both = exchanged(jnp.concatenate([dq, dkey], axis=1), "head")
    dkey = both[:, 64:].astype(f32).reshape(4, 4, 32, 128).sum(axis=0).reshape(128, 128).T
    return both[:, :64].reshape(index_query.shape), dkey


def solution(mesh):
    return jax.shard_map(
        local,
        mesh=mesh,
        in_specs=(
            P("seq", "head", None),
            P("seq", None),
            P("seq", "head"),
            P("seq", "head", None),
            P("seq", None),
            P("seq", "head"),
            P("seq", None),
        ),
        out_specs=(P("seq", "head", None), P("seq", None)),
        check_vma=False,
    )
```

profile of v0, /device:TPU:32, one launch (start us, length us, event | category | flops | bytes accessed | tf_op | source)
XLA Modules:
  0.0 151.8 jit_solution(6497461581287505006)
XLA Ops:
  0.6 1.0 fusion.10
  1.6 1.9 %collective-permute-start = (bf16[704,128]{1,0:T(8,128)(2,1)S(1)}, bf16[704,128]{1,0:T(8,128)(2,1)S(1)}, u32[]{:S(2)}, u32[]{:S(2)}) collective-permute-start(bf16[704,128]{1,0:T(8,128)(2,1)S(1)} %get-tuple-element.15), channel_id=1, source_target_pairs={{0,32},{16,48},{32,0},{48,16},{64,96},{80,112},{96,64},{112,80},{1... | collective-permute-start | bytes 540680 | tf_op jit(solution)/shard_map/ppermute | solution.py:34
  3.5 4.5 %collective-permute-done = bf16[704,128]{1,0:T(8,128)(2,1)S(1)} collective-permute-done((bf16[704,128]{1,0:T(8,128)(2,1)S(1)}, bf16[704,128]{1,0:T(8,128)(2,1)S(1)}, u32[]{:S(2)}, u32[]{:S(2)}) %collective-permute-start) | collective-permute-done | bytes 180256 | tf_op jit(solution)/shard_map/ppermute | solution.py:34
  8.0 0.0 copy-start
  8.0 3.1 %collective-permute-start.2 = (bf16[2,704,128]{2,1,0:T(8,128)(2,1)S(1)}, bf16[2,704,128]{2,1,0:T(8,128)(2,1)S(1)}, u32[]{:S(2)}, u32[]{:S(2)}) collective-permute-start(bf16[2,704,128]{2,1,0:T(8,128)(2,1)S(1)} %pad_maximum_fusion.1.refs_0_), channel_id=1, source_target_pairs={{0,192},{16,208},{32,224},{48,240},{64,0},{80,16},{96,32},{112,48}... | collective-permute-start | bytes 1081352 | tf_op jit(solution)/shard_map/ppermute | solution.py:30
  11.1 0.6 collective-permute-start.6
  11.7 1.0 collective-permute-start.4
  12.7 0.0 collective-permute-start.1
  12.7 12.9 %collective-permute-done.2.refs_2_ = bf16[2,704,128]{2,1,0:T(8,128)(2,1)S(1)} collective-permute-done((bf16[2,704,128]{2,1,0:T(8,128)(2,1)S(1)}, bf16[2,704,128]{2,1,0:T(8,128)(2,1)S(1)}, u32[]{:S(2)}, u32[]{:S(2)}) %collective-permute-start.2) | collective-permute-done | bytes 360480 | tf_op jit(solution)/shard_map/ppermute | solution.py:30
  25.7 0.0 copy-start.1
  25.7 0.0 collective-permute-start.3
  25.7 0.0 collective-permute-done.6.refs_6_.refs_2_
  25.7 0.0 copy-start.2
  25.7 0.5 collective-permute-start.7
  26.2 3.2 %collective-permute-done.4.refs_4_.refs_0_ = bf16[2,704,128]{2,1,0:T(8,128)(2,1)S(1)} collective-permute-done((bf16[2,704,128]{2,1,0:T(8,128)(2,1)S(1)}, bf16[2,704,128]{2,1,0:T(8,128)(2,1)S(1)}, u32[]{:S(2)}, u32[]{:S(2)}) %collective-permute-start.4) | collective-permute-done | bytes 360480 | tf_op jit(solution)/shard_map/ppermute | solution.py:30
  29.4 0.0 copy-start.3
  29.4 0.0 collective-permute-start.5
  29.4 6.4 %wide_queries.1.q_ref = bf16[8,256,640]{2,1,0:T(8,128)(2,1)} custom-call(bf16[8,576,256]{2,1,0:T(8,128)(2,1)} %bitcast.21, f32[8,256]{1,0:T(8,128)} %bitcast.29), custom_call_target="tpu_custom_call" | custom-call | tf_op jit(solution)/shard_map/wide_queries/pallas_call | solution.py:75
  35.8 0.0 collective-permute-done.1.refs_1_
  35.8 0.0 collective-permute-done.3.refs_3_
  35.8 0.0 copy-done
  35.8 0.0 copy-done.1
  35.8 0.7 copy-done.4
  36.5 0.7 copy-done.5
  37.3 7.1 %scores.2.refs_4_ = bf16[256,2048]{1,0:T(8,128)(2,1)} custom-call(bf16[8,256,640]{2,1,0:T(8,128)(2,1)} %wide_queries.1.q_ref, bf16[2,704,128]{2,1,0:T(8,128)(2,1)} %copy-done, bf16[2,704,128]{2,1,0:T(8,128)(2,1)} %copy-done.4, bf16[2,704,128]{2,1,0:T(8,128)(2,1)} %copy-done.1, bf16[2,704,128]{2,1,0:T(8,128)(2,1)} %copy-done.5), custom_call_target="tpu_custom_call" | custom-call | tf_op jit(solution)/shard_map/scores/pallas_call | solution.py:125
  44.3 0.0 copy-done.2
  44.3 0.0 copy-done.3
  44.4 0.0 collective-permute-done.7.refs_7_.refs_3_
  44.4 0.0 copy-start.6
  44.4 0.0 collective-permute-done.5.refs_5_.refs_1_
  44.4 0.7 copy-done.6
  45.1 0.7 copy-done.7
  45.8 7.1 %scores.3 = bf16[256,2048]{1,0:T(8,128)(2,1)} custom-call(bf16[8,256,640]{2,1,0:T(8,128)(2,1)} %wide_queries.1.q_ref, bf16[2,704,128]{2,1,0:T(8,128)(2,1)} %copy-done.3, bf16[2,704,128]{2,1,0:T(8,128)(2,1)} %copy-done.7, bf16[2,704,128]{2,1,0:T(8,128)(2,1)} %copy-done.2, bf16[2,704,128]{2,1,0:T(8,128)(2,1)} %copy-done.6, ...), custom_call_target="tpu_custom_call", output_to_operand_aliasing={{}: (5, {})} | custom-call | tf_op jit(solution)/shard_map/scores/pallas_call | solution.py:125
  52.9 4.4 %all-to-all-start.1 = ((bf16[4,64,2048]{2,1,0:T(8,128)(2,1)}), bf16[4,64,2048]{2,1,0:T(8,128)(2,1)S(1)}, u32[]{:S(2)}, u32[]{:S(2)}) async-start(bf16[4,64,2048]{2,1,0:T(8,128)(2,1)} %bitcast.20), calls=%async_computation.1 | async-start | bytes 2097152 | tf_op jit(solution)/shard_map/all_to_all | solution.py:42
  57.4 0.0 copy-done.11
  57.4 0.1 copy.13
  57.5 0.1 stack_reshape.15
  57.6 0.1 copy.15
  57.8 0.1 stack_reshape.17
  57.9 0.1 copy.14
  58.1 0.1 stack_reshape.16
  58.2 0.1 fusion.8
  58.2 0.0 copy-done.10
  58.3 0.7 pad_maximum_fusion.2
  59.0 14.0 %all-to-all-done.1 = bf16[4,64,2048]{2,1,0:T(8,128)(2,1)S(1)} async-done(((bf16[4,64,2048]{2,1,0:T(8,128)(2,1)}), bf16[4,64,2048]{2,1,0:T(8,128)(2,1)S(1)}, u32[]{:S(2)}, u32[]{:S(2)}) %all-to-all-start.1) | async-done | bytes 1048608 | tf_op jit(solution)/shard_map/all_to_all | solution.py:42
  73.0 8.3 %all-to-all-start = ((bf16[16,80,128]{2,1,0:T(8,128)(2,1)}), bf16[16,80,128]{2,1,0:T(8,128)(2,1)S(1)}, u32[]{:S(2)}, u32[]{:S(2)}) async-start(bf16[16,80,128]{2,1,0:T(8,128)(2,1)} %pad_maximum_fusion.2), calls=%async_computation | async-start | bytes 655360 | tf_op jit(solution)/shard_map/all_to_all | solution.py:42
  81.3 0.9 reduce_sum.33
  82.2 12.4 %all-to-all-done.q_ref = bf16[16,80,128]{2,1,0:T(8,128)(2,1)S(1)} async-done(((bf16[16,80,128]{2,1,0:T(8,128)(2,1)}), bf16[16,80,128]{2,1,0:T(8,128)(2,1)S(1)}, u32[]{:S(2)}, u32[]{:S(2)}) %all-to-all-start) | async-done | bytes 327712 | tf_op jit(solution)/shard_map/all_to_all | solution.py:42
  94.5 3.4 %all-to-all-start.2 = ((bf16[4,16,2048]{2,1,0:T(8,128)(2,1)}), bf16[4,16,2048]{2,1,0:T(8,128)(2,1)S(1)}, u32[]{:S(2)}, u32[]{:S(2)}) async-start(bf16[4,16,2048]{2,1,0:T(8,128)(2,1)} %bitcast.11), calls=%async_computation.2 | async-start | bytes 524288 | tf_op jit(solution)/shard_map/all_to_all | solution.py:42
  98.0 0.6 pad_add_fusion.at_ref
  98.6 0.0 copy-done.8
  98.6 5.4 %index_forward.1 = (f32[16,2048]{1,0:T(8,128)}, bf16[4,256,2048]{2,1,0:T(8,128)(2,1)}) custom-call(s32[4]{0:T(128)} %pad_add_fusion.at_ref, s32[2,16]{1,0:T(2,128)} %kept_ref.3, bf16[16,80,128]{2,1,0:T(8,128)(2,1)} %copy-done.8, bf16[2,704,128]{2,1,0:T(8,128)(2,1)} %copy-done, bf16[2,704,128]{2,1,0:T(8,128)(2,1)} %copy-done.4, ...), custom_call_target="tpu_custom_call" | custom-call | tf_op jit(solution)/shard_map/index_forward/pallas_call | solution.py:202
  104.0 4.2 %all-to-all-done.2.refs_8_ = bf16[4,16,2048]{2,1,0:T(8,128)(2,1)S(1)} async-done(((bf16[4,16,2048]{2,1,0:T(8,128)(2,1)}), bf16[4,16,2048]{2,1,0:T(8,128)(2,1)S(1)}, u32[]{:S(2)}, u32[]{:S(2)}) %all-to-all-start.2) | async-done | bytes 262176 | tf_op jit(solution)/shard_map/all_to_all | solution.py:42
  108.2 0.7 copy-done.9
  108.9 8.2 %index_backward.1 = (f32[8,128,128]{2,1,0:T(8,128)}, bf16[8,128,128]{2,1,0:T(8,128)(2,1)}, bf16[16,64,128]{2,1,0:T(8,128)(2,1)}) custom-call(s32[4]{0:T(128)} %pad_add_fusion.at_ref, s32[2,16]{1,0:T(2,128)} %kept_ref.3, f32[16,2048]{1,0:T(8,128)} %get-tuple-element.7.prob_ref, bf16[4,256,2048]{2,1,0:T(8,128)(2,1)} %get-tuple-element.8.z_ref, ...), custom_call_target="tpu_custom_call" | custom-call | tf_op jit(solution)/shard_map/index_backward/pallas_call | solution.py:261
  117.1 0.0 collective-permute-start.8
  117.1 1.7 %collective-permute-done.8 = bf16[8,128,128]{2,1,0:T(8,128)(2,1)S(1)} collective-permute-done((bf16[8,128,128]{2,1,0:T(8,128)(2,1)}, bf16[8,128,128]{2,1,0:T(8,128)(2,1)S(1)}, u32[]{:S(2)}, u32[]{:S(2)}) %collective-permute-start.8) | collective-permute-done | bytes 262176 | tf_op jit(solution)/shard_map/ppermute | solution.py:38
  118.9 1.1 add_convert_fusion
  120.0 12.6 %all_to_all.25 = bf16[32,32,128]{2,1,0:T(8,128)(2,1)S(1)} all-to-all(bf16[32,32,128]{2,1,0:T(8,128)(2,1)S(1)} %bitcast.22), channel_id=1, replica_groups={{0,1,2,3,32,33,34,35,64,65,66,67,96,97,98,99,128,129,130,131,160,161,16..., dimensions={0} | all-to-all | bytes 524288 | tf_op jit(solution)/shard_map/all_to_all | solution.py:42
  132.5 0.1 reduce_sum.34
  132.6 1.0 pad_maximum_fusion
  133.6 16.7 %all_to_all.26 = bf16[16,96,128]{2,1,0:T(8,128)(2,1)S(1)} all-to-all(bf16[16,96,128]{2,1,0:T(8,128)(2,1)S(1)} %pad_maximum_fusion), channel_id=1, replica_groups=mesh['seq'=16,'head'=16] {'head'}, dimensions={0} | all-to-all | bytes 786432 | tf_op jit(solution)/shard_map/all_to_all | solution.py:42
  150.4 0.7 copy.19
  151.1 0.7 slice.8
  (12 shorter events, 0.1 us)
Async XLA Ops:
  1.6 6.4 %collective-permute-start = (bf16[704,128]{1,0:T(8,128)(2,1)S(1)}, bf16[704,128]{1,0:T(8,128)(2,1)S(1)}, u32[]{:S(2)}, u32[]{:S(2)}) collective-permute-start(bf16[704,128]{1,0:T(8,128)(2,1)S(1)} %get-tuple-element.15), channel_id=1, source_target_pairs={{0,32},{16,48},{32,0},{48,16},{64,96},{80,112},{96,64},{112,80},{1... | collective-permute-start | bytes 540680 | tf_op jit(solution)/shard_map/ppermute | solution.py:34
  8.0 27.8 %copy-start = (bf16[2,704,128]{2,1,0:T(8,128)(2,1)}, bf16[2,704,128]{2,1,0:T(8,128)(2,1)S(1)}, u32[]{:S(2)}) copy-start(bf16[2,704,128]{2,1,0:T(8,128)(2,1)S(1)} %pad_maximum_fusion.1.refs_0_) | copy-start | bytes 1081348
  8.0 17.6 %collective-permute-start.2 = (bf16[2,704,128]{2,1,0:T(8,128)(2,1)S(1)}, bf16[2,704,128]{2,1,0:T(8,128)(2,1)S(1)}, u32[]{:S(2)}, u32[]{:S(2)}) collective-permute-start(bf16[2,704,128]{2,1,0:T(8,128)(2,1)S(1)} %pad_maximum_fusion.1.refs_0_), channel_id=1, source_target_pairs={{0,192},{16,208},{32,224},{48,240},{64,0},{80,16},{96,32},{112,48}... | collective-permute-start | bytes 1081352 | tf_op jit(solution)/shard_map/ppermute | solution.py:30
  11.1 14.5 %collective-permute-start.6 = (bf16[2,704,128]{2,1,0:T(8,128)(2,1)S(1)}, bf16[2,704,128]{2,1,0:T(8,128)(2,1)S(1)}, u32[]{:S(2)}, u32[]{:S(2)}) collective-permute-start(bf16[2,704,128]{2,1,0:T(8,128)(2,1)S(1)} %pad_maximum_fusion.1.refs_0_), channel_id=1, source_target_pairs={{0,128},{16,144},{32,160},{48,176},{64,192},{80,208},{96,224},{112... | collective-permute-start | bytes 1081352 | tf_op jit(solution)/shard_map/ppermute | solution.py:30
  11.7 17.6 %collective-permute-start.4 = (bf16[2,704,128]{2,1,0:T(8,128)(2,1)S(1)}, bf16[2,704,128]{2,1,0:T(8,128)(2,1)S(1)}, u32[]{:S(2)}, u32[]{:S(2)}) collective-permute-start(bf16[2,704,128]{2,1,0:T(8,128)(2,1)S(1)} %pad_maximum_fusion.1.refs_0_), channel_id=1, source_target_pairs={{0,64},{16,80},{32,96},{48,112},{64,128},{80,144},{96,160},{112,17... | collective-permute-start | bytes 1081352 | tf_op jit(solution)/shard_map/ppermute | solution.py:30
  12.7 23.1 %collective-permute-start.1 = (bf16[2,704,128]{2,1,0:T(8,128)(2,1)S(1)}, bf16[2,704,128]{2,1,0:T(8,128)(2,1)S(1)}, u32[]{:S(2)}, u32[]{:S(2)}) collective-permute-start(bf16[2,704,128]{2,1,0:T(8,128)(2,1)S(1)} %pad_maximum_fusion.1.refs_0_), channel_id=1, source_target_pairs={{0,16},{16,0},{32,48},{48,32},{64,80},{80,64},{96,112},{112,96},{1... | collective-permute-start | bytes 1081352 | tf_op jit(solution)/shard_map/ppermute | solution.py:38
  25.7 10.1 %copy-start.1 = (bf16[2,704,128]{2,1,0:T(8,128)(2,1)}, bf16[2,704,128]{2,1,0:T(8,128)(2,1)S(1)}, u32[]{:S(2)}) copy-start(bf16[2,704,128]{2,1,0:T(8,128)(2,1)S(1)} %collective-permute-done.2.refs_2_) | copy-start | bytes 1081348
  25.7 10.1 %collective-permute-start.3 = (bf16[2,704,128]{2,1,0:T(8,128)(2,1)S(1)}, bf16[2,704,128]{2,1,0:T(8,128)(2,1)S(1)}, u32[]{:S(2)}, u32[]{:S(2)}) collective-permute-start(bf16[2,704,128]{2,1,0:T(8,128)(2,1)S(1)} %collective-permute-done.2.refs_2_), channel_id=1, source_target_pairs={{0,16},{16,0},{32,48},{48,32},{64,80},{80,64},{96,112},{112,96},{1... | collective-permute-start | bytes 1081352 | tf_op jit(solution)/shard_map/ppermute | solution.py:38
  25.7 18.7 %copy-start.2 = (bf16[2,704,128]{2,1,0:T(8,128)(2,1)}, bf16[2,704,128]{2,1,0:T(8,128)(2,1)S(1)}, u32[]{:S(2)}) copy-start(bf16[2,704,128]{2,1,0:T(8,128)(2,1)S(1)} %collective-permute-done.6.refs_6_.refs_2_) | copy-start | bytes 1081348
  25.7 18.7 %collective-permute-start.7 = (bf16[2,704,128]{2,1,0:T(8,128)(2,1)S(1)}, bf16[2,704,128]{2,1,0:T(8,128)(2,1)S(1)}, u32[]{:S(2)}, u32[]{:S(2)}) collective-permute-start(bf16[2,704,128]{2,1,0:T(8,128)(2,1)S(1)} %collective-permute-done.6.refs_6_.refs_2_), channel_id=1, source_target_pairs={{0,16},{16,0},{32,48},{48,32},{64,80},{80,64},{96,112},{112,96},{1... | collective-permute-start | bytes 1081352 | tf_op jit(solution)/shard_map/ppermute | solution.py:38
  29.4 15.0 %copy-start.3 = (bf16[2,704,128]{2,1,0:T(8,128)(2,1)}, bf16[2,704,128]{2,1,0:T(8,128)(2,1)S(1)}, u32[]{:S(2)}) copy-start(bf16[2,704,128]{2,1,0:T(8,128)(2,1)S(1)} %collective-permute-done.4.refs_4_.refs_0_) | copy-start | bytes 1081348
  29.4 15.0 %collective-permute-start.5 = (bf16[2,704,128]{2,1,0:T(8,128)(2,1)S(1)}, bf16[2,704,128]{2,1,0:T(8,128)(2,1)S(1)}, u32[]{:S(2)}, u32[]{:S(2)}) collective-permute-start(bf16[2,704,128]{2,1,0:T(8,128)(2,1)S(1)} %collective-permute-done.4.refs_4_.refs_0_), channel_id=1, source_target_pairs={{0,16},{16,0},{32,48},{48,32},{64,80},{80,64},{96,112},{112,96},{1... | collective-permute-start | bytes 1081352 | tf_op jit(solution)/shard_map/ppermute | solution.py:38
  35.8 0.8 copy-start.4
  36.5 0.7 copy-start.5
  44.4 13.0 %copy-start.11 = (f32[256,4]{0,1:T(4,128)S(1)}, f32[256,4]{0,1:T(4,128)}, u32[]{:S(2)}) copy-start(f32[256,4]{0,1:T(4,128)} %param.12) | copy-start | bytes 12292
  44.4 0.7 copy-start.6
  45.1 0.7 copy-start.7
  52.9 5.3 %copy-start.10 = (bf16[256,4,128]{2,1,0:T(4,128)(2,1)S(1)}, bf16[256,4,128]{2,1,0:T(4,128)(2,1)}, u32[]{:S(2)}) copy-start(bf16[256,4,128]{2,1,0:T(4,128)(2,1)} %param.10) | copy-start | bytes 786436
  52.9 20.0 %all-to-all-start.1 = ((bf16[4,64,2048]{2,1,0:T(8,128)(2,1)}), bf16[4,64,2048]{2,1,0:T(8,128)(2,1)S(1)}, u32[]{:S(2)}, u32[]{:S(2)}) async-start(bf16[4,64,2048]{2,1,0:T(8,128)(2,1)} %bitcast.20), calls=%async_computation.1 | async-start | bytes 2097152 | tf_op jit(solution)/shard_map/all_to_all | solution.py:42
  73.0 21.6 %all-to-all-start = ((bf16[16,80,128]{2,1,0:T(8,128)(2,1)}), bf16[16,80,128]{2,1,0:T(8,128)(2,1)S(1)}, u32[]{:S(2)}, u32[]{:S(2)}) async-start(bf16[16,80,128]{2,1,0:T(8,128)(2,1)} %pad_maximum_fusion.2), calls=%async_computation | async-start | bytes 655360 | tf_op jit(solution)/shard_map/all_to_all | solution.py:42
  94.5 4.1 %copy-start.8 = (bf16[16,80,128]{2,1,0:T(8,128)(2,1)}, bf16[16,80,128]{2,1,0:T(8,128)(2,1)S(1)}, u32[]{:S(2)}) copy-start(bf16[16,80,128]{2,1,0:T(8,128)(2,1)S(1)} %all-to-all-done.q_ref) | copy-start | bytes 983044
  94.5 13.7 %all-to-all-start.2 = ((bf16[4,16,2048]{2,1,0:T(8,128)(2,1)}), bf16[4,16,2048]{2,1,0:T(8,128)(2,1)S(1)}, u32[]{:S(2)}, u32[]{:S(2)}) async-start(bf16[4,16,2048]{2,1,0:T(8,128)(2,1)} %bitcast.11), calls=%async_computation.2 | async-start | bytes 524288 | tf_op jit(solution)/shard_map/all_to_all | solution.py:42
  108.2 0.7 copy-start.9
  117.1 1.7 %collective-permute-start.8 = (bf16[8,128,128]{2,1,0:T(8,128)(2,1)}, bf16[8,128,128]{2,1,0:T(8,128)(2,1)S(1)}, u32[]{:S(2)}, u32[]{:S(2)}) collective-permute-start(bf16[8,128,128]{2,1,0:T(8,128)(2,1)} %get-tuple-element.11), channel_id=1, source_target_pairs={{0,16},{16,0},{32,48},{48,32},{64,80},{80,64},{96,112},{112,96},{1... | collective-permute-start | bytes 786440 | tf_op jit(solution)/shard_map/ppermute | solution.py:38
where the time goes:
time: 154 us; the launch traced here: 152 us
  waiting for transfers between devices  52.9 us (34%)
  Pallas kernels  34.2 us (22%)
  blocking collectives  29.3 us (19%)
  starting transfers between devices  23.2 us (15%)
  local copies, waits for them, and re-layouts  5.95 us (4%)
  other arithmetic  5.5 us (4%)
    all_to_all x3, waiting for transfers between devices, exchanged(): lax.all_to_all(value, axis, 0, 0, tiled=True, axis_index_groups=groups)  30.5 us
    all_to_all x2, blocking collectives, exchanged(): lax.all_to_all(value, axis, 0, 0, tiled=True, axis_index_groups=groups)  29.3 us
    ppermute x3, waiting for transfers between devices, along_y(): lax.ppermute(value, 'seq', [(i, (i + 4 * d) % 16) for i in range(16)])  16.1 us
    all_to_all x3, starting transfers between devices, exchanged(): lax.all_to_all(value, axis, 0, 0, tiled=True, axis_index_groups=groups)  16.1 us
    pallas_call x2, Pallas kernels, scores(): pl.pallas_call(score_body, grid=(len(pairs),), out_shape=sds((rows, 2048)...  14.2 us
    pallas_call x1, Pallas kernels, index_backward(): call(functools.partial(back_body, scale), (sds((8, 128, 128), f32), sds((...  8.22 us
    pallas_call x1, Pallas kernels, wide_queries(): pl.pallas_call(query_body, grid=(heads,), out_shape=sds((heads, rows, 640...  6.39 us
    pallas_call x1, Pallas kernels, index_forward(): call(functools.partial(index_body, scale), (sds((16, 2048), f32), sds((4,...  5.41 us
  transfers between devices with their start and end apart: 12, of which 7 were waited for; matrix products, arithmetic and copies ran while one was open for 2% of the time, Pallas kernels for 12%

commit v1 on v0

v1 whole, which is shorter than its diff:
```python
import functools

import jax
import jax.numpy as jnp
from jax import lax
from jax.experimental import pallas as pl
from jax.experimental.pallas import tpu as pltpu
from jax.sharding import PartitionSpec as P


attn_scale = 192.0 ** (-0.5)
LOG2E = 1.4426950408889634
STEPS = (1, 3, 2)
f32 = jnp.float32
bf16 = jnp.bfloat16
VM = pl.BlockSpec(memory_space=pltpu.VMEM)
SM = pl.BlockSpec(memory_space=pltpu.SMEM)

ROW_X = [[zh * 4 + x for x in range(4)] for zh in range(4)]
ROW_ZH = [[zh * 4 + x for zh in range(4)] for x in range(4)]
YZX = [
    [(y * 4 + z * 2 + c) * 16 + zh * 4 + x for y in range(4) for z in range(2) for x in range(4)]
    for zh in range(4)
    for c in range(2)
]


def along_y(value, d):
    return lax.ppermute(value, "seq", [(i, (i + 4 * d) % 16) for i in range(16)])


def along_z(value):
    return lax.ppermute(value, "seq", [(i, i ^ 2) for i in range(16)])


def other_core(value):
    return lax.ppermute(value, "seq", [(i, i ^ 1) for i in range(16)])


def exchanged(value, axis, groups=None):
    return lax.all_to_all(value, axis, 0, 0, tiled=True, axis_index_groups=groups)


def sds(shape, dtype):
    return jax.ShapeDtypeStruct(shape, dtype)


def call(body, outs, specs, mib, **more):
    return pl.pallas_call(
        body,
        out_shape=outs,
        in_specs=specs,
        out_specs=jax.tree.map(lambda _: VM, outs),
        compiler_params=pltpu.CompilerParams(vmem_limit_bytes=mib << 20),
        **more,
    )


def query_body(q_ref, lse_ref, out_ref, wide):
    heads, width, rows = q_ref.shape
    row = lax.broadcasted_iota(jnp.int32, (640 - width, rows), 0)
    for h in range(heads):
        value = lse_ref[h : h + 1, :] * (-1.0 / attn_scale)
        p0 = value.astype(bf16).astype(f32)
        p1 = (value - p0).astype(bf16).astype(f32)
        p2 = value - p0 - p1
        more = jnp.where(row == 0, p0, jnp.where(row == 1, p1, jnp.where(row == 2, p2, 0.0)))
        wide[h, 0:width, :] = q_ref[h]
        wide[h, width:, :] = more.astype(bf16)
        out_ref[h] = wide[h].T


def wide_queries(query, normalizer):
    heads, _, rows = query.shape
    return call(
        query_body,
        sds((heads, rows, 640), bf16),
        [VM, VM],
        12,
        scratch_shapes=[pltpu.VMEM((heads, 640, rows), bf16)],
        name="wide_queries",
    )(query, normalizer)


def score_body(q_ref, *refs):
    tiles, before, (out_ref, index_ref, keys) = refs[:8], refs[8:-3], refs[-3:]
    heads, rows, depth = q_ref.shape
    width = tiles[0].shape[0] - 128
    begin = 512 * len(before)
    if before:
        out_ref[:, 0:begin] = before[0][...]
        index_ref[0:begin] = before[1][...]
    for i, tile in enumerate(tiles):
        index_ref[begin + i * 128 : begin + i * 128 + 128] = tile[0:128, :]
    row = lax.broadcasted_iota(jnp.int32, (depth - width, 512), 0)
    for n in range(2):
        keys[n, width:, :] = jnp.where(row < 3, 1.0, 0.0).astype(bf16)
        for i in range(4):
            keys[n, 0:width, i * 128 : i * 128 + 128] = tiles[4 * n + i][128:, :]
        total = None
        for h in range(0, heads, 2):
            both = q_ref[h : h + 2].reshape(2 * rows, depth)
            s = jnp.dot(both, keys[n], preferred_element_type=f32)
            p = jnp.exp2(s * (attn_scale * LOG2E))
            p = p[:rows] + p[rows:]
            total = p if total is None else total + p
        for x in range(4):
            for zh in range(4):
                to, at = (x * 4 + zh) * 16, (zh * 4 + x) * 16
                out_ref[to : to + 16, begin + n * 512 : begin + n * 512 + 512] = total[
                    at : at + 16
                ].astype(bf16)


def scores(query, tiles, *before):
    _, rows, depth = query.shape
    cols = 1024 + 512 * len(before)
    return call(
        score_body,
        (sds((rows, cols), bf16), sds((cols, 128), bf16)),
        [VM] * (9 + len(before)),
        14,
        scratch_shapes=[pltpu.VMEM((2, depth, 512), bf16)],
        name="scores",
    )(query, *tiles, *before)


def weight_column(q_ref, j):
    row = jnp.sum(q_ref[j, 64:80, :].astype(f32), axis=0, keepdims=True)[:, 0:64]
    eye = lax.broadcasted_iota(jnp.int32, (64, 64), 0) == lax.broadcasted_iota(jnp.int32, (64, 64), 1)
    return jnp.sum(jnp.where(eye, row, 0.0), axis=1, keepdims=True)


def slot_tile(at_ref, slot):
    u, k, v = slot // 8, slot // 2 % 4, slot % 2
    y = lax.rem(at_ref[1] + ((0,) + STEPS)[k], 4)
    z = at_ref[2] if u == 0 else 1 - at_ref[2]
    c = at_ref[3] if v == 0 else 1 - at_ref[3]
    return y * 4 + z * 2 + c


def allowed(at_ref, kept_ref):
    half = jnp.where(at_ref[0] >= 8, 1, 0)
    flags = [
        jnp.full((16, 128), kept_ref[half, slot_tile(at_ref, slot)], jnp.int32) for slot in range(16)
    ]
    return jnp.concatenate(flags, axis=1) > 0


NT = (((1,), (1,)), ((), ()))
TN = (((0,), (0,)), ((), ()))


def index_body(scale, at_ref, kept_ref, q_ref, keys, prob_ref, acc):
    acc[...] = jnp.zeros_like(acc)

    @pl.loop(0, 4)
    def _(g):
        rows = q_ref[pl.ds(4 * g, 4), 0:64, :].reshape(256, 128)
        z = lax.dot_general(rows, keys[...], NT, preferred_element_type=f32)
        part = None
        for a in range(4):
            weight = weight_column(q_ref, 4 * g + a) * scale
            term = jnp.maximum(z[a * 64 : a * 64 + 64], 0.0) * weight
            part = term if part is None else part + term
        acc[...] += part

    pick = (
        lax.broadcasted_iota(jnp.int32, (16, 64), 1) // 4
        == lax.broadcasted_iota(jnp.int32, (16, 64), 0)
    ).astype(f32)
    logit = jnp.dot(pick, acc[...], precision=lax.Precision.HIGHEST, preferred_element_type=f32)
    keep = allowed(at_ref, kept_ref)
    top = jnp.max(jnp.where(keep, logit, -jnp.inf), axis=1, keepdims=True)
    expo = jnp.where(keep, jnp.exp(jnp.where(keep, logit, top) - top), 0.0)
    prob_ref[...] = expo / jnp.sum(expo, axis=1, keepdims=True)


def index_forward(at, kept, queries, keys, scale):
    return call(
        functools.partial(index_body, scale),
        sds((16, 2048), f32),
        [SM, SM, VM, VM],
        14,
        scratch_shapes=[pltpu.VMEM((64, 2048), f32)],
        name="index_forward",
    )(at, kept, queries, keys)


def back_body(scale, at_ref, kept_ref, prob_ref, q_ref, keys, sums, *refs):
    own_ref, send_ref, dq_ref, dz, dk, wide = refs
    total = sums[0].astype(f32)
    for j in range(1, sums.shape[0]):
        total += sums[j].astype(f32)
    head_sum = jnp.where(allowed(at_ref, kept_ref), total, 0.0)
    grad = prob_ref[...] - head_sum / jnp.sum(head_sum, axis=1, keepdims=True)
    for t in range(16):
        wide[4 * t : 4 * t + 4, :] = jnp.broadcast_to(grad[t : t + 1], (4, 2048))
    dk[...] = jnp.zeros_like(dk)

    @pl.loop(0, 4)
    def _(g):
        rows = q_ref[pl.ds(4 * g, 4), 0:64, :].reshape(256, 128)
        z = lax.dot_general(rows, keys[...], NT, preferred_element_type=f32)
        for a in range(4):
            at = a * 64
            value = wide[...] * weight_column(q_ref, 4 * g + a)
            dz[at : at + 64, :] = jnp.where(z[at : at + 64] > 0.0, value, 0.0).astype(bf16)
        dk[...] += lax.dot_general(rows, dz[...], TN, preferred_element_type=f32)
        dq = jnp.dot(dz[...], keys[...], preferred_element_type=f32) * scale
        dq_ref[pl.ds(4 * g, 4)] = dq.astype(bf16).reshape(4, 64, 128)

    for slot in range(16):
        tile = dk[:, slot * 128 : slot * 128 + 128] * scale
        place = lax.div(slot_tile(at_ref, slot), 2)
        if slot % 2 == 0:
            own_ref[place] = tile
        else:
            send_ref[place] = tile.astype(bf16)


def index_backward(at, kept, prob, queries, keys, sums, scale):
    return call(
        functools.partial(back_body, scale),
        (sds((8, 128, 128), f32), sds((8, 128, 128), bf16), sds((16, 64, 128), bf16)),
        [SM, SM] + [VM] * 4,
        16,
        scratch_shapes=[
            pltpu.VMEM((256, 2048), bf16),
            pltpu.VMEM((128, 2048), f32),
            pltpu.VMEM((64, 2048), f32),
        ],
        name="index_backward",
    )(at, kept, prob, queries, keys, sums)


def local(query_latent, key_latent, normalizer, index_query, index_key, index_weight, kept):
    index_scale = index_query.shape[2] ** (-0.5)
    head = lax.axis_index("head")
    seq = lax.axis_index("seq")
    at = jnp.stack([head, seq // 4, seq // 2 % 2, seq % 2]).astype(jnp.int32)

    tile = jnp.concatenate([index_key, key_latent.T], axis=0)
    tiles = []
    for u in range(2):
        if u == 1:
            tile = along_z(tile)
        for d in (0,) + STEPS:
            there = along_y(tile, -d) if d else tile
            tiles += [there, other_core(there)]

    w0 = lax.reduce_precision(index_weight, 8, 7)
    w1 = lax.reduce_precision(index_weight - w0, 8, 7)
    w2 = index_weight - w0 - w1
    weight = jnp.stack([w.reshape(16, 64) for w in (w0, w1, w2)], axis=1).astype(bf16)
    weight = jnp.pad(weight, ((0, 0), (0, 13), (0, 64)))
    queries = jnp.concatenate([index_query.reshape(16, 64, 128), weight], axis=1)
    queries = exchanged(queries, "head")

    query = wide_queries(jnp.transpose(query_latent, (1, 2, 0)), normalizer.T)
    first = scores(query, tiles[:8])
    part, index_keys = scores(query, tiles[8:], *first)
    part = exchanged(part.reshape(4, 64, 2048), "head", ROW_X)
    part = jnp.sum(part.astype(f32), axis=0).astype(bf16)
    sums = exchanged(part.reshape(4, 16, 2048), "head", ROW_ZH)

    prob = index_forward(at, kept, queries, index_keys, index_scale)
    own, send, dq = index_backward(at, kept, prob, queries, index_keys, sums, index_scale)

    got = other_core(send)
    dkey = (own + got.astype(f32)).astype(bf16)
    dkey = exchanged(dkey.reshape(32, 32, 128), ("seq", "head"), YZX)
    dkey = jnp.sum(dkey.astype(f32), axis=0).astype(bf16)
    dkey = jnp.broadcast_to(dkey, (16, 32, 128))
    both = exchanged(jnp.concatenate([dq, dkey], axis=1), "head")
    dkey = both[:, 64:].astype(f32).reshape(4, 4, 32, 128).sum(axis=0).reshape(128, 128).T
    return both[:, :64].reshape(index_query.shape), dkey


def solution(mesh):
    return jax.shard_map(
        local,
        mesh=mesh,
        in_specs=(
            P("seq", "head", None),
            P("seq", None),
            P("seq", "head"),
            P("seq", "head", None),
            P("seq", None),
            P("seq", "head"),
            P("seq", None),
        ),
        out_specs=(P("seq", "head", None), P("seq", None)),
        check_vma=False,
    )
```

time: 154 us -> 135 us (0.88)
  Pallas kernels: 34.2 us -> 16.5 us
  other arithmetic: 5.5 us -> 2.9 us
  blocking collectives: 29.3 us -> 31.2 us
  starting transfers between devices: 23.2 us -> 25 us
    pallas_call x4, Pallas kernels: 26 us -> 11.9 us  [the longest x2 8.2 us: scores(): call(score_body, (sds((rows, cols), bf16), sds((cols, 128), bf16)), [VM]...]
    ppermute x1, waiting for transfers between devices: 4.47 us -> 0.01 us  [along_z(): return lax.ppermute(value, 'seq', [(i, i ^ 2) for i in range(16)])]
    pallas_call x1, Pallas kernels: 8.22 us -> 4.62 us  [index_backward(): call(functools.partial(back_body, scale), (sds((8, 128, 128), f32), sds((...]
    ppermute x3 -> x6, starting transfers between devices: 4.69 us -> 6.92 us  [along_y(): lax.ppermute(value, 'seq', [(i, (i + 4 * d) % 16) for i in range(16)])]
    all_to_all x2, blocking collectives: 29.3 us -> 31.2 us  [exchanged(): lax.all_to_all(value, axis, 0, 0, tiled=True, axis_index_groups=groups)]
    ppermute x3 -> x6, waiting for transfers between devices: 16.1 us -> 18 us  [along_y(): lax.ppermute(value, 'seq', [(i, (i + 4 * d) % 16) for i in range(16)])]
    unnamed x25 -> x11, local copies, waits for them, and re-layouts: 4.37 us -> 3.11 us
  transfers between devices with their start and end apart: 12 -> 19, of which waited for: 7 -> 8; matrix products, arithmetic and copies ran while one was open for 2% -> 2% of each run, Pallas kernels for 12% -> 6%
where the time goes in v1:
time: 135 us; the launch traced here: 133 us
  waiting for transfers between devices  51.4 us (38%)
  blocking collectives  31.2 us (23%)
  starting transfers between devices  25 us (19%)
  Pallas kernels  16.5 us (12%)
  local copies, waits for them, and re-layouts  4.69 us (3%)
  other arithmetic  2.9 us (2%)
    all_to_all x3, waiting for transfers between devices, exchanged(): lax.all_to_all(value, axis, 0, 0, tiled=True, axis_index_groups=groups)  31.8 us
    all_to_all x2, blocking collectives, exchanged(): lax.all_to_all(value, axis, 0, 0, tiled=True, axis_index_groups=groups)  31.2 us
    ppermute x6, waiting for transfers between devices, along_y(): lax.ppermute(value, 'seq', [(i, (i + 4 * d) % 16) for i in range(16)])  18 us
    all_to_all x3, starting transfers between devices, exchanged(): lax.all_to_all(value, axis, 0, 0, tiled=True, axis_index_groups=groups)  16.1 us
    pallas_call x2, Pallas kernels, scores(): call(score_body, (sds((rows, cols), bf16), sds((cols, 128), bf16)), [VM]...  8.2 us
    ppermute x6, starting transfers between devices, along_y(): lax.ppermute(value, 'seq', [(i, (i + 4 * d) % 16) for i in range(16)])  6.92 us
    pallas_call x1, Pallas kernels, index_backward(): call(functools.partial(back_body, scale), (sds((8, 128, 128), f32), sds((...  4.62 us
    unnamed x11, local copies, waits for them, and re-layouts  3.11 us
  transfers between devices with their start and end apart: 19, of which 8 were waited for; matrix products, arithmetic and copies ran while one was open for 2% of the time, Pallas kernels for 6%

profile of v1, /device:TPU:32, one launch (start us, length us, event | category | flops | bytes accessed | tf_op | source)
XLA Modules:
  0.0 132.6 jit_solution(5421113153128778183)
XLA Ops:
  0.6 0.9 pad_maximum_fusion.2.refs_0_
  1.6 3.1 %collective-permute-start.9 = (bf16[704,128]{1,0:T(8,128)(2,1)S(1)}, bf16[704,128]{1,0:T(8,128)(2,1)S(1)}, u32[]{:S(2)}, u32[]{:S(2)}) collective-permute-start(bf16[704,128]{1,0:T(8,128)(2,1)S(1)} %pad_maximum_fusion.2.refs_0_), channel_id=1, source_target_pairs={{0,192},{16,208},{32,224},{48,240},{64,0},{80,16},{96,32},{112,48}... | collective-permute-start | bytes 540680 | tf_op jit(solution)/shard_map/ppermute | solution.py:29
  4.7 0.0 collective-permute-start.11
  4.7 0.8 collective-permute-start
  5.5 1.5 %collective-permute-start.13 = (bf16[704,128]{1,0:T(8,128)(2,1)S(1)}, bf16[704,128]{1,0:T(8,128)(2,1)S(1)}, u32[]{:S(2)}, u32[]{:S(2)}) collective-permute-start(bf16[704,128]{1,0:T(8,128)(2,1)S(1)} %pad_maximum_fusion.2.refs_0_), channel_id=1, source_target_pairs={{0,128},{16,144},{32,160},{48,176},{64,192},{80,208},{96,224},{112... | collective-permute-start | bytes 540680 | tf_op jit(solution)/shard_map/ppermute | solution.py:29
  7.0 0.0 collective-permute-start.8
  7.0 5.4 %collective-permute-done.9.refs_2_ = bf16[704,128]{1,0:T(8,128)(2,1)S(1)} collective-permute-done((bf16[704,128]{1,0:T(8,128)(2,1)S(1)}, bf16[704,128]{1,0:T(8,128)(2,1)S(1)}, u32[]{:S(2)}, u32[]{:S(2)}) %collective-permute-start.9) | collective-permute-done | bytes 180256 | tf_op jit(solution)/shard_map/ppermute | solution.py:29
  12.4 0.0 collective-permute-start.10
  12.4 3.4 %collective-permute-done.11.refs_4_ = bf16[704,128]{1,0:T(8,128)(2,1)S(1)} collective-permute-done((bf16[704,128]{1,0:T(8,128)(2,1)S(1)}, bf16[704,128]{1,0:T(8,128)(2,1)S(1)}, u32[]{:S(2)}, u32[]{:S(2)}) %collective-permute-start.11) | collective-permute-done | bytes 180256 | tf_op jit(solution)/shard_map/ppermute | solution.py:29
  15.7 0.0 collective-permute-start.12
  15.7 0.0 collective-permute-done.refs_0_
  15.7 0.8 collective-permute-start.2
  16.5 0.0 collective-permute-done.13.refs_6_
  16.5 1.2 collective-permute-start.4
  17.8 0.0 collective-permute-done.8.refs_1_
  17.8 0.3 collective-permute-start.6
  18.1 0.0 collective-permute-done.10.refs_3_
  18.1 0.0 collective-permute-start.1
  18.1 0.0 collective-permute-done.12.refs_5_
  18.1 0.5 collective-permute-start.14
  18.6 4.6 %collective-permute-done.2.refs_2_ = bf16[704,128]{1,0:T(8,128)(2,1)S(1)} collective-permute-done((bf16[704,128]{1,0:T(8,128)(2,1)S(1)}, bf16[704,128]{1,0:T(8,128)(2,1)S(1)}, u32[]{:S(2)}, u32[]{:S(2)}) %collective-permute-start.2) | collective-permute-done | bytes 180256 | tf_op jit(solution)/shard_map/ppermute | solution.py:29
  23.2 0.0 collective-permute-start.3
  23.2 4.7 %collective-permute-done.4.refs_4_ = bf16[704,128]{1,0:T(8,128)(2,1)S(1)} collective-permute-done((bf16[704,128]{1,0:T(8,128)(2,1)S(1)}, bf16[704,128]{1,0:T(8,128)(2,1)S(1)}, u32[]{:S(2)}, u32[]{:S(2)}) %collective-permute-start.4) | collective-permute-done | bytes 180256 | tf_op jit(solution)/shard_map/ppermute | solution.py:29
  27.9 0.0 collective-permute-start.5
  27.9 0.0 collective-permute-done.6.refs_6_
  27.9 0.5 collective-permute-start.7
  28.4 1.7 %copy-done = bf16[256,8,576]{0,2,1:T(8,128)(2,1)S(1)} copy-done((bf16[256,8,576]{0,2,1:T(8,128)(2,1)S(1)}, bf16[256,8,576]{0,2,1:T(8,128)(2,1)}, u32[]{:S(2)}) %copy-start) | copy-done | bytes 2359320
  30.0 0.7 copy-done.1
  30.7 0.7 wide_queries.1.q_ref
  31.5 0.0 collective-permute-done.14.refs_7_
  31.5 3.6 %scores.2 = (bf16[256,1024]{1,0:T(8,128)(2,1)S(1)}, bf16[1024,128]{1,0:T(8,128)(2,1)S(1)}) custom-call(bf16[8,256,640]{2,1,0:T(8,128)(2,1)S(1)} %wide_queries.1.q_ref, bf16[704,128]{1,0:T(8,128)(2,1)S(1)} %pad_maximum_fusion.2.refs_0_, bf16[704,128]{1,0:T(8,128)(2,1)S(1)} %collective-permute-done.8.refs_1_, ...), custom_call_target="tpu_custom_call" | custom-call | tf_op jit(solution)/shard_map/scores/pallas_call | solution.py:118
  35.1 0.0 collective-permute-done.1.refs_1_
  35.1 0.0 collective-permute-done.3.refs_3_
  35.1 0.0 collective-permute-done.5.refs_5_
  35.1 0.0 collective-permute-done.7.refs_7_
  35.1 0.0 copy-start.4
  35.1 0.0 copy-start.3
  35.1 4.6 %scores.3 = (bf16[256,2048]{1,0:T(8,128)(2,1)}, bf16[2048,128]{1,0:T(8,128)(2,1)S(1)}) custom-call(bf16[8,256,640]{2,1,0:T(8,128)(2,1)S(1)} %wide_queries.1.q_ref, bf16[704,128]{1,0:T(8,128)(2,1)S(1)} %collective-permute-done.refs_0_, bf16[704,128]{1,0:T(8,128)(2,1)S(1)} %collective-permute-done.1.refs_1_, ...), custom_call_target="tpu_custom_call" | custom-call | tf_op jit(solution)/shard_map/scores/pallas_call | solution.py:118
  39.8 4.4 %all-to-all-start.1 = ((bf16[4,64,2048]{2,1,0:T(8,128)(2,1)}), bf16[4,64,2048]{2,1,0:T(8,128)(2,1)S(1)}, u32[]{:S(2)}, u32[]{:S(2)}) async-start(bf16[4,64,2048]{2,1,0:T(8,128)(2,1)} %bitcast.8), calls=%async_computation.1 | async-start | bytes 2097152 | tf_op jit(solution)/shard_map/all_to_all | solution.py:41
  44.2 0.1 copy.12
  44.4 0.1 stack_reshape.15
  44.5 0.1 copy.13
  44.6 0.1 stack_reshape.16
  44.8 0.1 copy.14
  44.9 0.1 stack_reshape.17
  45.0 0.1 fusion.8
  45.1 0.8 pad_maximum_fusion.1
  45.9 13.6 %all-to-all-done.1 = bf16[4,64,2048]{2,1,0:T(8,128)(2,1)S(1)} async-done(((bf16[4,64,2048]{2,1,0:T(8,128)(2,1)}), bf16[4,64,2048]{2,1,0:T(8,128)(2,1)S(1)}, u32[]{:S(2)}, u32[]{:S(2)}) %all-to-all-start.1) | async-done | bytes 1048608 | tf_op jit(solution)/shard_map/all_to_all | solution.py:41
  59.5 8.3 %all-to-all-start = ((bf16[16,80,128]{2,1,0:T(8,128)(2,1)}), bf16[16,80,128]{2,1,0:T(8,128)(2,1)S(1)}, u32[]{:S(2)}, u32[]{:S(2)}) async-start(bf16[16,80,128]{2,1,0:T(8,128)(2,1)} %pad_maximum_fusion.1), calls=%async_computation | async-start | bytes 655360 | tf_op jit(solution)/shard_map/all_to_all | solution.py:41
  67.7 0.9 reduce_sum.33
  68.7 12.2 %all-to-all-done.q_ref = bf16[16,80,128]{2,1,0:T(8,128)(2,1)S(1)} async-done(((bf16[16,80,128]{2,1,0:T(8,128)(2,1)}), bf16[16,80,128]{2,1,0:T(8,128)(2,1)S(1)}, u32[]{:S(2)}, u32[]{:S(2)}) %all-to-all-start) | async-done | bytes 327712 | tf_op jit(solution)/shard_map/all_to_all | solution.py:41
  80.9 3.4 %all-to-all-start.2 = ((bf16[4,16,2048]{2,1,0:T(8,128)(2,1)}), bf16[4,16,2048]{2,1,0:T(8,128)(2,1)S(1)}, u32[]{:S(2)}, u32[]{:S(2)}) async-start(bf16[4,16,2048]{2,1,0:T(8,128)(2,1)} %bitcast.9), calls=%async_computation.2 | async-start | bytes 524288 | tf_op jit(solution)/shard_map/all_to_all | solution.py:41
  84.3 0.1 pad_add_fusion.at_ref
  84.4 3.0 %index_forward.1.prob_ref = f32[16,2048]{1,0:T(8,128)S(1)} custom-call(s32[4]{0:T(128)S(1)} %pad_add_fusion.at_ref, s32[2,16]{1,0:T(2,128)S(1)} %copy-done.2, bf16[16,80,128]{2,1,0:T(8,128)(2,1)S(1)} %all-to-all-done.q_ref, bf16[2048,128]{1,0:T(8,128)(2,1)S(1)} %get-tuple-element.11.keys), custom_call_target="tpu_custom_call" | custom-call | tf_op jit(solution)/shard_map/index_forward/pallas_call | solution.py:180
  87.4 6.0 %all-to-all-done.2.sums = bf16[4,16,2048]{2,1,0:T(8,128)(2,1)S(1)} async-done(((bf16[4,16,2048]{2,1,0:T(8,128)(2,1)}), bf16[4,16,2048]{2,1,0:T(8,128)(2,1)S(1)}, u32[]{:S(2)}, u32[]{:S(2)}) %all-to-all-start.2) | async-done | bytes 262176 | tf_op jit(solution)/shard_map/all_to_all | solution.py:41
  93.4 4.6 %index_backward.1 = (f32[8,128,128]{2,1,0:T(8,128)S(1)}, bf16[8,128,128]{2,1,0:T(8,128)(2,1)S(1)}, bf16[16,64,128]{2,1,0:T(8,128)(2,1)S(1)}) custom-call(s32[4]{0:T(128)S(1)} %pad_add_fusion.at_ref, s32[2,16]{1,0:T(2,128)S(1)} %copy-done.2, f32[16,2048]{1,0:T(8,128)S(1)} %index_forward.1.prob_ref, bf16[16,80,128]{2,1,0:T(8,128)(2,1)S(1)} %all-to-all-done.q_ref, ...), custom_call_target="tpu_custom_call" | custom-call | tf_op jit(solution)/shard_map/index_backward/pallas_call | solution.py:223
  98.1 0.1 collective-permute-start.15
  98.2 1.5 %collective-permute-done.15 = bf16[8,128,128]{2,1,0:T(8,128)(2,1)S(1)} collective-permute-done((bf16[8,128,128]{2,1,0:T(8,128)(2,1)S(1)}, bf16[8,128,128]{2,1,0:T(8,128)(2,1)S(1)}, u32[]{:S(2)}, u32[]{:S(2)}) %collective-permute-start.15) | collective-permute-done | bytes 262176 | tf_op jit(solution)/shard_map/ppermute | solution.py:37
  99.7 0.1 add_convert_fusion
  99.7 15.3 %all_to_all.25 = bf16[32,32,128]{2,1,0:T(8,128)(2,1)S(1)} all-to-all(bf16[32,32,128]{2,1,0:T(8,128)(2,1)S(1)} %bitcast.19), channel_id=1, replica_groups={{0,1,2,3,32,33,34,35,64,65,66,67,96,97,98,99,128,129,130,131,160,161,16..., dimensions={0} | all-to-all | bytes 524288 | tf_op jit(solution)/shard_map/all_to_all | solution.py:41
  115.1 0.1 reduce_sum.34
  115.2 15.9 %all_to_all.26 = bf16[16,96,128]{2,1,0:T(8,128)(2,1)S(1)} all-to-all(bf16[16,96,128]{2,1,0:T(8,128)(2,1)S(1)} %pad_maximum_fusion), channel_id=1, replica_groups=mesh['seq'=16,'head'=16] {'head'}, dimensions={0} | all-to-all | bytes 786432 | tf_op jit(solution)/shard_map/all_to_all | solution.py:41
  131.1 0.7 copy.18
  131.9 0.7 slice.8
  (11 shorter events, 0.1 us)
Async XLA Ops:
  1.6 10.8 %collective-permute-start.9 = (bf16[704,128]{1,0:T(8,128)(2,1)S(1)}, bf16[704,128]{1,0:T(8,128)(2,1)S(1)}, u32[]{:S(2)}, u32[]{:S(2)}) collective-permute-start(bf16[704,128]{1,0:T(8,128)(2,1)S(1)} %pad_maximum_fusion.2.refs_0_), channel_id=1, source_target_pairs={{0,192},{16,208},{32,224},{48,240},{64,0},{80,16},{96,32},{112,48}... | collective-permute-start | bytes 540680 | tf_op jit(solution)/shard_map/ppermute | solution.py:29
  4.7 11.1 %collective-permute-start.11 = (bf16[704,128]{1,0:T(8,128)(2,1)S(1)}, bf16[704,128]{1,0:T(8,128)(2,1)S(1)}, u32[]{:S(2)}, u32[]{:S(2)}) collective-permute-start(bf16[704,128]{1,0:T(8,128)(2,1)S(1)} %pad_maximum_fusion.2.refs_0_), channel_id=1, source_target_pairs={{0,64},{16,80},{32,96},{48,112},{64,128},{80,144},{96,160},{112,17... | collective-permute-start | bytes 540680 | tf_op jit(solution)/shard_map/ppermute | solution.py:29
  4.7 11.1 %collective-permute-start = (bf16[704,128]{1,0:T(8,128)(2,1)S(1)}, bf16[704,128]{1,0:T(8,128)(2,1)S(1)}, u32[]{:S(2)}, u32[]{:S(2)}) collective-permute-start(bf16[704,128]{1,0:T(8,128)(2,1)S(1)} %pad_maximum_fusion.2.refs_0_), channel_id=1, source_target_pairs={{0,32},{16,48},{32,0},{48,16},{64,96},{80,112},{96,64},{112,80},{1... | collective-permute-start | bytes 540680 | tf_op jit(solution)/shard_map/ppermute | solution.py:33
  5.5 11.1 %collective-permute-start.13 = (bf16[704,128]{1,0:T(8,128)(2,1)S(1)}, bf16[704,128]{1,0:T(8,128)(2,1)S(1)}, u32[]{:S(2)}, u32[]{:S(2)}) collective-permute-start(bf16[704,128]{1,0:T(8,128)(2,1)S(1)} %pad_maximum_fusion.2.refs_0_), channel_id=1, source_target_pairs={{0,128},{16,144},{32,160},{48,176},{64,192},{80,208},{96,224},{112... | collective-permute-start | bytes 540680 | tf_op jit(solution)/shard_map/ppermute | solution.py:29
  7.0 10.8 %collective-permute-start.8 = (bf16[704,128]{1,0:T(8,128)(2,1)S(1)}, bf16[704,128]{1,0:T(8,128)(2,1)S(1)}, u32[]{:S(2)}, u32[]{:S(2)}) collective-permute-start(bf16[704,128]{1,0:T(8,128)(2,1)S(1)} %pad_maximum_fusion.2.refs_0_), channel_id=1, source_target_pairs={{0,16},{16,0},{32,48},{48,32},{64,80},{80,64},{96,112},{112,96},{1... | collective-permute-start | bytes 540680 | tf_op jit(solution)/shard_map/ppermute | solution.py:37
  12.4 5.7 %collective-permute-start.10 = (bf16[704,128]{1,0:T(8,128)(2,1)S(1)}, bf16[704,128]{1,0:T(8,128)(2,1)S(1)}, u32[]{:S(2)}, u32[]{:S(2)}) collective-permute-start(bf16[704,128]{1,0:T(8,128)(2,1)S(1)} %collective-permute-done.9.refs_2_), channel_id=1, source_target_pairs={{0,16},{16,0},{32,48},{48,32},{64,80},{80,64},{96,112},{112,96},{1... | collective-permute-start | bytes 540680 | tf_op jit(solution)/shard_map/ppermute | solution.py:37
  15.7 2.4 %collective-permute-start.12 = (bf16[704,128]{1,0:T(8,128)(2,1)S(1)}, bf16[704,128]{1,0:T(8,128)(2,1)S(1)}, u32[]{:S(2)}, u32[]{:S(2)}) collective-permute-start(bf16[704,128]{1,0:T(8,128)(2,1)S(1)} %collective-permute-done.11.refs_4_), channel_id=1, source_target_pairs={{0,16},{16,0},{32,48},{48,32},{64,80},{80,64},{96,112},{112,96},{1... | collective-permute-start | bytes 540680 | tf_op jit(solution)/shard_map/ppermute | solution.py:37
  15.7 7.4 %collective-permute-start.2 = (bf16[704,128]{1,0:T(8,128)(2,1)S(1)}, bf16[704,128]{1,0:T(8,128)(2,1)S(1)}, u32[]{:S(2)}, u32[]{:S(2)}) collective-permute-start(bf16[704,128]{1,0:T(8,128)(2,1)S(1)} %collective-permute-done.refs_0_), channel_id=1, source_target_pairs={{0,192},{16,208},{32,224},{48,240},{64,0},{80,16},{96,32},{112,48}... | collective-permute-start | bytes 540680 | tf_op jit(solution)/shard_map/ppermute | solution.py:29
  16.5 11.3 %collective-permute-start.4 = (bf16[704,128]{1,0:T(8,128)(2,1)S(1)}, bf16[704,128]{1,0:T(8,128)(2,1)S(1)}, u32[]{:S(2)}, u32[]{:S(2)}) collective-permute-start(bf16[704,128]{1,0:T(8,128)(2,1)S(1)} %collective-permute-done.refs_0_), channel_id=1, source_target_pairs={{0,64},{16,80},{32,96},{48,112},{64,128},{80,144},{96,160},{112,17... | collective-permute-start | bytes 540680 | tf_op jit(solution)/shard_map/ppermute | solution.py:29
  17.8 10.1 %collective-permute-start.6 = (bf16[704,128]{1,0:T(8,128)(2,1)S(1)}, bf16[704,128]{1,0:T(8,128)(2,1)S(1)}, u32[]{:S(2)}, u32[]{:S(2)}) collective-permute-start(bf16[704,128]{1,0:T(8,128)(2,1)S(1)} %collective-permute-done.refs_0_), channel_id=1, source_target_pairs={{0,128},{16,144},{32,160},{48,176},{64,192},{80,208},{96,224},{112... | collective-permute-start | bytes 540680 | tf_op jit(solution)/shard_map/ppermute | solution.py:29
  18.1 17.0 %collective-permute-start.1 = (bf16[704,128]{1,0:T(8,128)(2,1)S(1)}, bf16[704,128]{1,0:T(8,128)(2,1)S(1)}, u32[]{:S(2)}, u32[]{:S(2)}) collective-permute-start(bf16[704,128]{1,0:T(8,128)(2,1)S(1)} %collective-permute-done.refs_0_), channel_id=1, source_target_pairs={{0,16},{16,0},{32,48},{48,32},{64,80},{80,64},{96,112},{112,96},{1... | collective-permute-start | bytes 540680 | tf_op jit(solution)/shard_map/ppermute | solution.py:37
  18.1 13.4 %collective-permute-start.14 = (bf16[704,128]{1,0:T(8,128)(2,1)S(1)}, bf16[704,128]{1,0:T(8,128)(2,1)S(1)}, u32[]{:S(2)}, u32[]{:S(2)}) collective-permute-start(bf16[704,128]{1,0:T(8,128)(2,1)S(1)} %collective-permute-done.13.refs_6_), channel_id=1, source_target_pairs={{0,16},{16,0},{32,48},{48,32},{64,80},{80,64},{96,112},{112,96},{1... | collective-permute-start | bytes 540680 | tf_op jit(solution)/shard_map/ppermute | solution.py:37
  23.2 11.9 %collective-permute-start.3 = (bf16[704,128]{1,0:T(8,128)(2,1)S(1)}, bf16[704,128]{1,0:T(8,128)(2,1)S(1)}, u32[]{:S(2)}, u32[]{:S(2)}) collective-permute-start(bf16[704,128]{1,0:T(8,128)(2,1)S(1)} %collective-permute-done.2.refs_2_), channel_id=1, source_target_pairs={{0,16},{16,0},{32,48},{48,32},{64,80},{80,64},{96,112},{112,96},{1... | collective-permute-start | bytes 540680 | tf_op jit(solution)/shard_map/ppermute | solution.py:37
  27.9 7.2 %collective-permute-start.5 = (bf16[704,128]{1,0:T(8,128)(2,1)S(1)}, bf16[704,128]{1,0:T(8,128)(2,1)S(1)}, u32[]{:S(2)}, u32[]{:S(2)}) collective-permute-start(bf16[704,128]{1,0:T(8,128)(2,1)S(1)} %collective-permute-done.4.refs_4_), channel_id=1, source_target_pairs={{0,16},{16,0},{32,48},{48,32},{64,80},{80,64},{96,112},{112,96},{1... | collective-permute-start | bytes 540680 | tf_op jit(solution)/shard_map/ppermute | solution.py:37
  27.9 7.2 %collective-permute-start.7 = (bf16[704,128]{1,0:T(8,128)(2,1)S(1)}, bf16[704,128]{1,0:T(8,128)(2,1)S(1)}, u32[]{:S(2)}, u32[]{:S(2)}) collective-permute-start(bf16[704,128]{1,0:T(8,128)(2,1)S(1)} %collective-permute-done.6.refs_6_), channel_id=1, source_target_pairs={{0,16},{16,0},{32,48},{48,32},{64,80},{80,64},{96,112},{112,96},{1... | collective-permute-start | bytes 540680 | tf_op jit(solution)/shard_map/ppermute | solution.py:37
  28.4 1.7 %copy-start = (bf16[256,8,576]{0,2,1:T(8,128)(2,1)S(1)}, bf16[256,8,576]{0,2,1:T(8,128)(2,1)}, u32[]{:S(2)}) copy-start(bf16[256,8,576]{0,2,1:T(8,128)(2,1)} %param.7) | copy-start | bytes 7077892
  30.0 0.7 copy-start.1
  35.1 9.1 %copy-start.4 = (f32[256,4]{0,1:T(4,128)S(1)}, f32[256,4]{0,1:T(4,128)}, u32[]{:S(2)}) copy-start(f32[256,4]{0,1:T(4,128)} %param.12) | copy-start | bytes 12292
  35.1 10.0 %copy-start.3 = (bf16[256,4,128]{2,1,0:T(4,128)(2,1)S(1)}, bf16[256,4,128]{2,1,0:T(4,128)(2,1)}, u32[]{:S(2)}) copy-start(bf16[256,4,128]{2,1,0:T(4,128)(2,1)} %param.10) | copy-start | bytes 786436
  39.8 44.6 %copy-start.2 = (s32[2,16]{1,0:T(2,128)S(1)}, s32[2,16]{1,0:T(2,128)}, u32[]{:S(2)}) copy-start(s32[2,16]{1,0:T(2,128)} %kept_ref.3) | copy-start | bytes 388
  39.8 19.7 %all-to-all-start.1 = ((bf16[4,64,2048]{2,1,0:T(8,128)(2,1)}), bf16[4,64,2048]{2,1,0:T(8,128)(2,1)S(1)}, u32[]{:S(2)}, u32[]{:S(2)}) async-start(bf16[4,64,2048]{2,1,0:T(8,128)(2,1)} %bitcast.8), calls=%async_computation.1 | async-start | bytes 2097152 | tf_op jit(solution)/shard_map/all_to_all | solution.py:41
  59.5 21.4 %all-to-all-start = ((bf16[16,80,128]{2,1,0:T(8,128)(2,1)}), bf16[16,80,128]{2,1,0:T(8,128)(2,1)S(1)}, u32[]{:S(2)}, u32[]{:S(2)}) async-start(bf16[16,80,128]{2,1,0:T(8,128)(2,1)} %pad_maximum_fusion.1), calls=%async_computation | async-start | bytes 655360 | tf_op jit(solution)/shard_map/all_to_all | solution.py:41
  80.9 12.6 %all-to-all-start.2 = ((bf16[4,16,2048]{2,1,0:T(8,128)(2,1)}), bf16[4,16,2048]{2,1,0:T(8,128)(2,1)S(1)}, u32[]{:S(2)}, u32[]{:S(2)}) async-start(bf16[4,16,2048]{2,1,0:T(8,128)(2,1)} %bitcast.9), calls=%async_computation.2 | async-start | bytes 524288 | tf_op jit(solution)/shard_map/all_to_all | solution.py:41
  98.1 1.6 %collective-permute-start.15 = (bf16[8,128,128]{2,1,0:T(8,128)(2,1)S(1)}, bf16[8,128,128]{2,1,0:T(8,128)(2,1)S(1)}, u32[]{:S(2)}, u32[]{:S(2)}) collective-permute-start(bf16[8,128,128]{2,1,0:T(8,128)(2,1)S(1)} %get-tuple-element.15), channel_id=1, source_target_pairs={{0,16},{16,0},{32,48},{48,32},{64,80},{80,64},{96,112},{112,96},{1... | collective-permute-start | bytes 786440 | tf_op jit(solution)/shard_map/ppermute | solution.py:37

commit v2 on v1

--- a/solution.py
+++ b/solution.py
@@ -15,6 +15,7 @@
 bf16 = jnp.bfloat16
 VM = pl.BlockSpec(memory_space=pltpu.VMEM)
 SM = pl.BlockSpec(memory_space=pltpu.SMEM)
+HB = pl.BlockSpec(memory_space=pltpu.HBM)
 
 ROW_X = [[zh * 4 + x for x in range(4)] for zh in range(4)]
 ROW_ZH = [[zh * 4 + x for zh in range(4)] for x in range(4)]
@@ -37,6 +38,14 @@
     return lax.ppermute(value, "seq", [(i, i ^ 1) for i in range(16)])
 
 
+def along_x(value, d):
+    return lax.ppermute(value, "head", [(i, i // 4 * 4 + (i + d) % 4) for i in range(16)])
+
+
+def along_zh(value, d):
+    return lax.ppermute(value, "head", [(i, (i + 4 * d) % 16) for i in range(16)])
+
+
 def exchanged(value, axis, groups=None):
     return lax.all_to_all(value, axis, 0, 0, tiled=True, axis_index_groups=groups)
 
@@ -45,84 +54,129 @@
     return jax.ShapeDtypeStruct(shape, dtype)
 
 
-def call(body, outs, specs, mib, **more):
+def call(body, outs, specs, mib, out_specs=None, **more):
     return pl.pallas_call(
         body,
         out_shape=outs,
         in_specs=specs,
-        out_specs=jax.tree.map(lambda _: VM, outs),
+        out_specs=out_specs or jax.tree.map(lambda _: VM, outs),
         compiler_params=pltpu.CompilerParams(vmem_limit_bytes=mib << 20),
         **more,
     )
 
 
-def query_body(q_ref, lse_ref, out_ref, wide):
+def query_body(q_ref, lse_ref, out_ref, wide, turned, in_sem, out_sem):
     heads, width, rows = q_ref.shape
+    loads = [
+        pltpu.make_async_copy(q_ref.at[h], wide.at[h, 0:width, :], in_sem.at[h]) for h in range(heads)
+    ]
+    for load in loads:
+        load.start()
     row = lax.broadcasted_iota(jnp.int32, (640 - width, rows), 0)
+    stores = []
     for h in range(heads):
         value = lse_ref[h : h + 1, :] * (-1.0 / attn_scale)
         p0 = value.astype(bf16).astype(f32)
         p1 = (value - p0).astype(bf16).astype(f32)
         p2 = value - p0 - p1
         more = jnp.where(row == 0, p0, jnp.where(row == 1, p1, jnp.where(row == 2, p2, 0.0)))
-        wide[h, 0:width, :] = q_ref[h]
         wide[h, width:, :] = more.astype(bf16)
-        out_ref[h] = wide[h].T
+        loads[h].wait()
+        flat = wide[h].T
+        for x in range(4):
+            for zh in range(4):
+                at = (zh * 4 + x) * 16
+                turned[h, x, zh * 16 : zh * 16 + 16, :] = flat[at : at + 16]
+        stores.append(pltpu.make_async_copy(turned.at[h], out_ref.at[:, h], out_sem.at[h]))
+        stores[-1].start()
+    for store in stores:
+        store.wait()
 
 
 def wide_queries(query, normalizer):
     heads, _, rows = query.shape
     return call(
         query_body,
-        sds((heads, rows, 640), bf16),
-        [VM, VM],
+        pltpu.HBM((4, heads, rows // 4, 640), bf16),
+        [HB, VM],
         12,
-        scratch_shapes=[pltpu.VMEM((heads, 640, rows), bf16)],
+        out_specs=HB,
+        scratch_shapes=[
+            pltpu.VMEM((heads, 640, rows), bf16),
+            pltpu.VMEM((heads, 4, rows // 4, 640), bf16),
+            pltpu.SemaphoreType.DMA((heads,)),
+            pltpu.SemaphoreType.DMA((heads,)),
+        ],
         name="wide_queries",
-    )(query, normalizer)
-
-
-def score_body(q_ref, *refs):
-    tiles, before, (out_ref, index_ref, keys) = refs[:8], refs[8:-3], refs[-3:]
-    heads, rows, depth = q_ref.shape
+    )(pltpu.with_memory_space_constraint(query, pltpu.HBM), normalizer)
+
+
+def score_body(q_hbm, *refs):
+    tiles, (out_ref, index_ref, q_ref, keys, q_sem, k_sem, i_sem) = refs[:16], refs[16:]
+    groups, heads, rows, depth = q_ref.shape
     width = tiles[0].shape[0] - 128
-    begin = 512 * len(before)
-    if before:
-        out_ref[:, 0:begin] = before[0][...]
-        index_ref[0:begin] = before[1][...]
+    key_loads, index_loads = [], []
     for i, tile in enumerate(tiles):
-        index_ref[begin + i * 128 : begin + i * 128 + 128] = tile[0:128, :]
+        place = keys.at[i // 4, 0:width, i % 4 * 128 : i % 4 * 128 + 128]
+        key_loads.append(pltpu.make_async_copy(tile.at[128 : 128 + width, :], place, k_sem.at[i]))
+        place = index_ref.at[i * 128 : i * 128 + 128, :]
+        index_loads.append(pltpu.make_async_copy(tile.at[0:128, :], place, i_sem.at[i]))
+    q_loads = [
+        pltpu.make_async_copy(q_hbm.at[a], q_ref.at[a], q_sem.at[a]) for a in range(groups)
+    ]
+    for load in q_loads[:1] + key_loads[:4] + q_loads[1:] + key_loads[4:] + index_loads:
+        load.start()
     row = lax.broadcasted_iota(jnp.int32, (depth - width, 512), 0)
-    for n in range(2):
+    for n in range(4):
         keys[n, width:, :] = jnp.where(row < 3, 1.0, 0.0).astype(bf16)
-        for i in range(4):
-            keys[n, 0:width, i * 128 : i * 128 + 128] = tiles[4 * n + i][128:, :]
+        for load in key_loads[4 * n : 4 * n + 4]:
+            load.wait()
         total = None
-        for h in range(0, heads, 2):
-            both = q_ref[h : h + 2].reshape(2 * rows, depth)
-            s = jnp.dot(both, keys[n], preferred_element_type=f32)
+        for a in range(groups):
+            if n == 0:
+                q_loads[a].wait()
+            some = q_ref[a].reshape(heads * rows, depth)
+            s = jnp.dot(some, keys[n], preferred_element_type=f32)
             p = jnp.exp2(s * (attn_scale * LOG2E))
-            p = p[:rows] + p[rows:]
-            total = p if total is None else total + p
-        for x in range(4):
-            for zh in range(4):
-                to, at = (x * 4 + zh) * 16, (zh * 4 + x) * 16
-                out_ref[to : to + 16, begin + n * 512 : begin + n * 512 + 512] = total[
-                    at : at + 16
-                ].astype(bf16)
-
-
-def scores(query, tiles, *before):
-    _, rows, depth = query.shape
-    cols = 1024 + 512 * len(before)
+            for h in range(heads):
+                part = p[h * rows : h * rows + rows]
+                total = part if total is None else total + part
+        out_ref[:, n * 512 : n * 512 + 512] = total.astype(bf16)
+    for load in index_loads:
+        load.wait()
+
+
+def scores(query, tiles):
+    groups, _, rows, depth = query.shape
     return call(
         score_body,
-        (sds((rows, cols), bf16), sds((cols, 128), bf16)),
-        [VM] * (9 + len(before)),
-        14,
-        scratch_shapes=[pltpu.VMEM((2, depth, 512), bf16)],
+        (sds((rows, 2048), bf16), sds((2048, 128), bf16)),
+        [HB] * 17,
+        16,
+        scratch_shapes=[
+            pltpu.VMEM(query.shape, bf16),
+            pltpu.VMEM((4, depth, 512), bf16),
+            pltpu.SemaphoreType.DMA((groups,)),
+            pltpu.SemaphoreType.DMA((16,)),
+            pltpu.SemaphoreType.DMA((16,)),
+        ],
         name="scores",
-    )(query, *tiles, *before)
+    )(*[pltpu.with_memory_space_constraint(v, pltpu.HBM) for v in (query, *tiles)])
+
+
+def pack_body(at_ref, q_ref, w_ref, *outs):
+    for d, ref in zip((0,) + STEPS, outs):
+        x = lax.rem(at_ref[1] + d, 4)
+        for zh in range(4):
+            ref[zh, 0:64, :] = q_ref[zh * 4 + x]
+            ref[zh, 64:80, :] = w_ref[zh * 4 + x]
+
+
+def spread_body(at_ref, *refs):
+    for d, ref in zip((0,) + STEPS, refs[4:]):
+        zh = lax.rem(at_ref[0] + d, 4)
+        for a in range(4):
+            ref[a] = refs[a][zh]
 
 
 def weight_column(q_ref, j):
@@ -133,14 +187,14 @@
 
 def slot_tile(at_ref, slot):
     u, k, v = slot // 8, slot // 2 % 4, slot % 2
-    y = lax.rem(at_ref[1] + ((0,) + STEPS)[k], 4)
-    z = at_ref[2] if u == 0 else 1 - at_ref[2]
-    c = at_ref[3] if v == 0 else 1 - at_ref[3]
+    y = lax.rem(at_ref[2] + ((0,) + STEPS)[k], 4)
+    z = at_ref[3] if u == 0 else 1 - at_ref[3]
+    c = at_ref[4] if v == 0 else 1 - at_ref[4]
     return y * 4 + z * 2 + c
 
 
 def allowed(at_ref, kept_ref):
-    half = jnp.where(at_ref[0] >= 8, 1, 0)
+    half = jnp.where(at_ref[0] >= 2, 1, 0)
     flags = [
         jnp.full((16, 128), kept_ref[half, slot_tile(at_ref, slot)], jnp.int32) for slot in range(16)
     ]
@@ -151,7 +205,11 @@
 TN = (((0,), (0,)), ((), ()))
 
 
-def index_body(scale, at_ref, kept_ref, q_ref, keys, prob_ref, acc):
+def index_body(scale, at_ref, kept_ref, *refs):
+    keys, prob_ref, q_ref, acc = refs[4:]
+    for g in range(4):
+        for a in range(4):
+            q_ref[4 * g + a] = refs[g][a]
     acc[...] = jnp.zeros_like(acc)
 
     @pl.loop(0, 4)
@@ -179,12 +237,12 @@
 def index_forward(at, kept, queries, keys, scale):
     return call(
         functools.partial(index_body, scale),
-        sds((16, 2048), f32),
-        [SM, SM, VM, VM],
+        (sds((16, 2048), f32), sds((16, 80, 128), bf16)),
+        [SM, SM] + [VM] * 5,
         14,
         scratch_shapes=[pltpu.VMEM((64, 2048), f32)],
         name="index_forward",
-    )(at, kept, queries, keys)
+    )(at, kept, *queries, keys)
 
 
 def back_body(scale, at_ref, kept_ref, prob_ref, q_ref, keys, sums, *refs):
@@ -208,7 +266,11 @@
             dz[at : at + 64, :] = jnp.where(z[at : at + 64] > 0.0, value, 0.0).astype(bf16)
         dk[...] += lax.dot_general(rows, dz[...], TN, preferred_element_type=f32)
         dq = jnp.dot(dz[...], keys[...], preferred_element_type=f32) * scale
-        dq_ref[pl.ds(4 * g, 4)] = dq.astype(bf16).reshape(4, 64, 128)
+        e = jnp.where(g < 2, g, 5 - g)
+        zh = lax.rem(at_ref[0] + 4 - e, 4)
+        for a, d in enumerate((0,) + STEPS):
+            x = lax.rem(at_ref[1] + 4 - d, 4)
+            dq_ref[zh * 4 + x] = dq[a * 64 : a * 64 + 64].astype(bf16)
 
     for slot in range(16):
         tile = dk[:, slot * 128 : slot * 128 + 128] * scale
@@ -238,7 +300,7 @@
     index_scale = index_query.shape[2] ** (-0.5)
     head = lax.axis_index("head")
     seq = lax.axis_index("seq")
-    at = jnp.stack([head, seq // 4, seq // 2 % 2, seq % 2]).astype(jnp.int32)
+    at = jnp.stack([head // 4, head % 4, seq // 4, seq // 2 % 2, seq % 2]).astype(jnp.int32)
 
     tile = jnp.concatenate([index_key, key_latent.T], axis=0)
     tiles = []
@@ -254,17 +316,24 @@
     w2 = index_weight - w0 - w1
     weight = jnp.stack([w.reshape(16, 64) for w in (w0, w1, w2)], axis=1).astype(bf16)
     weight = jnp.pad(weight, ((0, 0), (0, 13), (0, 64)))
-    queries = jnp.concatenate([index_query.reshape(16, 64, 128), weight], axis=1)
-    queries = exchanged(queries, "head")
+    four = (sds((4, 80, 128), bf16),) * 4
+    parts = call(pack_body, four, [SM, VM, VM], 6, name="pack")(
+        at, index_query.reshape(16, 64, 128), weight
+    )
+    got = [parts[0]]
+    for part, d in zip(parts[1:], STEPS):
+        got.append(along_x(part, d))
+    parts = call(spread_body, four, [SM] + [VM] * 4, 6, name="spread")(at, *got)
+    queries = [parts[0]]
+    for part, d in zip(parts[1:], STEPS):
+        queries.append(along_zh(part, d))
 
     query = wide_queries(jnp.transpose(query_latent, (1, 2, 0)), normalizer.T)
-    first = scores(query, tiles[:8])
-    part, index_keys = scores(query, tiles[8:], *first)
-    part = exchanged(part.reshape(4, 64, 2048), "head", ROW_X)
-    part = jnp.sum(part.astype(f32), axis=0).astype(bf16)
+    query = exchanged(query, "head", ROW_X)
+    part, index_keys = scores(query, tiles)
     sums = exchanged(part.reshape(4, 16, 2048), "head", ROW_ZH)
 
-    prob = index_forward(at, kept, queries, index_keys, index_scale)
+    prob, queries = index_forward(at, kept, queries, index_keys, index_scale)
     own, send, dq = index_backward(at, kept, prob, queries, index_keys, sums, index_scale)
 
     got = other_core(send)

time: 135 us -> 132 us (0.978)
  waiting for transfers between devices: 51.4 us -> 33.3 us
  starting transfers between devices: 25 us -> 34.4 us
  Pallas kernels: 16.5 us -> 22.7 us
  blocking collectives: 31.2 us -> 34.1 us
  other arithmetic: 2.9 us -> 0.23 us
    all_to_all x3 -> x2, waiting for transfers between devices: 31.8 us -> 3.13 us  [exchanged(): lax.all_to_all(value, axis, 0, 0, tiled=True, axis_index_groups=groups)]
    ppermute x0 -> x6, starting transfers between devices: none -> 13.5 us  [the longest x3 10.1 us: along_zh(): lax.ppermute(value, 'head', [(i, (i + 4 * d) % 16) for i in range(16)])]
    ppermute x0 -> x6, waiting for transfers between devices: none -> 9.33 us  [the longest x3 5.94 us: along_x(): lax.ppermute(value, 'head', [(i, i // 4 * 4 + (i + d) % 4) for i in range...]
    pallas_call x4 -> x5, Pallas kernels: 11.9 us -> 17.9 us  [the longest x1 10.8 us: scores(): call(score_body, (sds((rows, 2048), bf16), sds((2048, 128), bf16)), [HB]...]
    all_to_all x3 -> x2, starting transfers between devices: 16.1 us -> 12.3 us  [exchanged(): lax.all_to_all(value, axis, 0, 0, tiled=True, axis_index_groups=groups)]
    all_to_all x2, blocking collectives: 31.2 us -> 34.1 us  [exchanged(): lax.all_to_all(value, axis, 0, 0, tiled=True, axis_index_groups=groups)]
    unnamed x11 -> x45, local copies, waits for them, and re-layouts: 3.11 us -> 2.57 us
  transfers between devices with their start and end apart: 19 -> 24, of which waited for: 8 -> 11; matrix products, arithmetic and copies ran while one was open for 2% -> 1% of each run, Pallas kernels for 6% -> 3%
where the time goes in v2:
time: 132 us; the launch traced here: 130 us
  starting transfers between devices  34.4 us (26%)
  blocking collectives  34.1 us (26%)
  waiting for transfers between devices  33.3 us (25%)
  Pallas kernels  22.7 us (17%)
  local copies, waits for them, and re-layouts  4.24 us (3%)
    all_to_all x2, blocking collectives, exchanged(): lax.all_to_all(value, axis, 0, 0, tiled=True, axis_index_groups=groups)  34.1 us
    ppermute x6, waiting for transfers between devices, along_y(): lax.ppermute(value, 'seq', [(i, (i + 4 * d) % 16) for i in range(16)])  18.1 us
    all_to_all x2, starting transfers between devices, exchanged(): lax.all_to_all(value, axis, 0, 0, tiled=True, axis_index_groups=groups)  12.3 us
    pallas_call x1, Pallas kernels, scores(): call(score_body, (sds((rows, 2048), bf16), sds((2048, 128), bf16)), [HB]...  10.8 us
    ppermute x3, starting transfers between devices, along_zh(): lax.ppermute(value, 'head', [(i, (i + 4 * d) % 16) for i in range(16)])  10.1 us
    ppermute x6, starting transfers between devices, along_y(): lax.ppermute(value, 'seq', [(i, (i + 4 * d) % 16) for i in range(16)])  6.66 us
    ppermute x3, waiting for transfers between devices, along_x(): lax.ppermute(value, 'head', [(i, i // 4 * 4 + (i + d) % 4) for i in range...  5.94 us
    pallas_call x1, Pallas kernels, index_backward(): call(functools.partial(back_body, scale), (sds((8, 128, 128), f32), sds((...  4.71 us
  transfers between devices with their start and end apart: 24, of which 11 were waited for; matrix products, arithmetic and copies ran while one was open for 1% of the time, Pallas kernels for 3%

profile of v2, /device:TPU:32, one launch (start us, length us, event | category | flops | bytes accessed | tf_op | source)
XLA Modules:
  0.0 129.9 jit_solution(3608467579079371989)
XLA Ops:
  0.6 0.7 copy-done.1
  1.3 3.0 %wide_queries.1 = bf16[4,8,64,640]{3,2,1,0:T(8,128)(2,1)} custom-call(bf16[8,576,256]{2,1,0:T(8,128)(2,1)} %bitcast.19, f32[8,256]{1,0:T(8,128)S(1)} %bitcast.18), custom_call_target="tpu_custom_call" | custom-call | tf_op jit(solution)/shard_map/wide_queries/pallas_call | solution.py:98
  4.3 0.0 copy-start.19
  4.3 0.0 copy-start.20
  4.3 4.7 %all-to-all-start = ((bf16[4,8,64,640]{3,2,1,0:T(8,128)(2,1)}), bf16[4,8,64,640]{3,2,1,0:T(8,128)(2,1)}, u32[]{:S(2)}, u32[]{:S(2)}) async-start(bf16[4,8,64,640]{3,2,1,0:T(8,128)(2,1)} %wide_queries.1), calls=%async_computation | async-start | bytes 5242880 | tf_op jit(solution)/shard_map/all_to_all | solution.py:50
  9.1 3.1 %collective-permute-start.7 = (bf16[704,128]{1,0:T(8,128)(2,1)S(1)}, bf16[704,128]{1,0:T(8,128)(2,1)S(1)}, u32[]{:S(2)}, u32[]{:S(2)}) collective-permute-start(bf16[704,128]{1,0:T(8,128)(2,1)S(1)} %pad_maximum_fusion.1.refs_0_), channel_id=1, source_target_pairs={{0,192},{16,208},{32,224},{48,240},{64,0},{80,16},{96,32},{112,48}... | collective-permute-start | bytes 540680 | tf_op jit(solution)/shard_map/ppermute | solution.py:30
  12.2 0.0 collective-permute-start.9
  12.2 0.8 collective-permute-start.13
  13.0 0.0 collective-permute-start.6
  13.0 1.5 %collective-permute-start.11 = (bf16[704,128]{1,0:T(8,128)(2,1)S(1)}, bf16[704,128]{1,0:T(8,128)(2,1)S(1)}, u32[]{:S(2)}, u32[]{:S(2)}) collective-permute-start(bf16[704,128]{1,0:T(8,128)(2,1)S(1)} %pad_maximum_fusion.1.refs_0_), channel_id=1, source_target_pairs={{0,128},{16,144},{32,160},{48,176},{64,192},{80,208},{96,224},{112... | collective-permute-start | bytes 540680 | tf_op jit(solution)/shard_map/ppermute | solution.py:30
  14.5 1.5 %collective-permute-done.7.refs_2_ = bf16[704,128]{1,0:T(8,128)(2,1)S(1)} collective-permute-done((bf16[704,128]{1,0:T(8,128)(2,1)S(1)}, bf16[704,128]{1,0:T(8,128)(2,1)S(1)}, u32[]{:S(2)}, u32[]{:S(2)}) %collective-permute-start.7) | collective-permute-done | bytes 180256 | tf_op jit(solution)/shard_map/ppermute | solution.py:30
  16.0 0.0 collective-permute-start.8
  16.0 7.3 %collective-permute-done.9.refs_4_ = bf16[704,128]{1,0:T(8,128)(2,1)S(1)} collective-permute-done((bf16[704,128]{1,0:T(8,128)(2,1)S(1)}, bf16[704,128]{1,0:T(8,128)(2,1)S(1)}, u32[]{:S(2)}, u32[]{:S(2)}) %collective-permute-start.9) | collective-permute-done | bytes 180256 | tf_op jit(solution)/shard_map/ppermute | solution.py:30
  23.3 0.0 collective-permute-start.10
  23.3 0.0 collective-permute-done.13.refs_8_
  23.3 0.1 collective-permute-start.15
  23.4 2.0 %collective-permute-start.17 = (bf16[704,128]{1,0:T(8,128)(2,1)S(1)}, bf16[704,128]{1,0:T(8,128)(2,1)S(1)}, u32[]{:S(2)}, u32[]{:S(2)}) collective-permute-start(bf16[704,128]{1,0:T(8,128)(2,1)S(1)} %collective-permute-done.13.refs_8_), channel_id=1, source_target_pairs={{0,64},{16,80},{32,96},{48,112},{64,128},{80,144},{96,160},{112,17... | collective-permute-start | bytes 540680 | tf_op jit(solution)/shard_map/ppermute | solution.py:30
  25.4 0.0 collective-permute-done.11.refs_6_
  25.4 0.0 collective-permute-start.19
  25.4 0.1 collective-permute-start.14
  25.6 0.5 collective-permute-start.12
  26.0 4.8 %collective-permute-done.15.refs_10_ = bf16[704,128]{1,0:T(8,128)(2,1)S(1)} collective-permute-done((bf16[704,128]{1,0:T(8,128)(2,1)S(1)}, bf16[704,128]{1,0:T(8,128)(2,1)S(1)}, u32[]{:S(2)}, u32[]{:S(2)}) %collective-permute-start.15) | collective-permute-done | bytes 180256 | tf_op jit(solution)/shard_map/ppermute | solution.py:30
  30.8 4.6 %collective-permute-done.17.refs_12_ = bf16[704,128]{1,0:T(8,128)(2,1)S(1)} collective-permute-done((bf16[704,128]{1,0:T(8,128)(2,1)S(1)}, bf16[704,128]{1,0:T(8,128)(2,1)S(1)}, u32[]{:S(2)}, u32[]{:S(2)}) %collective-permute-start.17) | collective-permute-done | bytes 180256 | tf_op jit(solution)/shard_map/ppermute | solution.py:30
  35.4 0.0 collective-permute-start.18
  35.4 0.0 collective-permute-done.19.refs_14_
  35.4 0.5 collective-permute-start.20
  35.9 0.0 collective-permute-done.12.refs_7_
  36.0 0.0 collective-permute-done.16.refs_11_
  36.0 0.8 collective-permute-done.18.refs_13_
  36.8 0.3 collective-permute-done.20.refs_15_
  37.1 0.4 copy-done.17
  37.5 0.7 copy-done.18
  38.2 3.1 %all-to-all-done.q_hbm = bf16[4,8,64,640]{3,2,1,0:T(8,128)(2,1)} async-done(((bf16[4,8,64,640]{3,2,1,0:T(8,128)(2,1)}), bf16[4,8,64,640]{3,2,1,0:T(8,128)(2,1)}, u32[]{:S(2)}, u32[]{:S(2)}) %all-to-all-start) | async-done | bytes 2621472 | tf_op jit(solution)/shard_map/all_to_all | solution.py:50
  41.4 10.8 %scores.1 = (bf16[64,2048]{1,0:T(8,128)(2,1)}, bf16[2048,128]{1,0:T(8,128)(2,1)S(1)}) custom-call(bf16[4,8,64,640]{3,2,1,0:T(8,128)(2,1)} %all-to-all-done.q_hbm, bf16[704,128]{1,0:T(8,128)(2,1)} %copy-done.3, bf16[704,128]{1,0:T(8,128)(2,1)} %copy-done.7, bf16[704,128]{1,0:T(8,128)(2,1)} %copy-done.4, bf16[704,128]{1,0:T(8,128)(2,1)} %copy-done.9, ...), custom_call_target="tpu_custom_call" | custom-call | tf_op jit(solution)/shard_map/scores/pallas_call | solution.py:151
  52.3 7.6 %all-to-all-start.1 = ((bf16[4,16,2048]{2,1,0:T(8,128)(2,1)}), bf16[4,16,2048]{2,1,0:T(8,128)(2,1)S(1)}, u32[]{:S(2)}, u32[]{:S(2)}) async-start(bf16[4,16,2048]{2,1,0:T(8,128)(2,1)} %bitcast.9), calls=%async_computation.1 | async-start | bytes 524288 | tf_op jit(solution)/shard_map/all_to_all | solution.py:50
  59.8 0.1 copy.14
  60.0 0.1 stack_reshape.17
  60.1 0.1 copy.13
  60.3 0.1 stack_reshape.16
  60.4 0.1 copy.12
  60.5 0.1 stack_reshape.15
  60.7 0.1 stack.27.at_ref
  60.8 0.1 fusion.8.w_ref
  60.9 0.6 pack.1
  61.4 0.6 collective-permute-start
  62.1 2.7 %collective-permute-start.1 = (bf16[4,80,128]{2,1,0:T(8,128)(2,1)S(1)}, bf16[4,80,128]{2,1,0:T(8,128)(2,1)S(1)}, u32[]{:S(2)}, u32[]{:S(2)}) collective-permute-start(bf16[4,80,128]{2,1,0:T(8,128)(2,1)S(1)} %get-tuple-element.19), channel_id=1, source_target_pairs={{0,3},{1,0},{2,1},{3,2},{4,7},{5,4},{6,5},{7,6},{8,11},{9,8},{10,9... | collective-permute-start | bytes 245768 | tf_op jit(solution)/shard_map/ppermute | solution.py:42
  64.7 0.0 collective-permute-start.2
  64.8 3.3 %collective-permute-done.refs_1_ = bf16[4,80,128]{2,1,0:T(8,128)(2,1)S(1)} collective-permute-done((bf16[4,80,128]{2,1,0:T(8,128)(2,1)S(1)}, bf16[4,80,128]{2,1,0:T(8,128)(2,1)S(1)}, u32[]{:S(2)}, u32[]{:S(2)}) %collective-permute-start) | collective-permute-done | bytes 81952 | tf_op jit(solution)/shard_map/ppermute | solution.py:42
  68.0 2.6 %collective-permute-done.2.refs_3_ = bf16[4,80,128]{2,1,0:T(8,128)(2,1)S(1)} collective-permute-done((bf16[4,80,128]{2,1,0:T(8,128)(2,1)S(1)}, bf16[4,80,128]{2,1,0:T(8,128)(2,1)S(1)}, u32[]{:S(2)}, u32[]{:S(2)}) %collective-permute-start.2) | collective-permute-done | bytes 81952 | tf_op jit(solution)/shard_map/ppermute | solution.py:42
  70.7 0.6 spread.1
  71.3 3.0 %collective-permute-start.3 = (bf16[4,80,128]{2,1,0:T(8,128)(2,1)S(1)}, bf16[4,80,128]{2,1,0:T(8,128)(2,1)S(1)}, u32[]{:S(2)}, u32[]{:S(2)}) collective-permute-start(bf16[4,80,128]{2,1,0:T(8,128)(2,1)S(1)} %get-tuple-element.22), channel_id=1, source_target_pairs={{0,4},{1,5},{2,6},{3,7},{4,8},{5,9},{6,10},{7,11},{8,12},{9,13},{1... | collective-permute-start | bytes 245768 | tf_op jit(solution)/shard_map/ppermute | solution.py:46
  74.3 1.3 %collective-permute-start.4 = (bf16[4,80,128]{2,1,0:T(8,128)(2,1)S(1)}, bf16[4,80,128]{2,1,0:T(8,128)(2,1)S(1)}, u32[]{:S(2)}, u32[]{:S(2)}) collective-permute-start(bf16[4,80,128]{2,1,0:T(8,128)(2,1)S(1)} %get-tuple-element.23), channel_id=1, source_target_pairs={{0,12},{1,13},{2,14},{3,15},{4,0},{5,1},{6,2},{7,3},{8,4},{9,5},{1... | collective-permute-start | bytes 245768 | tf_op jit(solution)/shard_map/ppermute | solution.py:46
  75.6 5.8 %collective-permute-start.5 = (bf16[4,80,128]{2,1,0:T(8,128)(2,1)S(1)}, bf16[4,80,128]{2,1,0:T(8,128)(2,1)S(1)}, u32[]{:S(2)}, u32[]{:S(2)}) collective-permute-start(bf16[4,80,128]{2,1,0:T(8,128)(2,1)S(1)} %get-tuple-element.24), channel_id=1, source_target_pairs={{0,8},{1,9},{2,10},{3,11},{4,12},{5,13},{6,14},{7,15},{8,0},{9,1},... | collective-permute-start | bytes 245768 | tf_op jit(solution)/shard_map/ppermute | solution.py:46
  81.4 3.4 %collective-permute-done.5.refs_3_ = bf16[4,80,128]{2,1,0:T(8,128)(2,1)S(1)} collective-permute-done((bf16[4,80,128]{2,1,0:T(8,128)(2,1)S(1)}, bf16[4,80,128]{2,1,0:T(8,128)(2,1)S(1)}, u32[]{:S(2)}, u32[]{:S(2)}) %collective-permute-start.5) | collective-permute-done | bytes 81952 | tf_op jit(solution)/shard_map/ppermute | solution.py:46
  84.8 3.0 %index_forward.1 = (f32[16,2048]{1,0:T(8,128)S(1)}, bf16[16,80,128]{2,1,0:T(8,128)(2,1)S(1)}) custom-call(s32[5]{0:T(128)S(1)} %stack.27.at_ref, s32[2,16]{1,0:T(2,128)S(1)} %copy-done.2, bf16[4,80,128]{2,1,0:T(8,128)(2,1)S(1)} %get-tuple-element.21.refs_0_, bf16[4,80,128]{2,1,0:T(8,128)(2,1)S(1)} %collective-permute-done.3.refs_1_, ...), custom_call_target="tpu_custom_call" | custom-call | tf_op jit(solution)/shard_map/index_forward/pallas_call | solution.py:238
  87.8 4.7 %index_backward.1 = (f32[8,128,128]{2,1,0:T(8,128)S(1)}, bf16[8,128,128]{2,1,0:T(8,128)(2,1)S(1)}, bf16[16,64,128]{2,1,0:T(8,128)(2,1)S(1)}) custom-call(s32[5]{0:T(128)S(1)} %stack.27.at_ref, s32[2,16]{1,0:T(2,128)S(1)} %copy-done.2, f32[16,2048]{1,0:T(8,128)S(1)} %get-tuple-element.26.prob_ref, bf16[16,80,128]{2,1,0:T(8,128)(2,1)S(1)} %get-tuple-element.27.q_ref, ...), custom_call_target="tpu_custom_call" | custom-call | tf_op jit(solution)/shard_map/index_backward/pallas_call | solution.py:285
  92.6 0.1 collective-permute-start.21
  92.7 1.5 %collective-permute-done.21 = bf16[8,128,128]{2,1,0:T(8,128)(2,1)S(1)} collective-permute-done((bf16[8,128,128]{2,1,0:T(8,128)(2,1)S(1)}, bf16[8,128,128]{2,1,0:T(8,128)(2,1)S(1)}, u32[]{:S(2)}, u32[]{:S(2)}) %collective-permute-start.21) | collective-permute-done | bytes 262176 | tf_op jit(solution)/shard_map/ppermute | solution.py:38
  94.2 0.1 add_convert_fusion
  94.2 14.3 %all_to_all.20 = bf16[32,32,128]{2,1,0:T(8,128)(2,1)S(1)} all-to-all(bf16[32,32,128]{2,1,0:T(8,128)(2,1)S(1)} %bitcast.20), channel_id=1, replica_groups={{0,1,2,3,32,33,34,35,64,65,66,67,96,97,98,99,128,129,130,131,160,161,16..., dimensions={0} | all-to-all | bytes 524288 | tf_op jit(solution)/shard_map/all_to_all | solution.py:50
  108.5 0.1 reduce_sum.21
  108.6 19.8 %all_to_all.21 = bf16[16,96,128]{2,1,0:T(8,128)(2,1)S(1)} all-to-all(bf16[16,96,128]{2,1,0:T(8,128)(2,1)S(1)} %pad_maximum_fusion), channel_id=1, replica_groups=mesh['seq'=16,'head'=16] {'head'}, dimensions={0} | all-to-all | bytes 786432 | tf_op jit(solution)/shard_map/all_to_all | solution.py:50
  128.5 0.7 copy.18
  129.2 0.7 slice.8
  (54 shorter events, 0.2 us)
Async XLA Ops:
  0.6 0.7 copy-start.1
  4.3 4.7 %copy-start.19 = (bf16[128,576]{0,1:T(8,128)(2,1)S(1)}, bf16[128,576]{0,1:T(8,128)(2,1)}, u32[]{:S(2)}) copy-start(bf16[128,576]{0,1:T(8,128)(2,1)} %param.8) | copy-start | bytes 442372
  4.3 4.7 %copy-start.20 = (bf16[128,128]{1,0:T(8,128)(2,1)S(1)}, bf16[128,128]{1,0:T(8,128)(2,1)}, u32[]{:S(2)}) copy-start(bf16[128,128]{1,0:T(8,128)(2,1)} %param.11) | copy-start | bytes 98308
  4.3 37.0 %all-to-all-start = ((bf16[4,8,64,640]{3,2,1,0:T(8,128)(2,1)}), bf16[4,8,64,640]{3,2,1,0:T(8,128)(2,1)}, u32[]{:S(2)}, u32[]{:S(2)}) async-start(bf16[4,8,64,640]{3,2,1,0:T(8,128)(2,1)} %wide_queries.1), calls=%async_computation | async-start | bytes 5242880 | tf_op jit(solution)/shard_map/all_to_all | solution.py:50
  9.1 32.2 %copy-start.3 = (bf16[704,128]{1,0:T(8,128)(2,1)}, bf16[704,128]{1,0:T(8,128)(2,1)S(1)}, u32[]{:S(2)}) copy-start(bf16[704,128]{1,0:T(8,128)(2,1)S(1)} %pad_maximum_fusion.1.refs_0_) | copy-start | bytes 540676
  9.1 6.9 %collective-permute-start.7 = (bf16[704,128]{1,0:T(8,128)(2,1)S(1)}, bf16[704,128]{1,0:T(8,128)(2,1)S(1)}, u32[]{:S(2)}, u32[]{:S(2)}) collective-permute-start(bf16[704,128]{1,0:T(8,128)(2,1)S(1)} %pad_maximum_fusion.1.refs_0_), channel_id=1, source_target_pairs={{0,192},{16,208},{32,224},{48,240},{64,0},{80,16},{96,32},{112,48}... | collective-permute-start | bytes 540680 | tf_op jit(solution)/shard_map/ppermute | solution.py:30
  12.2 11.1 %collective-permute-start.9 = (bf16[704,128]{1,0:T(8,128)(2,1)S(1)}, bf16[704,128]{1,0:T(8,128)(2,1)S(1)}, u32[]{:S(2)}, u32[]{:S(2)}) collective-permute-start(bf16[704,128]{1,0:T(8,128)(2,1)S(1)} %pad_maximum_fusion.1.refs_0_), channel_id=1, source_target_pairs={{0,64},{16,80},{32,96},{48,112},{64,128},{80,144},{96,160},{112,17... | collective-permute-start | bytes 540680 | tf_op jit(solution)/shard_map/ppermute | solution.py:30
  12.2 11.1 %collective-permute-start.13 = (bf16[704,128]{1,0:T(8,128)(2,1)S(1)}, bf16[704,128]{1,0:T(8,128)(2,1)S(1)}, u32[]{:S(2)}, u32[]{:S(2)}) collective-permute-start(bf16[704,128]{1,0:T(8,128)(2,1)S(1)} %pad_maximum_fusion.1.refs_0_), channel_id=1, source_target_pairs={{0,32},{16,48},{32,0},{48,16},{64,96},{80,112},{96,64},{112,80},{1... | collective-permute-start | bytes 540680 | tf_op jit(solution)/shard_map/ppermute | solution.py:34
  13.0 10.4 %collective-permute-start.6 = (bf16[704,128]{1,0:T(8,128)(2,1)S(1)}, bf16[704,128]{1,0:T(8,128)(2,1)S(1)}, u32[]{:S(2)}, u32[]{:S(2)}) collective-permute-start(bf16[704,128]{1,0:T(8,128)(2,1)S(1)} %pad_maximum_fusion.1.refs_0_), channel_id=1, source_target_pairs={{0,16},{16,0},{32,48},{48,32},{64,80},{80,64},{96,112},{112,96},{1... | collective-permute-start | bytes 540680 | tf_op jit(solution)/shard_map/ppermute | solution.py:38
  13.0 12.4 %collective-permute-start.11 = (bf16[704,128]{1,0:T(8,128)(2,1)S(1)}, bf16[704,128]{1,0:T(8,128)(2,1)S(1)}, u32[]{:S(2)}, u32[]{:S(2)}) collective-permute-start(bf16[704,128]{1,0:T(8,128)(2,1)S(1)} %pad_maximum_fusion.1.refs_0_), channel_id=1, source_target_pairs={{0,128},{16,144},{32,160},{48,176},{64,192},{80,208},{96,224},{112... | collective-permute-start | bytes 540680 | tf_op jit(solution)/shard_map/ppermute | solution.py:30
  16.0 25.3 %copy-start.4 = (bf16[704,128]{1,0:T(8,128)(2,1)}, bf16[704,128]{1,0:T(8,128)(2,1)S(1)}, u32[]{:S(2)}) copy-start(bf16[704,128]{1,0:T(8,128)(2,1)S(1)} %collective-permute-done.7.refs_2_) | copy-start | bytes 540676
  16.0 9.4 %collective-permute-start.8 = (bf16[704,128]{1,0:T(8,128)(2,1)S(1)}, bf16[704,128]{1,0:T(8,128)(2,1)S(1)}, u32[]{:S(2)}, u32[]{:S(2)}) collective-permute-start(bf16[704,128]{1,0:T(8,128)(2,1)S(1)} %collective-permute-done.7.refs_2_), channel_id=1, source_target_pairs={{0,16},{16,0},{32,48},{48,32},{64,80},{80,64},{96,112},{112,96},{1... | collective-permute-start | bytes 540680 | tf_op jit(solution)/shard_map/ppermute | solution.py:38
  23.3 18.1 %copy-start.5 = (bf16[704,128]{1,0:T(8,128)(2,1)}, bf16[704,128]{1,0:T(8,128)(2,1)S(1)}, u32[]{:S(2)}) copy-start(bf16[704,128]{1,0:T(8,128)(2,1)S(1)} %collective-permute-done.9.refs_4_) | copy-start | bytes 540676
  23.3 2.3 %collective-permute-start.10 = (bf16[704,128]{1,0:T(8,128)(2,1)S(1)}, bf16[704,128]{1,0:T(8,128)(2,1)S(1)}, u32[]{:S(2)}, u32[]{:S(2)}) collective-permute-start(bf16[704,128]{1,0:T(8,128)(2,1)S(1)} %collective-permute-done.9.refs_4_), channel_id=1, source_target_pairs={{0,16},{16,0},{32,48},{48,32},{64,80},{80,64},{96,112},{112,96},{1... | collective-permute-start | bytes 540680 | tf_op jit(solution)/shard_map/ppermute | solution.py:38
  23.3 18.1 %copy-start.6 = (bf16[704,128]{1,0:T(8,128)(2,1)}, bf16[704,128]{1,0:T(8,128)(2,1)S(1)}, u32[]{:S(2)}) copy-start(bf16[704,128]{1,0:T(8,128)(2,1)S(1)} %collective-permute-done.13.refs_8_) | copy-start | bytes 540676
  23.3 7.5 %collective-permute-start.15 = (bf16[704,128]{1,0:T(8,128)(2,1)S(1)}, bf16[704,128]{1,0:T(8,128)(2,1)S(1)}, u32[]{:S(2)}, u32[]{:S(2)}) collective-permute-start(bf16[704,128]{1,0:T(8,128)(2,1)S(1)} %collective-permute-done.13.refs_8_), channel_id=1, source_target_pairs={{0,192},{16,208},{32,224},{48,240},{64,0},{80,16},{96,32},{112,48}... | collective-permute-start | bytes 540680 | tf_op jit(solution)/shard_map/ppermute | solution.py:30
  23.4 18.0 %copy-start.7 = (bf16[704,128]{1,0:T(8,128)(2,1)}, bf16[704,128]{1,0:T(8,128)(2,1)S(1)}, u32[]{:S(2)}) copy-start(bf16[704,128]{1,0:T(8,128)(2,1)S(1)} %collective-permute-done.6.refs_1_) | copy-start | bytes 540676
  23.4 12.0 %collective-permute-start.17 = (bf16[704,128]{1,0:T(8,128)(2,1)S(1)}, bf16[704,128]{1,0:T(8,128)(2,1)S(1)}, u32[]{:S(2)}, u32[]{:S(2)}) collective-permute-start(bf16[704,128]{1,0:T(8,128)(2,1)S(1)} %collective-permute-done.13.refs_8_), channel_id=1, source_target_pairs={{0,64},{16,80},{32,96},{48,112},{64,128},{80,144},{96,160},{112,17... | collective-permute-start | bytes 540680 | tf_op jit(solution)/shard_map/ppermute | solution.py:30
  25.4 16.0 %copy-start.8 = (bf16[704,128]{1,0:T(8,128)(2,1)}, bf16[704,128]{1,0:T(8,128)(2,1)S(1)}, u32[]{:S(2)}) copy-start(bf16[704,128]{1,0:T(8,128)(2,1)S(1)} %collective-permute-done.11.refs_6_) | copy-start | bytes 540676
  25.4 10.0 %collective-permute-start.19 = (bf16[704,128]{1,0:T(8,128)(2,1)S(1)}, bf16[704,128]{1,0:T(8,128)(2,1)S(1)}, u32[]{:S(2)}, u32[]{:S(2)}) collective-permute-start(bf16[704,128]{1,0:T(8,128)(2,1)S(1)} %collective-permute-done.13.refs_8_), channel_id=1, source_target_pairs={{0,128},{16,144},{32,160},{48,176},{64,192},{80,208},{96,224},{112... | collective-permute-start | bytes 540680 | tf_op jit(solution)/shard_map/ppermute | solution.py:30
  25.4 15.9 %copy-start.9 = (bf16[704,128]{1,0:T(8,128)(2,1)}, bf16[704,128]{1,0:T(8,128)(2,1)S(1)}, u32[]{:S(2)}) copy-start(bf16[704,128]{1,0:T(8,128)(2,1)S(1)} %collective-permute-done.8.refs_3_) | copy-start | bytes 540676
  25.4 10.5 %collective-permute-start.14 = (bf16[704,128]{1,0:T(8,128)(2,1)S(1)}, bf16[704,128]{1,0:T(8,128)(2,1)S(1)}, u32[]{:S(2)}, u32[]{:S(2)}) collective-permute-start(bf16[704,128]{1,0:T(8,128)(2,1)S(1)} %collective-permute-done.13.refs_8_), channel_id=1, source_target_pairs={{0,16},{16,0},{32,48},{48,32},{64,80},{80,64},{96,112},{112,96},{1... | collective-permute-start | bytes 540680 | tf_op jit(solution)/shard_map/ppermute | solution.py:38
  25.5 15.8 %copy-start.10 = (bf16[704,128]{1,0:T(8,128)(2,1)}, bf16[704,128]{1,0:T(8,128)(2,1)S(1)}, u32[]{:S(2)}) copy-start(bf16[704,128]{1,0:T(8,128)(2,1)S(1)} %collective-permute-done.10.refs_5_) | copy-start | bytes 540676
  25.6 10.4 %collective-permute-start.12 = (bf16[704,128]{1,0:T(8,128)(2,1)S(1)}, bf16[704,128]{1,0:T(8,128)(2,1)S(1)}, u32[]{:S(2)}, u32[]{:S(2)}) collective-permute-start(bf16[704,128]{1,0:T(8,128)(2,1)S(1)} %collective-permute-done.11.refs_6_), channel_id=1, source_target_pairs={{0,16},{16,0},{32,48},{48,32},{64,80},{80,64},{96,112},{112,96},{1... | collective-permute-start | bytes 540680 | tf_op jit(solution)/shard_map/ppermute | solution.py:38
  30.8 10.6 %copy-start.11 = (bf16[704,128]{1,0:T(8,128)(2,1)}, bf16[704,128]{1,0:T(8,128)(2,1)S(1)}, u32[]{:S(2)}) copy-start(bf16[704,128]{1,0:T(8,128)(2,1)S(1)} %collective-permute-done.15.refs_10_) | copy-start | bytes 540676
  30.8 5.2 %collective-permute-start.16 = (bf16[704,128]{1,0:T(8,128)(2,1)S(1)}, bf16[704,128]{1,0:T(8,128)(2,1)S(1)}, u32[]{:S(2)}, u32[]{:S(2)}) collective-permute-start(bf16[704,128]{1,0:T(8,128)(2,1)S(1)} %collective-permute-done.15.refs_10_), channel_id=1, source_target_pairs={{0,16},{16,0},{32,48},{48,32},{64,80},{80,64},{96,112},{112,96},{1... | collective-permute-start | bytes 540680 | tf_op jit(solution)/shard_map/ppermute | solution.py:38
  35.4 6.0 %copy-start.12 = (bf16[704,128]{1,0:T(8,128)(2,1)}, bf16[704,128]{1,0:T(8,128)(2,1)S(1)}, u32[]{:S(2)}) copy-start(bf16[704,128]{1,0:T(8,128)(2,1)S(1)} %collective-permute-done.17.refs_12_) | copy-start | bytes 540676
  35.4 1.4 %collective-permute-start.18 = (bf16[704,128]{1,0:T(8,128)(2,1)S(1)}, bf16[704,128]{1,0:T(8,128)(2,1)S(1)}, u32[]{:S(2)}, u32[]{:S(2)}) collective-permute-start(bf16[704,128]{1,0:T(8,128)(2,1)S(1)} %collective-permute-done.17.refs_12_), channel_id=1, source_target_pairs={{0,16},{16,0},{32,48},{48,32},{64,80},{80,64},{96,112},{112,96},{1... | collective-permute-start | bytes 540680 | tf_op jit(solution)/shard_map/ppermute | solution.py:38
  35.4 6.0 %copy-start.13 = (bf16[704,128]{1,0:T(8,128)(2,1)}, bf16[704,128]{1,0:T(8,128)(2,1)S(1)}, u32[]{:S(2)}) copy-start(bf16[704,128]{1,0:T(8,128)(2,1)S(1)} %collective-permute-done.19.refs_14_) | copy-start | bytes 540676
  35.4 1.7 %collective-permute-start.20 = (bf16[704,128]{1,0:T(8,128)(2,1)S(1)}, bf16[704,128]{1,0:T(8,128)(2,1)S(1)}, u32[]{:S(2)}, u32[]{:S(2)}) collective-permute-start(bf16[704,128]{1,0:T(8,128)(2,1)S(1)} %collective-permute-done.19.refs_14_), channel_id=1, source_target_pairs={{0,16},{16,0},{32,48},{48,32},{64,80},{80,64},{96,112},{112,96},{1... | collective-permute-start | bytes 540680 | tf_op jit(solution)/shard_map/ppermute | solution.py:38
  35.9 23.9 %copy-start.21 = (f32[256,4]{0,1:T(4,128)S(1)}, f32[256,4]{0,1:T(4,128)}, u32[]{:S(2)}) copy-start(f32[256,4]{0,1:T(4,128)} %param.12) | copy-start | bytes 12292
  35.9 24.9 %copy-start = (bf16[256,4,128]{2,1,0:T(4,128)(2,1)S(1)}, bf16[256,4,128]{2,1,0:T(4,128)(2,1)}, u32[]{:S(2)}) copy-start(bf16[256,4,128]{2,1,0:T(4,128)(2,1)} %param.10) | copy-start | bytes 786436
  35.9 48.9 %copy-start.2 = (s32[2,16]{1,0:T(2,128)S(1)}, s32[2,16]{1,0:T(2,128)}, u32[]{:S(2)}) copy-start(s32[2,16]{1,0:T(2,128)} %kept_ref.3) | copy-start | bytes 388
  36.0 5.5 %copy-start.15 = (bf16[704,128]{1,0:T(8,128)(2,1)}, bf16[704,128]{1,0:T(8,128)(2,1)S(1)}, u32[]{:S(2)}) copy-start(bf16[704,128]{1,0:T(8,128)(2,1)S(1)} %collective-permute-done.12.refs_7_) | copy-start | bytes 540676
  36.0 5.5 %copy-start.14 = (bf16[704,128]{1,0:T(8,128)(2,1)}, bf16[704,128]{1,0:T(8,128)(2,1)S(1)}, u32[]{:S(2)}) copy-start(bf16[704,128]{1,0:T(8,128)(2,1)S(1)} %collective-permute-done.14.refs_9_) | copy-start | bytes 540676
  36.0 1.1 copy-start.16
  36.8 0.7 copy-start.17
  37.5 0.7 copy-start.18
  52.3 35.6 %all-to-all-start.1 = ((bf16[4,16,2048]{2,1,0:T(8,128)(2,1)}), bf16[4,16,2048]{2,1,0:T(8,128)(2,1)S(1)}, u32[]{:S(2)}, u32[]{:S(2)}) async-start(bf16[4,16,2048]{2,1,0:T(8,128)(2,1)} %bitcast.9), calls=%async_computation.1 | async-start | bytes 524288 | tf_op jit(solution)/shard_map/all_to_all | solution.py:50
  61.4 6.6 %collective-permute-start = (bf16[4,80,128]{2,1,0:T(8,128)(2,1)S(1)}, bf16[4,80,128]{2,1,0:T(8,128)(2,1)S(1)}, u32[]{:S(2)}, u32[]{:S(2)}) collective-permute-start(bf16[4,80,128]{2,1,0:T(8,128)(2,1)S(1)} %get-tuple-element.18), channel_id=1, source_target_pairs={{0,1},{1,2},{2,3},{3,0},{4,5},{5,6},{6,7},{7,4},{8,9},{9,10},{10,1... | collective-permute-start | bytes 245768 | tf_op jit(solution)/shard_map/ppermute | solution.py:42
  62.1 6.0 %collective-permute-start.1 = (bf16[4,80,128]{2,1,0:T(8,128)(2,1)S(1)}, bf16[4,80,128]{2,1,0:T(8,128)(2,1)S(1)}, u32[]{:S(2)}, u32[]{:S(2)}) collective-permute-start(bf16[4,80,128]{2,1,0:T(8,128)(2,1)S(1)} %get-tuple-element.19), channel_id=1, source_target_pairs={{0,3},{1,0},{2,1},{3,2},{4,7},{5,4},{6,5},{7,6},{8,11},{9,8},{10,9... | collective-permute-start | bytes 245768 | tf_op jit(solution)/shard_map/ppermute | solution.py:42
  64.7 5.9 %collective-permute-start.2 = (bf16[4,80,128]{2,1,0:T(8,128)(2,1)S(1)}, bf16[4,80,128]{2,1,0:T(8,128)(2,1)S(1)}, u32[]{:S(2)}, u32[]{:S(2)}) collective-permute-start(bf16[4,80,128]{2,1,0:T(8,128)(2,1)S(1)} %get-tuple-element.20), channel_id=1, source_target_pairs={{0,2},{1,3},{2,0},{3,1},{4,6},{5,7},{6,4},{7,5},{8,10},{9,11},{10,... | collective-permute-start | bytes 245768 | tf_op jit(solution)/shard_map/ppermute | solution.py:42
  71.3 10.1 %collective-permute-start.3 = (bf16[4,80,128]{2,1,0:T(8,128)(2,1)S(1)}, bf16[4,80,128]{2,1,0:T(8,128)(2,1)S(1)}, u32[]{:S(2)}, u32[]{:S(2)}) collective-permute-start(bf16[4,80,128]{2,1,0:T(8,128)(2,1)S(1)} %get-tuple-element.22), channel_id=1, source_target_pairs={{0,4},{1,5},{2,6},{3,7},{4,8},{5,9},{6,10},{7,11},{8,12},{9,13},{1... | collective-permute-start | bytes 245768 | tf_op jit(solution)/shard_map/ppermute | solution.py:46
  74.3 7.2 %collective-permute-start.4 = (bf16[4,80,128]{2,1,0:T(8,128)(2,1)S(1)}, bf16[4,80,128]{2,1,0:T(8,128)(2,1)S(1)}, u32[]{:S(2)}, u32[]{:S(2)}) collective-permute-start(bf16[4,80,128]{2,1,0:T(8,128)(2,1)S(1)} %get-tuple-element.23), channel_id=1, source_target_pairs={{0,12},{1,13},{2,14},{3,15},{4,0},{5,1},{6,2},{7,3},{8,4},{9,5},{1... | collective-permute-start | bytes 245768 | tf_op jit(solution)/shard_map/ppermute | solution.py:46
  75.6 9.2 %collective-permute-start.5 = (bf16[4,80,128]{2,1,0:T(8,128)(2,1)S(1)}, bf16[4,80,128]{2,1,0:T(8,128)(2,1)S(1)}, u32[]{:S(2)}, u32[]{:S(2)}) collective-permute-start(bf16[4,80,128]{2,1,0:T(8,128)(2,1)S(1)} %get-tuple-element.24), channel_id=1, source_target_pairs={{0,8},{1,9},{2,10},{3,11},{4,12},{5,13},{6,14},{7,15},{8,0},{9,1},... | collective-permute-start | bytes 245768 | tf_op jit(solution)/shard_map/ppermute | solution.py:46
  92.6 1.6 %collective-permute-start.21 = (bf16[8,128,128]{2,1,0:T(8,128)(2,1)S(1)}, bf16[8,128,128]{2,1,0:T(8,128)(2,1)S(1)}, u32[]{:S(2)}, u32[]{:S(2)}) collective-permute-start(bf16[8,128,128]{2,1,0:T(8,128)(2,1)S(1)} %get-tuple-element.31), channel_id=1, source_target_pairs={{0,16},{16,0},{32,48},{48,32},{64,80},{80,64},{96,112},{112,96},{1... | collective-permute-start | bytes 786440 | tf_op jit(solution)/shard_map/ppermute | solution.py:38

commit v3 on v2

--- a/solution.py
+++ b/solution.py
@@ -65,14 +65,16 @@
     )
 
 
-def query_body(q_ref, lse_ref, out_ref, wide, turned, in_sem, out_sem):
+def query_body(q_ref, lse_hbm, out_ref, wide, turned, lse_ref, in_sem, out_sem):
     heads, width, rows = q_ref.shape
     loads = [
         pltpu.make_async_copy(q_ref.at[h], wide.at[h, 0:width, :], in_sem.at[h]) for h in range(heads)
     ]
-    for load in loads:
+    lse_load = pltpu.make_async_copy(lse_hbm, lse_ref, in_sem.at[heads])
+    for load in [lse_load] + loads:
         load.start()
     row = lax.broadcasted_iota(jnp.int32, (640 - width, rows), 0)
+    lse_load.wait()
     stores = []
     for h in range(heads):
         value = lse_ref[h : h + 1, :] * (-1.0 / attn_scale)
@@ -98,52 +100,50 @@
     return call(
         query_body,
         pltpu.HBM((4, heads, rows // 4, 640), bf16),
-        [HB, VM],
+        [HB, HB],
         12,
         out_specs=HB,
         scratch_shapes=[
             pltpu.VMEM((heads, 640, rows), bf16),
             pltpu.VMEM((heads, 4, rows // 4, 640), bf16),
-            pltpu.SemaphoreType.DMA((heads,)),
+            pltpu.VMEM((heads, rows), f32),
+            pltpu.SemaphoreType.DMA((heads + 1,)),
             pltpu.SemaphoreType.DMA((heads,)),
         ],
         name="wide_queries",
-    )(pltpu.with_memory_space_constraint(query, pltpu.HBM), normalizer)
+    )(*[pltpu.with_memory_space_constraint(v, pltpu.HBM) for v in (query, normalizer)])
 
 
 def score_body(q_hbm, *refs):
-    tiles, (out_ref, index_ref, q_ref, keys, q_sem, k_sem, i_sem) = refs[:16], refs[16:]
+    tiles, (out_ref, index_ref, q_ref, keys, acc, q_sem) = refs[:16], refs[16:]
     groups, heads, rows, depth = q_ref.shape
     width = tiles[0].shape[0] - 128
-    key_loads, index_loads = [], []
-    for i, tile in enumerate(tiles):
-        place = keys.at[i // 4, 0:width, i % 4 * 128 : i % 4 * 128 + 128]
-        key_loads.append(pltpu.make_async_copy(tile.at[128 : 128 + width, :], place, k_sem.at[i]))
-        place = index_ref.at[i * 128 : i * 128 + 128, :]
-        index_loads.append(pltpu.make_async_copy(tile.at[0:128, :], place, i_sem.at[i]))
     q_loads = [
         pltpu.make_async_copy(q_hbm.at[a], q_ref.at[a], q_sem.at[a]) for a in range(groups)
     ]
-    for load in q_loads[:1] + key_loads[:4] + q_loads[1:] + key_loads[4:] + index_loads:
+    for load in q_loads:
         load.start()
     row = lax.broadcasted_iota(jnp.int32, (depth - width, 512), 0)
     for n in range(4):
         keys[n, width:, :] = jnp.where(row < 3, 1.0, 0.0).astype(bf16)
-        for load in key_loads[4 * n : 4 * n + 4]:
-            load.wait()
-        total = None
-        for a in range(groups):
-            if n == 0:
-                q_loads[a].wait()
-            some = q_ref[a].reshape(heads * rows, depth)
+    for i, tile in enumerate(tiles):
+        keys[i // 4, 0:width, i % 4 * 128 : i % 4 * 128 + 128] = tile[128 : 128 + width, :]
+        index_ref[i * 128 : i * 128 + 128, :] = tile[0:128, :]
+    for a in range(groups):
+        q_loads[a].wait()
+        some = q_ref[a].reshape(heads * rows, depth)
+        for n in range(4):
+            at = n * 512
             s = jnp.dot(some, keys[n], preferred_element_type=f32)
             p = jnp.exp2(s * (attn_scale * LOG2E))
+            total = acc[:, at : at + 512] if a else None
             for h in range(heads):
                 part = p[h * rows : h * rows + rows]
                 total = part if total is None else total + part
-        out_ref[:, n * 512 : n * 512 + 512] = total.astype(bf16)
-    for load in index_loads:
-        load.wait()
+            if a + 1 < groups:
+                acc[:, at : at + 512] = total
+            else:
+                out_ref[:, at : at + 512] = total.astype(bf16)
 
 
 def scores(query, tiles):
@@ -151,32 +151,31 @@
     return call(
         score_body,
         (sds((rows, 2048), bf16), sds((2048, 128), bf16)),
-        [HB] * 17,
+        [HB] + [VM] * 16,
         16,
         scratch_shapes=[
             pltpu.VMEM(query.shape, bf16),
             pltpu.VMEM((4, depth, 512), bf16),
+            pltpu.VMEM((rows, 2048), f32),
             pltpu.SemaphoreType.DMA((groups,)),
-            pltpu.SemaphoreType.DMA((16,)),
-            pltpu.SemaphoreType.DMA((16,)),
         ],
         name="scores",
-    )(*[pltpu.with_memory_space_constraint(v, pltpu.HBM) for v in (query, *tiles)])
+    )(pltpu.with_memory_space_constraint(query, pltpu.HBM), *tiles)
 
 
 def pack_body(at_ref, q_ref, w_ref, *outs):
     for d, ref in zip((0,) + STEPS, outs):
-        x = lax.rem(at_ref[1] + d, 4)
-        for zh in range(4):
-            ref[zh, 0:64, :] = q_ref[zh * 4 + x]
-            ref[zh, 64:80, :] = w_ref[zh * 4 + x]
+        zh = lax.rem(at_ref[0] + d, 4)
+        for x in range(4):
+            ref[x, 0:64, :] = q_ref[zh * 4 + x]
+            ref[x, 64:80, :] = w_ref[zh * 4 + x]
 
 
 def spread_body(at_ref, *refs):
     for d, ref in zip((0,) + STEPS, refs[4:]):
-        zh = lax.rem(at_ref[0] + d, 4)
-        for a in range(4):
-            ref[a] = refs[a][zh]
+        x = lax.rem(at_ref[1] + d, 4)
+        for e in range(4):
+            ref[e] = refs[e][x]
 
 
 def weight_column(q_ref, j):
@@ -266,10 +265,10 @@
             dz[at : at + 64, :] = jnp.where(z[at : at + 64] > 0.0, value, 0.0).astype(bf16)
         dk[...] += lax.dot_general(rows, dz[...], TN, preferred_element_type=f32)
         dq = jnp.dot(dz[...], keys[...], preferred_element_type=f32) * scale
-        e = jnp.where(g < 2, g, 5 - g)
-        zh = lax.rem(at_ref[0] + 4 - e, 4)
-        for a, d in enumerate((0,) + STEPS):
-            x = lax.rem(at_ref[1] + 4 - d, 4)
+        d = jnp.where(g < 2, g, 5 - g)
+        x = lax.rem(at_ref[1] + 4 - d, 4)
+        for a, e in enumerate((0,) + STEPS):
+            zh = lax.rem(at_ref[0] + 4 - e, 4)
             dq_ref[zh * 4 + x] = dq[a * 64 : a * 64 + 64].astype(bf16)
 
     for slot in range(16):
@@ -322,11 +321,11 @@
     )
     got = [parts[0]]
     for part, d in zip(parts[1:], STEPS):
-        got.append(along_x(part, d))
+        got.append(along_zh(part, d))
     parts = call(spread_body, four, [SM] + [VM] * 4, 6, name="spread")(at, *got)
     queries = [parts[0]]
     for part, d in zip(parts[1:], STEPS):
-        queries.append(along_zh(part, d))
+        queries.append(along_x(part, d))
 
     query = wide_queries(jnp.transpose(query_latent, (1, 2, 0)), normalizer.T)
     query = exchanged(query, "head", ROW_X)

time: 132 us -> 132 us (level)
  waiting for transfers between devices: 33.3 us -> 36.1 us
  blocking collectives: 34.1 us -> 31.4 us
  Pallas kernels: 22.7 us -> 20.9 us
  local copies, waits for them, and re-layouts: 4.24 us -> 5.62 us
    ppermute x3, waiting for transfers between devices: 3.39 us -> 6.35 us  [along_zh(): lax.ppermute(value, 'head', [(i, (i + 4 * d) % 16) for i in range(16)])]
    all_to_all x2, blocking collectives: 34.1 us -> 31.4 us  [exchanged(): lax.all_to_all(value, axis, 0, 0, tiled=True, axis_index_groups=groups)]
    pallas_call x1, Pallas kernels: 10.8 us -> 9.06 us  [scores(): call(score_body, (sds((rows, 2048), bf16), sds((2048, 128), bf16)), [HB]...]
    unnamed x45 -> x19, local copies, waits for them, and re-layouts: 2.57 us -> 3.95 us
  transfers between devices with their start and end apart: 24 -> 24, of which waited for: 11 -> 12; matrix products, arithmetic and copies ran while one was open for 1% -> 1% of each run, Pallas kernels for 3% -> 3%
where the time goes in v3:
time: 132 us; the launch traced here: 129 us
  waiting for transfers between devices  36.1 us (27%)
  starting transfers between devices  34.3 us (26%)
  blocking collectives  31.4 us (24%)
  Pallas kernels  20.9 us (16%)
  local copies, waits for them, and re-layouts  5.62 us (4%)
    all_to_all x2, blocking collectives, exchanged(): lax.all_to_all(value, axis, 0, 0, tiled=True, axis_index_groups=groups)  31.4 us
    ppermute x6, waiting for transfers between devices, along_y(): lax.ppermute(value, 'seq', [(i, (i + 4 * d) % 16) for i in range(16)])  18.2 us
    all_to_all x2, starting transfers between devices, exchanged(): lax.all_to_all(value, axis, 0, 0, tiled=True, axis_index_groups=groups)  12.3 us
    ppermute x3, starting transfers between devices, along_zh(): lax.ppermute(value, 'head', [(i, (i + 4 * d) % 16) for i in range(16)])  10.1 us
    pallas_call x1, Pallas kernels, scores(): call(score_body, (sds((rows, 2048), bf16), sds((2048, 128), bf16)), [HB]...  9.06 us
    ppermute x6, starting transfers between devices, along_y(): lax.ppermute(value, 'seq', [(i, (i + 4 * d) % 16) for i in range(16)])  6.6 us
    ppermute x3, waiting for transfers between devices, along_zh(): lax.ppermute(value, 'head', [(i, (i + 4 * d) % 16) for i in range(16)])  6.35 us
    ppermute x3, waiting for transfers between devices, along_x(): lax.ppermute(value, 'head', [(i, i // 4 * 4 + (i + d) % 4) for i in range...  5.94 us
  transfers between devices with their start and end apart: 24, of which 12 were waited for; matrix products, arithmetic and copies ran while one was open for 1% of the time, Pallas kernels for 3%

profile of v3, /device:TPU:32, one launch (start us, length us, event | category | flops | bytes accessed | tf_op | source)
XLA Modules:
  0.0 129.5 jit_solution(2170512949534901695)
XLA Ops:
  0.6 3.0 %wide_queries.1 = bf16[4,8,64,640]{3,2,1,0:T(8,128)(2,1)} custom-call(bf16[8,576,256]{2,1,0:T(8,128)(2,1)} %bitcast.18, f32[8,256]{1,0:T(8,128)} %bitcast.24), custom_call_target="tpu_custom_call" | custom-call | tf_op jit(solution)/shard_map/wide_queries/pallas_call | solution.py:100
  3.7 0.0 copy-start.6
  3.7 0.0 copy-start.7
  3.7 4.7 %all-to-all-start = ((bf16[4,8,64,640]{3,2,1,0:T(8,128)(2,1)}), bf16[4,8,64,640]{3,2,1,0:T(8,128)(2,1)}, u32[]{:S(2)}, u32[]{:S(2)}) async-start(bf16[4,8,64,640]{3,2,1,0:T(8,128)(2,1)} %wide_queries.1), calls=%async_computation | async-start | bytes 5242880 | tf_op jit(solution)/shard_map/all_to_all | solution.py:50
  8.4 3.1 %collective-permute-start.7 = (bf16[704,128]{1,0:T(8,128)(2,1)S(1)}, bf16[704,128]{1,0:T(8,128)(2,1)S(1)}, u32[]{:S(2)}, u32[]{:S(2)}) collective-permute-start(bf16[704,128]{1,0:T(8,128)(2,1)S(1)} %pad_maximum_fusion.1.refs_0_), channel_id=1, source_target_pairs={{0,192},{16,208},{32,224},{48,240},{64,0},{80,16},{96,32},{112,48}... | collective-permute-start | bytes 540680 | tf_op jit(solution)/shard_map/ppermute | solution.py:30
  11.5 0.8 collective-permute-start.13
  12.3 0.0 collective-permute-start.6
  12.4 1.5 %collective-permute-start.11 = (bf16[704,128]{1,0:T(8,128)(2,1)S(1)}, bf16[704,128]{1,0:T(8,128)(2,1)S(1)}, u32[]{:S(2)}, u32[]{:S(2)}) collective-permute-start(bf16[704,128]{1,0:T(8,128)(2,1)S(1)} %pad_maximum_fusion.1.refs_0_), channel_id=1, source_target_pairs={{0,128},{16,144},{32,160},{48,176},{64,192},{80,208},{96,224},{112... | collective-permute-start | bytes 540680 | tf_op jit(solution)/shard_map/ppermute | solution.py:30
  13.8 1.5 %collective-permute-done.7.refs_2_ = bf16[704,128]{1,0:T(8,128)(2,1)S(1)} collective-permute-done((bf16[704,128]{1,0:T(8,128)(2,1)S(1)}, bf16[704,128]{1,0:T(8,128)(2,1)S(1)}, u32[]{:S(2)}, u32[]{:S(2)}) %collective-permute-start.7) | collective-permute-done | bytes 180256 | tf_op jit(solution)/shard_map/ppermute | solution.py:30
  15.3 7.3 %collective-permute-done.9.refs_4_ = bf16[704,128]{1,0:T(8,128)(2,1)S(1)} collective-permute-done((bf16[704,128]{1,0:T(8,128)(2,1)S(1)}, bf16[704,128]{1,0:T(8,128)(2,1)S(1)}, u32[]{:S(2)}, u32[]{:S(2)}) %collective-permute-start.9) | collective-permute-done | bytes 180256 | tf_op jit(solution)/shard_map/ppermute | solution.py:30
  22.6 0.0 collective-permute-start.10
  22.6 0.0 collective-permute-done.13.refs_8_
  22.6 2.0 %collective-permute-start.17 = (bf16[704,128]{1,0:T(8,128)(2,1)S(1)}, bf16[704,128]{1,0:T(8,128)(2,1)S(1)}, u32[]{:S(2)}, u32[]{:S(2)}) collective-permute-start(bf16[704,128]{1,0:T(8,128)(2,1)S(1)} %collective-permute-done.13.refs_8_), channel_id=1, source_target_pairs={{0,64},{16,80},{32,96},{48,112},{64,128},{80,144},{96,160},{112,17... | collective-permute-start | bytes 540680 | tf_op jit(solution)/shard_map/ppermute | solution.py:30
  24.6 0.0 collective-permute-done.11.refs_6_
  24.6 0.0 collective-permute-start.19
  24.6 0.0 collective-permute-done.8.refs_3_
  24.7 0.1 collective-permute-start.14
  24.8 0.5 collective-permute-start.12
  25.3 4.8 %collective-permute-done.15.refs_10_ = bf16[704,128]{1,0:T(8,128)(2,1)S(1)} collective-permute-done((bf16[704,128]{1,0:T(8,128)(2,1)S(1)}, bf16[704,128]{1,0:T(8,128)(2,1)S(1)}, u32[]{:S(2)}, u32[]{:S(2)}) %collective-permute-start.15) | collective-permute-done | bytes 180256 | tf_op jit(solution)/shard_map/ppermute | solution.py:30
  30.0 4.7 %collective-permute-done.17.refs_12_ = bf16[704,128]{1,0:T(8,128)(2,1)S(1)} collective-permute-done((bf16[704,128]{1,0:T(8,128)(2,1)S(1)}, bf16[704,128]{1,0:T(8,128)(2,1)S(1)}, u32[]{:S(2)}, u32[]{:S(2)}) %collective-permute-start.17) | collective-permute-done | bytes 180256 | tf_op jit(solution)/shard_map/ppermute | solution.py:30
  34.7 0.0 collective-permute-start.18
  34.7 0.0 collective-permute-done.19.refs_14_
  34.7 0.5 collective-permute-start.20
  35.3 0.0 collective-permute-done.12.refs_7_
  35.3 0.0 collective-permute-done.16.refs_11_
  35.3 0.9 collective-permute-done.18.refs_13_
  36.2 0.7 copy-done.1
  36.8 0.0 collective-permute-done.20.refs_15_
  36.8 0.7 copy-done.3
  37.5 3.2 %all-to-all-done.q_hbm = bf16[4,8,64,640]{3,2,1,0:T(8,128)(2,1)} async-done(((bf16[4,8,64,640]{3,2,1,0:T(8,128)(2,1)}), bf16[4,8,64,640]{3,2,1,0:T(8,128)(2,1)}, u32[]{:S(2)}, u32[]{:S(2)}) %all-to-all-start) | async-done | bytes 2621472 | tf_op jit(solution)/shard_map/all_to_all | solution.py:50
  40.7 0.9 copy-done.2
  41.6 0.9 copy-done.4
  42.5 9.1 %scores.1 = (bf16[64,2048]{1,0:T(8,128)(2,1)}, bf16[2048,128]{1,0:T(8,128)(2,1)S(1)}) custom-call(bf16[4,8,64,640]{3,2,1,0:T(8,128)(2,1)} %all-to-all-done.q_hbm, bf16[704,128]{1,0:T(8,128)(2,1)S(1)} %pad_maximum_fusion.1.refs_0_, bf16[704,128]{1,0:T(8,128)(2,1)S(1)} %collective-permute-done.6.refs_1_, bf16[704,128]{1,0:T(8,128)(2,1)S(1)} %collective-permute-done.7.refs_2_, ...), custom_call_target="tpu_custom_call" | custom-call | tf_op jit(solution)/shard_map/scores/pallas_call | solution.py:151
  51.6 7.6 %all-to-all-start.1 = ((bf16[4,16,2048]{2,1,0:T(8,128)(2,1)}), bf16[4,16,2048]{2,1,0:T(8,128)(2,1)S(1)}, u32[]{:S(2)}, u32[]{:S(2)}) async-start(bf16[4,16,2048]{2,1,0:T(8,128)(2,1)} %bitcast.9), calls=%async_computation.1 | async-start | bytes 524288 | tf_op jit(solution)/shard_map/all_to_all | solution.py:50
  59.2 0.1 copy.14
  59.3 0.1 stack_reshape.17
  59.4 0.1 copy.13
  59.6 0.1 stack_reshape.16
  59.7 0.1 copy.12
  59.9 0.1 stack_reshape.15
  60.0 0.1 stack.27.at_ref
  60.1 0.1 fusion.8.w_ref
  60.2 0.6 pack.1
  60.8 3.0 %collective-permute-start = (bf16[4,80,128]{2,1,0:T(8,128)(2,1)S(1)}, bf16[4,80,128]{2,1,0:T(8,128)(2,1)S(1)}, u32[]{:S(2)}, u32[]{:S(2)}) collective-permute-start(bf16[4,80,128]{2,1,0:T(8,128)(2,1)S(1)} %get-tuple-element.18), channel_id=1, source_target_pairs={{0,4},{1,5},{2,6},{3,7},{4,8},{5,9},{6,10},{7,11},{8,12},{9,13},{1... | collective-permute-start | bytes 245768 | tf_op jit(solution)/shard_map/ppermute | solution.py:46
  63.8 1.3 %collective-permute-start.1 = (bf16[4,80,128]{2,1,0:T(8,128)(2,1)S(1)}, bf16[4,80,128]{2,1,0:T(8,128)(2,1)S(1)}, u32[]{:S(2)}, u32[]{:S(2)}) collective-permute-start(bf16[4,80,128]{2,1,0:T(8,128)(2,1)S(1)} %get-tuple-element.19), channel_id=1, source_target_pairs={{0,12},{1,13},{2,14},{3,15},{4,0},{5,1},{6,2},{7,3},{8,4},{9,5},{1... | collective-permute-start | bytes 245768 | tf_op jit(solution)/shard_map/ppermute | solution.py:46
  65.1 5.8 %collective-permute-start.2 = (bf16[4,80,128]{2,1,0:T(8,128)(2,1)S(1)}, bf16[4,80,128]{2,1,0:T(8,128)(2,1)S(1)}, u32[]{:S(2)}, u32[]{:S(2)}) collective-permute-start(bf16[4,80,128]{2,1,0:T(8,128)(2,1)S(1)} %get-tuple-element.20), channel_id=1, source_target_pairs={{0,8},{1,9},{2,10},{3,11},{4,12},{5,13},{6,14},{7,15},{8,0},{9,1},... | collective-permute-start | bytes 245768 | tf_op jit(solution)/shard_map/ppermute | solution.py:46
  70.9 1.8 %collective-permute-done.refs_1_ = bf16[4,80,128]{2,1,0:T(8,128)(2,1)S(1)} collective-permute-done((bf16[4,80,128]{2,1,0:T(8,128)(2,1)S(1)}, bf16[4,80,128]{2,1,0:T(8,128)(2,1)S(1)}, u32[]{:S(2)}, u32[]{:S(2)}) %collective-permute-start) | collective-permute-done | bytes 81952 | tf_op jit(solution)/shard_map/ppermute | solution.py:46
  72.7 4.5 %collective-permute-done.2.refs_3_ = bf16[4,80,128]{2,1,0:T(8,128)(2,1)S(1)} collective-permute-done((bf16[4,80,128]{2,1,0:T(8,128)(2,1)S(1)}, bf16[4,80,128]{2,1,0:T(8,128)(2,1)S(1)}, u32[]{:S(2)}, u32[]{:S(2)}) %collective-permute-start.2) | collective-permute-done | bytes 81952 | tf_op jit(solution)/shard_map/ppermute | solution.py:46
  77.3 0.6 spread.1
  77.8 0.6 collective-permute-start.3
  78.5 2.7 %collective-permute-start.4 = (bf16[4,80,128]{2,1,0:T(8,128)(2,1)S(1)}, bf16[4,80,128]{2,1,0:T(8,128)(2,1)S(1)}, u32[]{:S(2)}, u32[]{:S(2)}) collective-permute-start(bf16[4,80,128]{2,1,0:T(8,128)(2,1)S(1)} %get-tuple-element.23), channel_id=1, source_target_pairs={{0,3},{1,0},{2,1},{3,2},{4,7},{5,4},{6,5},{7,6},{8,11},{9,8},{10,9... | collective-permute-start | bytes 245768 | tf_op jit(solution)/shard_map/ppermute | solution.py:42
  81.1 2.4 %collective-permute-done.3.refs_1_ = bf16[4,80,128]{2,1,0:T(8,128)(2,1)S(1)} collective-permute-done((bf16[4,80,128]{2,1,0:T(8,128)(2,1)S(1)}, bf16[4,80,128]{2,1,0:T(8,128)(2,1)S(1)}, u32[]{:S(2)}, u32[]{:S(2)}) %collective-permute-start.3) | collective-permute-done | bytes 81952 | tf_op jit(solution)/shard_map/ppermute | solution.py:42
  83.6 0.5 collective-permute-done.4.refs_2_
  84.0 3.1 %collective-permute-done.5.refs_3_ = bf16[4,80,128]{2,1,0:T(8,128)(2,1)S(1)} collective-permute-done((bf16[4,80,128]{2,1,0:T(8,128)(2,1)S(1)}, bf16[4,80,128]{2,1,0:T(8,128)(2,1)S(1)}, u32[]{:S(2)}, u32[]{:S(2)}) %collective-permute-start.5) | collective-permute-done | bytes 81952 | tf_op jit(solution)/shard_map/ppermute | solution.py:42
  87.1 3.0 %index_forward.1 = (f32[16,2048]{1,0:T(8,128)S(1)}, bf16[16,80,128]{2,1,0:T(8,128)(2,1)S(1)}) custom-call(s32[5]{0:T(128)S(1)} %stack.27.at_ref, s32[2,16]{1,0:T(2,128)S(1)} %copy-done.5, bf16[4,80,128]{2,1,0:T(8,128)(2,1)S(1)} %get-tuple-element.21.refs_0_, bf16[4,80,128]{2,1,0:T(8,128)(2,1)S(1)} %collective-permute-done.3.refs_1_, ...), custom_call_target="tpu_custom_call" | custom-call | tf_op jit(solution)/shard_map/index_forward/pallas_call | solution.py:237
  90.1 4.6 %index_backward.1 = (f32[8,128,128]{2,1,0:T(8,128)S(1)}, bf16[8,128,128]{2,1,0:T(8,128)(2,1)S(1)}, bf16[16,64,128]{2,1,0:T(8,128)(2,1)S(1)}) custom-call(s32[5]{0:T(128)S(1)} %stack.27.at_ref, s32[2,16]{1,0:T(2,128)S(1)} %copy-done.5, f32[16,2048]{1,0:T(8,128)S(1)} %get-tuple-element.26.prob_ref, bf16[16,80,128]{2,1,0:T(8,128)(2,1)S(1)} %get-tuple-element.27.q_ref, ...), custom_call_target="tpu_custom_call" | custom-call | tf_op jit(solution)/shard_map/index_backward/pallas_call | solution.py:284
  94.7 0.1 collective-permute-start.21
  94.8 1.5 %collective-permute-done.21 = bf16[8,128,128]{2,1,0:T(8,128)(2,1)S(1)} collective-permute-done((bf16[8,128,128]{2,1,0:T(8,128)(2,1)S(1)}, bf16[8,128,128]{2,1,0:T(8,128)(2,1)S(1)}, u32[]{:S(2)}, u32[]{:S(2)}) %collective-permute-start.21) | collective-permute-done | bytes 262176 | tf_op jit(solution)/shard_map/ppermute | solution.py:38
  96.4 0.1 add_convert_fusion
  96.4 14.3 %all_to_all.20 = bf16[32,32,128]{2,1,0:T(8,128)(2,1)S(1)} all-to-all(bf16[32,32,128]{2,1,0:T(8,128)(2,1)S(1)} %bitcast.19), channel_id=1, replica_groups={{0,1,2,3,32,33,34,35,64,65,66,67,96,97,98,99,128,129,130,131,160,161,16..., dimensions={0} | all-to-all | bytes 524288 | tf_op jit(solution)/shard_map/all_to_all | solution.py:50
  110.7 0.1 reduce_sum.21
  110.8 17.1 %all_to_all.21 = bf16[16,96,128]{2,1,0:T(8,128)(2,1)S(1)} all-to-all(bf16[16,96,128]{2,1,0:T(8,128)(2,1)S(1)} %pad_maximum_fusion), channel_id=1, replica_groups=mesh['seq'=16,'head'=16] {'head'}, dimensions={0} | all-to-all | bytes 786432 | tf_op jit(solution)/shard_map/all_to_all | solution.py:50
  128.0 0.7 copy.18
  128.7 0.7 slice.8
  (28 shorter events, 0.1 us)
Async XLA Ops:
  3.7 4.7 %copy-start.6 = (bf16[128,576]{0,1:T(8,128)(2,1)S(1)}, bf16[128,576]{0,1:T(8,128)(2,1)}, u32[]{:S(2)}) copy-start(bf16[128,576]{0,1:T(8,128)(2,1)} %param.8) | copy-start | bytes 442372
  3.7 4.7 %copy-start.7 = (bf16[128,128]{1,0:T(8,128)(2,1)S(1)}, bf16[128,128]{1,0:T(8,128)(2,1)}, u32[]{:S(2)}) copy-start(bf16[128,128]{1,0:T(8,128)(2,1)} %param.11) | copy-start | bytes 98308
  3.7 37.0 %all-to-all-start = ((bf16[4,8,64,640]{3,2,1,0:T(8,128)(2,1)}), bf16[4,8,64,640]{3,2,1,0:T(8,128)(2,1)}, u32[]{:S(2)}, u32[]{:S(2)}) async-start(bf16[4,8,64,640]{3,2,1,0:T(8,128)(2,1)} %wide_queries.1), calls=%async_computation | async-start | bytes 5242880 | tf_op jit(solution)/shard_map/all_to_all | solution.py:50
  8.4 6.9 %collective-permute-start.7 = (bf16[704,128]{1,0:T(8,128)(2,1)S(1)}, bf16[704,128]{1,0:T(8,128)(2,1)S(1)}, u32[]{:S(2)}, u32[]{:S(2)}) collective-permute-start(bf16[704,128]{1,0:T(8,128)(2,1)S(1)} %pad_maximum_fusion.1.refs_0_), channel_id=1, source_target_pairs={{0,192},{16,208},{32,224},{48,240},{64,0},{80,16},{96,32},{112,48}... | collective-permute-start | bytes 540680 | tf_op jit(solution)/shard_map/ppermute | solution.py:30
  11.5 11.1 %collective-permute-start.9 = (bf16[704,128]{1,0:T(8,128)(2,1)S(1)}, bf16[704,128]{1,0:T(8,128)(2,1)S(1)}, u32[]{:S(2)}, u32[]{:S(2)}) collective-permute-start(bf16[704,128]{1,0:T(8,128)(2,1)S(1)} %pad_maximum_fusion.1.refs_0_), channel_id=1, source_target_pairs={{0,64},{16,80},{32,96},{48,112},{64,128},{80,144},{96,160},{112,17... | collective-permute-start | bytes 540680 | tf_op jit(solution)/shard_map/ppermute | solution.py:30
  11.5 11.1 %collective-permute-start.13 = (bf16[704,128]{1,0:T(8,128)(2,1)S(1)}, bf16[704,128]{1,0:T(8,128)(2,1)S(1)}, u32[]{:S(2)}, u32[]{:S(2)}) collective-permute-start(bf16[704,128]{1,0:T(8,128)(2,1)S(1)} %pad_maximum_fusion.1.refs_0_), channel_id=1, source_target_pairs={{0,32},{16,48},{32,0},{48,16},{64,96},{80,112},{96,64},{112,80},{1... | collective-permute-start | bytes 540680 | tf_op jit(solution)/shard_map/ppermute | solution.py:34
  12.3 10.3 %collective-permute-start.6 = (bf16[704,128]{1,0:T(8,128)(2,1)S(1)}, bf16[704,128]{1,0:T(8,128)(2,1)S(1)}, u32[]{:S(2)}, u32[]{:S(2)}) collective-permute-start(bf16[704,128]{1,0:T(8,128)(2,1)S(1)} %pad_maximum_fusion.1.refs_0_), channel_id=1, source_target_pairs={{0,16},{16,0},{32,48},{48,32},{64,80},{80,64},{96,112},{112,96},{1... | collective-permute-start | bytes 540680 | tf_op jit(solution)/shard_map/ppermute | solution.py:38
  12.4 12.3 %collective-permute-start.11 = (bf16[704,128]{1,0:T(8,128)(2,1)S(1)}, bf16[704,128]{1,0:T(8,128)(2,1)S(1)}, u32[]{:S(2)}, u32[]{:S(2)}) collective-permute-start(bf16[704,128]{1,0:T(8,128)(2,1)S(1)} %pad_maximum_fusion.1.refs_0_), channel_id=1, source_target_pairs={{0,128},{16,144},{32,160},{48,176},{64,192},{80,208},{96,224},{112... | collective-permute-start | bytes 540680 | tf_op jit(solution)/shard_map/ppermute | solution.py:30
  15.3 9.3 %collective-permute-start.8 = (bf16[704,128]{1,0:T(8,128)(2,1)S(1)}, bf16[704,128]{1,0:T(8,128)(2,1)S(1)}, u32[]{:S(2)}, u32[]{:S(2)}) collective-permute-start(bf16[704,128]{1,0:T(8,128)(2,1)S(1)} %collective-permute-done.7.refs_2_), channel_id=1, source_target_pairs={{0,16},{16,0},{32,48},{48,32},{64,80},{80,64},{96,112},{112,96},{1... | collective-permute-start | bytes 540680 | tf_op jit(solution)/shard_map/ppermute | solution.py:38
  22.6 2.2 %collective-permute-start.10 = (bf16[704,128]{1,0:T(8,128)(2,1)S(1)}, bf16[704,128]{1,0:T(8,128)(2,1)S(1)}, u32[]{:S(2)}, u32[]{:S(2)}) collective-permute-start(bf16[704,128]{1,0:T(8,128)(2,1)S(1)} %collective-permute-done.9.refs_4_), channel_id=1, source_target_pairs={{0,16},{16,0},{32,48},{48,32},{64,80},{80,64},{96,112},{112,96},{1... | collective-permute-start | bytes 540680 | tf_op jit(solution)/shard_map/ppermute | solution.py:38
  22.6 7.4 %collective-permute-start.15 = (bf16[704,128]{1,0:T(8,128)(2,1)S(1)}, bf16[704,128]{1,0:T(8,128)(2,1)S(1)}, u32[]{:S(2)}, u32[]{:S(2)}) collective-permute-start(bf16[704,128]{1,0:T(8,128)(2,1)S(1)} %collective-permute-done.13.refs_8_), channel_id=1, source_target_pairs={{0,192},{16,208},{32,224},{48,240},{64,0},{80,16},{96,32},{112,48}... | collective-permute-start | bytes 540680 | tf_op jit(solution)/shard_map/ppermute | solution.py:30
  22.6 12.1 %collective-permute-start.17 = (bf16[704,128]{1,0:T(8,128)(2,1)S(1)}, bf16[704,128]{1,0:T(8,128)(2,1)S(1)}, u32[]{:S(2)}, u32[]{:S(2)}) collective-permute-start(bf16[704,128]{1,0:T(8,128)(2,1)S(1)} %collective-permute-done.13.refs_8_), channel_id=1, source_target_pairs={{0,64},{16,80},{32,96},{48,112},{64,128},{80,144},{96,160},{112,17... | collective-permute-start | bytes 540680 | tf_op jit(solution)/shard_map/ppermute | solution.py:30
  24.6 10.1 %collective-permute-start.19 = (bf16[704,128]{1,0:T(8,128)(2,1)S(1)}, bf16[704,128]{1,0:T(8,128)(2,1)S(1)}, u32[]{:S(2)}, u32[]{:S(2)}) collective-permute-start(bf16[704,128]{1,0:T(8,128)(2,1)S(1)} %collective-permute-done.13.refs_8_), channel_id=1, source_target_pairs={{0,128},{16,144},{32,160},{48,176},{64,192},{80,208},{96,224},{112... | collective-permute-start | bytes 540680 | tf_op jit(solution)/shard_map/ppermute | solution.py:30
  24.7 10.6 %collective-permute-start.14 = (bf16[704,128]{1,0:T(8,128)(2,1)S(1)}, bf16[704,128]{1,0:T(8,128)(2,1)S(1)}, u32[]{:S(2)}, u32[]{:S(2)}) collective-permute-start(bf16[704,128]{1,0:T(8,128)(2,1)S(1)} %collective-permute-done.13.refs_8_), channel_id=1, source_target_pairs={{0,16},{16,0},{32,48},{48,32},{64,80},{80,64},{96,112},{112,96},{1... | collective-permute-start | bytes 540680 | tf_op jit(solution)/shard_map/ppermute | solution.py:38
  24.8 10.5 %collective-permute-start.12 = (bf16[704,128]{1,0:T(8,128)(2,1)S(1)}, bf16[704,128]{1,0:T(8,128)(2,1)S(1)}, u32[]{:S(2)}, u32[]{:S(2)}) collective-permute-start(bf16[704,128]{1,0:T(8,128)(2,1)S(1)} %collective-permute-done.11.refs_6_), channel_id=1, source_target_pairs={{0,16},{16,0},{32,48},{48,32},{64,80},{80,64},{96,112},{112,96},{1... | collective-permute-start | bytes 540680 | tf_op jit(solution)/shard_map/ppermute | solution.py:38
  30.0 5.2 %collective-permute-start.16 = (bf16[704,128]{1,0:T(8,128)(2,1)S(1)}, bf16[704,128]{1,0:T(8,128)(2,1)S(1)}, u32[]{:S(2)}, u32[]{:S(2)}) collective-permute-start(bf16[704,128]{1,0:T(8,128)(2,1)S(1)} %collective-permute-done.15.refs_10_), channel_id=1, source_target_pairs={{0,16},{16,0},{32,48},{48,32},{64,80},{80,64},{96,112},{112,96},{1... | collective-permute-start | bytes 540680 | tf_op jit(solution)/shard_map/ppermute | solution.py:38
  34.7 1.4 %collective-permute-start.18 = (bf16[704,128]{1,0:T(8,128)(2,1)S(1)}, bf16[704,128]{1,0:T(8,128)(2,1)S(1)}, u32[]{:S(2)}, u32[]{:S(2)}) collective-permute-start(bf16[704,128]{1,0:T(8,128)(2,1)S(1)} %collective-permute-done.17.refs_12_), channel_id=1, source_target_pairs={{0,16},{16,0},{32,48},{48,32},{64,80},{80,64},{96,112},{112,96},{1... | collective-permute-start | bytes 540680 | tf_op jit(solution)/shard_map/ppermute | solution.py:38
  34.7 2.1 %collective-permute-start.20 = (bf16[704,128]{1,0:T(8,128)(2,1)S(1)}, bf16[704,128]{1,0:T(8,128)(2,1)S(1)}, u32[]{:S(2)}, u32[]{:S(2)}) collective-permute-start(bf16[704,128]{1,0:T(8,128)(2,1)S(1)} %collective-permute-done.19.refs_14_), channel_id=1, source_target_pairs={{0,16},{16,0},{32,48},{48,32},{64,80},{80,64},{96,112},{112,96},{1... | collective-permute-start | bytes 540680 | tf_op jit(solution)/shard_map/ppermute | solution.py:38
  35.2 23.9 %copy-start.8 = (f32[256,4]{0,1:T(4,128)S(1)}, f32[256,4]{0,1:T(4,128)}, u32[]{:S(2)}) copy-start(f32[256,4]{0,1:T(4,128)} %param.12) | copy-start | bytes 12292
  35.2 51.8 %copy-start.5 = (s32[2,16]{1,0:T(2,128)S(1)}, s32[2,16]{1,0:T(2,128)}, u32[]{:S(2)}) copy-start(s32[2,16]{1,0:T(2,128)} %kept_ref.3) | copy-start | bytes 388
  35.3 24.9 %copy-start = (bf16[256,4,128]{2,1,0:T(4,128)(2,1)S(1)}, bf16[256,4,128]{2,1,0:T(4,128)(2,1)}, u32[]{:S(2)}) copy-start(bf16[256,4,128]{2,1,0:T(4,128)(2,1)} %param.10) | copy-start | bytes 786436
  36.2 0.7 copy-start.1
  36.8 0.7 copy-start.3
  40.7 0.9 copy-start.2
  41.6 0.9 copy-start.4
  51.6 38.5 %all-to-all-start.1 = ((bf16[4,16,2048]{2,1,0:T(8,128)(2,1)}), bf16[4,16,2048]{2,1,0:T(8,128)(2,1)S(1)}, u32[]{:S(2)}, u32[]{:S(2)}) async-start(bf16[4,16,2048]{2,1,0:T(8,128)(2,1)} %bitcast.9), calls=%async_computation.1 | async-start | bytes 524288 | tf_op jit(solution)/shard_map/all_to_all | solution.py:50
  60.8 12.0 %collective-permute-start = (bf16[4,80,128]{2,1,0:T(8,128)(2,1)S(1)}, bf16[4,80,128]{2,1,0:T(8,128)(2,1)S(1)}, u32[]{:S(2)}, u32[]{:S(2)}) collective-permute-start(bf16[4,80,128]{2,1,0:T(8,128)(2,1)S(1)} %get-tuple-element.18), channel_id=1, source_target_pairs={{0,4},{1,5},{2,6},{3,7},{4,8},{5,9},{6,10},{7,11},{8,12},{9,13},{1... | collective-permute-start | bytes 245768 | tf_op jit(solution)/shard_map/ppermute | solution.py:46
  63.8 9.0 %collective-permute-start.1 = (bf16[4,80,128]{2,1,0:T(8,128)(2,1)S(1)}, bf16[4,80,128]{2,1,0:T(8,128)(2,1)S(1)}, u32[]{:S(2)}, u32[]{:S(2)}) collective-permute-start(bf16[4,80,128]{2,1,0:T(8,128)(2,1)S(1)} %get-tuple-element.19), channel_id=1, source_target_pairs={{0,12},{1,13},{2,14},{3,15},{4,0},{5,1},{6,2},{7,3},{8,4},{9,5},{1... | collective-permute-start | bytes 245768 | tf_op jit(solution)/shard_map/ppermute | solution.py:46
  65.1 12.2 %collective-permute-start.2 = (bf16[4,80,128]{2,1,0:T(8,128)(2,1)S(1)}, bf16[4,80,128]{2,1,0:T(8,128)(2,1)S(1)}, u32[]{:S(2)}, u32[]{:S(2)}) collective-permute-start(bf16[4,80,128]{2,1,0:T(8,128)(2,1)S(1)} %get-tuple-element.20), channel_id=1, source_target_pairs={{0,8},{1,9},{2,10},{3,11},{4,12},{5,13},{6,14},{7,15},{8,0},{9,1},... | collective-permute-start | bytes 245768 | tf_op jit(solution)/shard_map/ppermute | solution.py:46
  77.8 5.7 %collective-permute-start.3 = (bf16[4,80,128]{2,1,0:T(8,128)(2,1)S(1)}, bf16[4,80,128]{2,1,0:T(8,128)(2,1)S(1)}, u32[]{:S(2)}, u32[]{:S(2)}) collective-permute-start(bf16[4,80,128]{2,1,0:T(8,128)(2,1)S(1)} %get-tuple-element.22), channel_id=1, source_target_pairs={{0,1},{1,2},{2,3},{3,0},{4,5},{5,6},{6,7},{7,4},{8,9},{9,10},{10,1... | collective-permute-start | bytes 245768 | tf_op jit(solution)/shard_map/ppermute | solution.py:42
  78.5 5.5 %collective-permute-start.4 = (bf16[4,80,128]{2,1,0:T(8,128)(2,1)S(1)}, bf16[4,80,128]{2,1,0:T(8,128)(2,1)S(1)}, u32[]{:S(2)}, u32[]{:S(2)}) collective-permute-start(bf16[4,80,128]{2,1,0:T(8,128)(2,1)S(1)} %get-tuple-element.23), channel_id=1, source_target_pairs={{0,3},{1,0},{2,1},{3,2},{4,7},{5,4},{6,5},{7,6},{8,11},{9,8},{10,9... | collective-permute-start | bytes 245768 | tf_op jit(solution)/shard_map/ppermute | solution.py:42
  81.1 5.9 %collective-permute-start.5 = (bf16[4,80,128]{2,1,0:T(8,128)(2,1)S(1)}, bf16[4,80,128]{2,1,0:T(8,128)(2,1)S(1)}, u32[]{:S(2)}, u32[]{:S(2)}) collective-permute-start(bf16[4,80,128]{2,1,0:T(8,128)(2,1)S(1)} %get-tuple-element.24), channel_id=1, source_target_pairs={{0,2},{1,3},{2,0},{3,1},{4,6},{5,7},{6,4},{7,5},{8,10},{9,11},{10,... | collective-permute-start | bytes 245768 | tf_op jit(solution)/shard_map/ppermute | solution.py:42
  94.7 1.6 %collective-permute-start.21 = (bf16[8,128,128]{2,1,0:T(8,128)(2,1)S(1)}, bf16[8,128,128]{2,1,0:T(8,128)(2,1)S(1)}, u32[]{:S(2)}, u32[]{:S(2)}) collective-permute-start(bf16[8,128,128]{2,1,0:T(8,128)(2,1)S(1)} %get-tuple-element.31), channel_id=1, source_target_pairs={{0,16},{16,0},{32,48},{48,32},{64,80},{80,64},{96,112},{112,96},{1... | collective-permute-start | bytes 786440 | tf_op jit(solution)/shard_map/ppermute | solution.py:38

commit v4 on v3

--- a/solution.py
+++ b/solution.py
@@ -17,7 +17,6 @@
 SM = pl.BlockSpec(memory_space=pltpu.SMEM)
 HB = pl.BlockSpec(memory_space=pltpu.HBM)
 
-ROW_X = [[zh * 4 + x for x in range(4)] for zh in range(4)]
 ROW_ZH = [[zh * 4 + x for zh in range(4)] for x in range(4)]
 YZX = [
     [(y * 4 + z * 2 + c) * 16 + zh * 4 + x for y in range(4) for z in range(2) for x in range(4)]
@@ -40,10 +39,6 @@
 
 def along_x(value, d):
     return lax.ppermute(value, "head", [(i, i // 4 * 4 + (i + d) % 4) for i in range(16)])
-
-
-def along_zh(value, d):
-    return lax.ppermute(value, "head", [(i, (i + 4 * d) % 16) for i in range(16)])
 
 
 def exchanged(value, axis, groups=None):
@@ -65,7 +60,7 @@
     )
 
 
-def query_body(q_ref, lse_hbm, out_ref, wide, turned, lse_ref, in_sem, out_sem):
+def query_body(at_ref, q_ref, lse_hbm, o0, o1, o2, o3, wide, turned, lse_ref, in_sem, out_sem):
     heads, width, rows = q_ref.shape
     loads = [
         pltpu.make_async_copy(q_ref.at[h], wide.at[h, 0:width, :], in_sem.at[h]) for h in range(heads)
@@ -89,37 +84,45 @@
             for zh in range(4):
                 at = (zh * 4 + x) * 16
                 turned[h, x, zh * 16 : zh * 16 + 16, :] = flat[at : at + 16]
-        stores.append(pltpu.make_async_copy(turned.at[h], out_ref.at[:, h], out_sem.at[h]))
-        stores[-1].start()
+        for i, out in enumerate((o0, o1, o2, o3)):
+            x = lax.rem(at_ref[1] + ((0,) + STEPS)[i], 4)
+            store = pltpu.make_async_copy(turned.at[h, x], out.at[h], out_sem.at[4 * h + i])
+            store.start()
+            stores.append(store)
     for store in stores:
         store.wait()
 
 
-def wide_queries(query, normalizer):
+def in_hbm(*values):
+    return [pltpu.with_memory_space_constraint(v, pltpu.HBM) for v in values]
+
+
+def wide_queries(at, query, normalizer):
     heads, _, rows = query.shape
     return call(
         query_body,
-        pltpu.HBM((4, heads, rows // 4, 640), bf16),
-        [HB, HB],
+        (pltpu.HBM((heads, rows // 4, 640), bf16),) * 4,
+        [SM, HB, HB],
         12,
-        out_specs=HB,
+        out_specs=(HB,) * 4,
         scratch_shapes=[
             pltpu.VMEM((heads, 640, rows), bf16),
             pltpu.VMEM((heads, 4, rows // 4, 640), bf16),
             pltpu.VMEM((heads, rows), f32),
             pltpu.SemaphoreType.DMA((heads + 1,)),
-            pltpu.SemaphoreType.DMA((heads,)),
+            pltpu.SemaphoreType.DMA((4 * heads,)),
         ],
         name="wide_queries",
-    )(*[pltpu.with_memory_space_constraint(v, pltpu.HBM) for v in (query, normalizer)])
-
-
-def score_body(q_hbm, *refs):
-    tiles, (out_ref, index_ref, q_ref, keys, acc, q_sem) = refs[:16], refs[16:]
-    groups, heads, rows, depth = q_ref.shape
+    )(at, *in_hbm(query, normalizer))
+
+
+def score_body(groups, last, *refs):
+    q_hbm, tiles, refs = refs[:groups], refs[groups : groups + 16], refs[groups + 16 :]
+    before, (out_ref, *index, q_ref, keys, acc, q_sem) = refs[:last], refs[last:]
+    heads, rows, depth = q_ref.shape[1:]
     width = tiles[0].shape[0] - 128
     q_loads = [
-        pltpu.make_async_copy(q_hbm.at[a], q_ref.at[a], q_sem.at[a]) for a in range(groups)
+        pltpu.make_async_copy(q_hbm[a], q_ref.at[a], q_sem.at[a]) for a in range(groups)
     ]
     for load in q_loads:
         load.start()
@@ -128,7 +131,8 @@
         keys[n, width:, :] = jnp.where(row < 3, 1.0, 0.0).astype(bf16)
     for i, tile in enumerate(tiles):
         keys[i // 4, 0:width, i % 4 * 128 : i % 4 * 128 + 128] = tile[128 : 128 + width, :]
-        index_ref[i * 128 : i * 128 + 128, :] = tile[0:128, :]
+        for index_ref in index:
+            index_ref[i * 128 : i * 128 + 128, :] = tile[0:128, :]
     for a in range(groups):
         q_loads[a].wait()
         some = q_ref[a].reshape(heads * rows, depth)
@@ -137,45 +141,33 @@
             s = jnp.dot(some, keys[n], preferred_element_type=f32)
             p = jnp.exp2(s * (attn_scale * LOG2E))
             total = acc[:, at : at + 512] if a else None
+            for ref in before if a == 0 else ():
+                total = ref[:, at : at + 512]
             for h in range(heads):
                 part = p[h * rows : h * rows + rows]
                 total = part if total is None else total + part
             if a + 1 < groups:
                 acc[:, at : at + 512] = total
             else:
-                out_ref[:, at : at + 512] = total.astype(bf16)
-
-
-def scores(query, tiles):
-    groups, _, rows, depth = query.shape
+                out_ref[:, at : at + 512] = total.astype(out_ref.dtype)
+
+
+def scores(queries, tiles, *before):
+    heads, rows, depth = queries[0].shape
+    groups, last = len(queries), len(before)
     return call(
-        score_body,
-        (sds((rows, 2048), bf16), sds((2048, 128), bf16)),
-        [HB] + [VM] * 16,
+        functools.partial(score_body, groups, last),
+        (sds((rows, 2048), bf16),) if last else (sds((rows, 2048), f32), sds((2048, 128), bf16)),
+        [HB] * groups + [VM] * (16 + last),
         16,
         scratch_shapes=[
-            pltpu.VMEM(query.shape, bf16),
+            pltpu.VMEM((groups, heads, rows, depth), bf16),
             pltpu.VMEM((4, depth, 512), bf16),
             pltpu.VMEM((rows, 2048), f32),
             pltpu.SemaphoreType.DMA((groups,)),
         ],
         name="scores",
-    )(pltpu.with_memory_space_constraint(query, pltpu.HBM), *tiles)
-
-
-def pack_body(at_ref, q_ref, w_ref, *outs):
-    for d, ref in zip((0,) + STEPS, outs):
-        zh = lax.rem(at_ref[0] + d, 4)
-        for x in range(4):
-            ref[x, 0:64, :] = q_ref[zh * 4 + x]
-            ref[x, 64:80, :] = w_ref[zh * 4 + x]
-
-
-def spread_body(at_ref, *refs):
-    for d, ref in zip((0,) + STEPS, refs[4:]):
-        x = lax.rem(at_ref[1] + d, 4)
-        for e in range(4):
-            ref[e] = refs[e][x]
+    )(*in_hbm(*queries), *tiles, *before)
 
 
 def weight_column(q_ref, j):
@@ -204,11 +196,7 @@
 TN = (((0,), (0,)), ((), ()))
 
 
-def index_body(scale, at_ref, kept_ref, *refs):
-    keys, prob_ref, q_ref, acc = refs[4:]
-    for g in range(4):
-        for a in range(4):
-            q_ref[4 * g + a] = refs[g][a]
+def index_body(scale, at_ref, kept_ref, q_ref, keys, prob_ref, acc):
     acc[...] = jnp.zeros_like(acc)
 
     @pl.loop(0, 4)
@@ -236,12 +224,12 @@
 def index_forward(at, kept, queries, keys, scale):
     return call(
         functools.partial(index_body, scale),
-        (sds((16, 2048), f32), sds((16, 80, 128), bf16)),
-        [SM, SM] + [VM] * 5,
+        sds((16, 2048), f32),
+        [SM, SM, VM, VM],
         14,
         scratch_shapes=[pltpu.VMEM((64, 2048), f32)],
         name="index_forward",
-    )(at, kept, *queries, keys)
+    )(at, kept, queries, keys)
 
 
 def back_body(scale, at_ref, kept_ref, prob_ref, q_ref, keys, sums, *refs):
@@ -265,11 +253,7 @@
             dz[at : at + 64, :] = jnp.where(z[at : at + 64] > 0.0, value, 0.0).astype(bf16)
         dk[...] += lax.dot_general(rows, dz[...], TN, preferred_element_type=f32)
         dq = jnp.dot(dz[...], keys[...], preferred_element_type=f32) * scale
-        d = jnp.where(g < 2, g, 5 - g)
-        x = lax.rem(at_ref[1] + 4 - d, 4)
-        for a, e in enumerate((0,) + STEPS):
-            zh = lax.rem(at_ref[0] + 4 - e, 4)
-            dq_ref[zh * 4 + x] = dq[a * 64 : a * 64 + 64].astype(bf16)
+        dq_ref[pl.ds(4 * g, 4)] = dq.astype(bf16).reshape(4, 64, 128)
 
     for slot in range(16):
         tile = dk[:, slot * 128 : slot * 128 + 128] * scale
@@ -278,6 +262,16 @@
             own_ref[place] = tile
         else:
             send_ref[place] = tile.astype(bf16)
+
+
+def last_body(both_ref, dq_ref, dk_ref):
+    for x in range(4):
+        total = both_ref[x, 64:96].astype(f32)
+        for zh in range(1, 4):
+            total += both_ref[4 * zh + x, 64:96].astype(f32)
+        dk_ref[:, x * 32 : x * 32 + 32] = total.T
+    for j in range(16):
+        dq_ref[j] = both_ref[j, 0:64]
 
 
 def index_backward(at, kept, prob, queries, keys, sums, scale):
@@ -315,24 +309,18 @@
     w2 = index_weight - w0 - w1
     weight = jnp.stack([w.reshape(16, 64) for w in (w0, w1, w2)], axis=1).astype(bf16)
     weight = jnp.pad(weight, ((0, 0), (0, 13), (0, 64)))
-    four = (sds((4, 80, 128), bf16),) * 4
-    parts = call(pack_body, four, [SM, VM, VM], 6, name="pack")(
-        at, index_query.reshape(16, 64, 128), weight
-    )
-    got = [parts[0]]
+    queries = jnp.concatenate([index_query.reshape(16, 64, 128), weight], axis=1)
+    queries = exchanged(queries, "head")
+
+    parts = wide_queries(at, jnp.transpose(query_latent, (1, 2, 0)), normalizer.T)
+    query = [parts[0]]
     for part, d in zip(parts[1:], STEPS):
-        got.append(along_zh(part, d))
-    parts = call(spread_body, four, [SM] + [VM] * 4, 6, name="spread")(at, *got)
-    queries = [parts[0]]
-    for part, d in zip(parts[1:], STEPS):
-        queries.append(along_x(part, d))
-
-    query = wide_queries(jnp.transpose(query_latent, (1, 2, 0)), normalizer.T)
-    query = exchanged(query, "head", ROW_X)
-    part, index_keys = scores(query, tiles)
+        query.append(along_x(part, d))
+    part, index_keys = scores(query[:3], tiles)
+    (part,) = scores(query[3:], tiles, part)
     sums = exchanged(part.reshape(4, 16, 2048), "head", ROW_ZH)
 
-    prob, queries = index_forward(at, kept, queries, index_keys, index_scale)
+    prob = index_forward(at, kept, queries, index_keys, index_scale)
     own, send, dq = index_backward(at, kept, prob, queries, index_keys, sums, index_scale)
 
     got = other_core(send)
@@ -341,8 +329,10 @@
     dkey = jnp.sum(dkey.astype(f32), axis=0).astype(bf16)
     dkey = jnp.broadcast_to(dkey, (16, 32, 128))
     both = exchanged(jnp.concatenate([dq, dkey], axis=1), "head")
-    dkey = both[:, 64:].astype(f32).reshape(4, 4, 32, 128).sum(axis=0).reshape(128, 128).T
-    return both[:, :64].reshape(index_query.shape), dkey
+    dq, dkey = call(
+        last_body, (sds((16, 64, 128), bf16), sds((128, 128), f32)), [VM], 6, name="last"
+    )(both)
+    return dq.reshape(index_query.shape), dkey
 
 
 def solution(mesh):

time: 132 us -> 121 us (0.917)
  the two profiles are of different devices: /device:TPU:32 before, /device:TPU:2 now
where the time goes in v4:
time: 121 us; the launch traced here: 120 us
  starting transfers between devices  39.1 us (32%)
  blocking collectives  39.1 us (32%)
  Pallas kernels  22.4 us (19%)
  waiting for transfers between devices  14.3 us (12%)
  other arithmetic  2.62 us (2%)
  local copies, waits for them, and re-layouts  1.77 us (1%)
    all_to_all x2, blocking collectives, exchanged(): lax.all_to_all(value, axis, 0, 0, tiled=True, axis_index_groups=groups)  39.1 us
    all_to_all x2, starting transfers between devices, exchanged(): lax.all_to_all(value, axis, 0, 0, tiled=True, axis_index_groups=groups)  18.2 us
    ppermute x6, starting transfers between devices, along_y(): lax.ppermute(value, 'seq', [(i, (i + 4 * d) % 16) for i in range(16)])  13.2 us
    pallas_call x2, Pallas kernels, scores(): call(functools.partial(score_body, groups, last), (sds((rows, 2048), bf16...  10.2 us
    all_to_all x2, waiting for transfers between devices, exchanged(): lax.all_to_all(value, axis, 0, 0, tiled=True, axis_index_groups=groups)  6.76 us
    ppermute x9, waiting for transfers between devices, other_core(): return lax.ppermute(value, 'seq', [(i, i ^ 1) for i in range(16)])  4.73 us
    pallas_call x1, Pallas kernels, index_backward(): call(functools.partial(back_body, scale), (sds((8, 128, 128), f32), sds((...  4.63 us
    ppermute x3, starting transfers between devices, along_x(): lax.ppermute(value, 'head', [(i, i // 4 * 4 + (i + d) % 4) for i in range...  4.23 us
  transfers between devices with their start and end apart: 21, of which 9 were waited for; matrix products, arithmetic and copies ran while one was open for 2% of the time, Pallas kernels for 14%

profile of v4, /device:TPU:2, one launch (start us, length us, event | category | flops | bytes accessed | tf_op | source)
XLA Modules:
  0.0 120.1 jit_solution(2184710119079409134)
XLA Ops:
  0.6 1.0 pad_maximum_fusion.2.refs_3_.refs_1_
  1.6 2.0 %collective-permute-start.9 = (bf16[704,128]{1,0:T(8,128)(2,1)S(1)}, bf16[704,128]{1,0:T(8,128)(2,1)S(1)}, u32[]{:S(2)}, u32[]{:S(2)}) collective-permute-start(bf16[704,128]{1,0:T(8,128)(2,1)S(1)} %pad_maximum_fusion.2.refs_3_.refs_1_), channel_id=1, source_target_pairs={{0,32},{16,48},{32,0},{48,16},{64,96},{80,112},{96,64},{112,80},{1... | collective-permute-start | bytes 540680 | tf_op jit(solution)/shard_map/ppermute | solution.py:33
  3.6 3.0 %collective-permute-start.3 = (bf16[704,128]{1,0:T(8,128)(2,1)S(1)}, bf16[704,128]{1,0:T(8,128)(2,1)S(1)}, u32[]{:S(2)}, u32[]{:S(2)}) collective-permute-start(bf16[704,128]{1,0:T(8,128)(2,1)S(1)} %pad_maximum_fusion.2.refs_3_.refs_1_), channel_id=1, source_target_pairs={{0,192},{16,208},{32,224},{48,240},{64,0},{80,16},{96,32},{112,48}... | collective-permute-start | bytes 540680 | tf_op jit(solution)/shard_map/ppermute | solution.py:29
  6.6 0.0 collective-permute-start.5
  6.6 2.2 %collective-permute-start.7 = (bf16[704,128]{1,0:T(8,128)(2,1)S(1)}, bf16[704,128]{1,0:T(8,128)(2,1)S(1)}, u32[]{:S(2)}, u32[]{:S(2)}) collective-permute-start(bf16[704,128]{1,0:T(8,128)(2,1)S(1)} %pad_maximum_fusion.2.refs_3_.refs_1_), channel_id=1, source_target_pairs={{0,128},{16,144},{32,160},{48,176},{64,192},{80,208},{96,224},{112... | collective-permute-start | bytes 540680 | tf_op jit(solution)/shard_map/ppermute | solution.py:29
  8.8 0.0 collective-permute-start.2
  8.8 0.0 collective-permute-done.9.refs_11_.refs_9_
  8.8 2.3 %collective-permute-start.11 = (bf16[704,128]{1,0:T(8,128)(2,1)S(1)}, bf16[704,128]{1,0:T(8,128)(2,1)S(1)}, u32[]{:S(2)}, u32[]{:S(2)}) collective-permute-start(bf16[704,128]{1,0:T(8,128)(2,1)S(1)} %collective-permute-done.9.refs_11_.refs_9_), channel_id=1, source_target_pairs={{0,192},{16,208},{32,224},{48,240},{64,0},{80,16},{96,32},{112,48}... | collective-permute-start | bytes 540680 | tf_op jit(solution)/shard_map/ppermute | solution.py:29
  11.2 2.8 %collective-permute-done.3.refs_5_.refs_3_ = bf16[704,128]{1,0:T(8,128)(2,1)S(1)} collective-permute-done((bf16[704,128]{1,0:T(8,128)(2,1)S(1)}, bf16[704,128]{1,0:T(8,128)(2,1)S(1)}, u32[]{:S(2)}, u32[]{:S(2)}) %collective-permute-start.3) | collective-permute-done | bytes 180256 | tf_op jit(solution)/shard_map/ppermute | solution.py:29
  14.0 0.0 collective-permute-start.13
  14.0 0.7 reduce-precision_convert_fusion.1
  14.7 0.1 copy.12
  14.9 0.1 stack_reshape.15
  15.0 0.1 copy.13
  15.1 0.1 stack_reshape.16
  15.3 0.1 copy.14
  15.4 0.1 stack_reshape.17
  15.6 0.1 stack.27.at_ref
  15.7 3.8 %wide_queries.1 = (bf16[8,64,640]{2,1,0:T(8,128)(2,1)}, bf16[8,64,640]{2,1,0:T(8,128)(2,1)}, bf16[8,64,640]{2,1,0:T(8,128)(2,1)}, bf16[8,64,640]{2,1,0:T(8,128)(2,1)}) custom-call(s32[5]{0:T(128)S(1)} %stack.27.at_ref, bf16[8,576,256]{2,1,0:T(8,128)(2,1)} %bitcast.12, f32[8,256]{1,0:T(8,128)} %bitcast.16), custom_call_target="tpu_custom_call" | custom-call | tf_op jit(solution)/shard_map/wide_queries/pallas_call | solution.py:102
  19.4 0.1 fusion.8
  19.5 0.0 collective-permute-done.5.refs_7_.refs_5_
  19.5 1.6 %collective-permute-start = (bf16[8,64,640]{2,1,0:T(8,128)(2,1)}, bf16[8,64,640]{2,1,0:T(8,128)(2,1)S(1)}, u32[]{:S(2)}, u32[]{:S(2)}) collective-permute-start(bf16[8,64,640]{2,1,0:T(8,128)(2,1)} %get-tuple-element.14), channel_id=1, source_target_pairs={{0,1},{1,2},{2,3},{3,0},{4,5},{5,6},{6,7},{7,4},{8,9},{9,10},{10,1... | collective-permute-start | bytes 1966088 | tf_op jit(solution)/shard_map/ppermute | solution.py:41
  21.1 0.0 collective-permute-done.7.refs_9_.refs_7_
  21.1 0.5 collective-permute-start.1
  21.6 0.0 collective-permute-done.2.refs_4_.refs_2_
  21.6 2.1 %collective-permute-start.17 = (bf16[8,64,640]{2,1,0:T(8,128)(2,1)}, bf16[8,64,640]{2,1,0:T(8,128)(2,1)}, u32[]{:S(2)}, u32[]{:S(2)}) collective-permute-start(bf16[8,64,640]{2,1,0:T(8,128)(2,1)} %get-tuple-element.17), channel_id=1, source_target_pairs={{0,2},{1,3},{2,0},{3,1},{4,6},{5,7},{6,4},{7,5},{8,10},{9,11},{10,... | collective-permute-start | bytes 1966088 | tf_op jit(solution)/shard_map/ppermute | solution.py:41
  23.7 0.0 collective-permute-done.11.refs_13_.refs_11_
  23.7 5.6 %collective-permute-start.15 = (bf16[704,128]{1,0:T(8,128)(2,1)S(1)}, bf16[704,128]{1,0:T(8,128)(2,1)S(1)}, u32[]{:S(2)}, u32[]{:S(2)}) collective-permute-start(bf16[704,128]{1,0:T(8,128)(2,1)S(1)} %collective-permute-done.9.refs_11_.refs_9_), channel_id=1, source_target_pairs={{0,128},{16,144},{32,160},{48,176},{64,192},{80,208},{96,224},{112... | collective-permute-start | bytes 540680 | tf_op jit(solution)/shard_map/ppermute | solution.py:29
  29.4 0.0 collective-permute-done.13.refs_15_.refs_13_
  29.4 0.0 collective-permute-start.10
  29.4 0.8 pad_maximum_fusion.1
  30.1 10.2 %all-to-all-start = ((bf16[16,80,128]{2,1,0:T(8,128)(2,1)}), bf16[16,80,128]{2,1,0:T(8,128)(2,1)S(1)}, u32[]{:S(2)}, u32[]{:S(2)}) async-start(bf16[16,80,128]{2,1,0:T(8,128)(2,1)} %pad_maximum_fusion.1), calls=%async_computation | async-start | bytes 655360 | tf_op jit(solution)/shard_map/all_to_all | solution.py:45
  40.3 0.0 collective-permute-done.15.refs_17_.refs_15_
  40.3 0.1 collective-permute-start.4
  40.4 0.0 collective-permute-done.10.refs_12_.refs_10_
  40.4 0.5 collective-permute-start.6
  40.9 0.9 collective-permute-done.4.refs_6_.refs_4_
  41.8 0.1 collective-permute-start.8
  42.0 0.1 collective-permute-done.6.refs_8_.refs_6_
  42.1 0.3 collective-permute-start.12
  42.3 0.9 collective-permute-done.8.refs_10_.refs_8_
  43.2 0.1 collective-permute-start.14
  43.4 0.1 collective-permute-done.12.refs_14_.refs_12_
  43.5 0.3 collective-permute-start.16
  43.8 0.9 collective-permute-done.14.refs_16_.refs_14_
  44.7 0.3 collective-permute-done.16.refs_18_.refs_16_
  44.9 0.0 collective-permute-done.refs_1_
  44.9 0.0 collective-permute-done.1.refs_2_
  44.9 0.8 copy-done.1
  45.8 6.5 %scores.2 = (f32[64,2048]{1,0:T(8,128)S(1)}, bf16[2048,128]{1,0:T(8,128)(2,1)S(1)}) custom-call(bf16[8,64,640]{2,1,0:T(8,128)(2,1)} %get-tuple-element.13.refs_0_, bf16[8,64,640]{2,1,0:T(8,128)(2,1)} %copy-done.1, bf16[8,64,640]{2,1,0:T(8,128)(2,1)} %collective-permute-done.1.refs_2_, bf16[704,128]{1,0:T(8,128)(2,1)S(1)} %pad_maximum_fusion.2.refs_3_.refs_1_, ...), custom_call_target="tpu_custom_call" | custom-call | tf_op jit(solution)/shard_map/scores/pallas_call | solution.py:158
  52.3 0.0 copy-start
  52.3 3.6 %scores.3 = bf16[64,2048]{1,0:T(8,128)(2,1)} custom-call(bf16[8,64,640]{2,1,0:T(8,128)(2,1)} %collective-permute-done.17.refs_0_, bf16[704,128]{1,0:T(8,128)(2,1)S(1)} %pad_maximum_fusion.2.refs_3_.refs_1_, bf16[704,128]{1,0:T(8,128)(2,1)S(1)} %collective-permute-done.2.refs_4_.refs_2_, bf16[704,128]{1,0:T(8,128)(2,1)S(1)} %collective-permute-done.3.refs_5_.refs_3_, ...), custom_call_target="tpu_custom_call" | custom-call | tf_op jit(solution)/shard_map/scores/pallas_call | solution.py:158
  56.0 0.0 all-to-all-done.q_ref
  56.0 8.0 %all-to-all-start.1 = ((bf16[4,16,2048]{2,1,0:T(8,128)(2,1)}), bf16[4,16,2048]{2,1,0:T(8,128)(2,1)S(1)}, u32[]{:S(2)}, u32[]{:S(2)}) async-start(bf16[4,16,2048]{2,1,0:T(8,128)(2,1)} %bitcast.9), calls=%async_computation.1 | async-start | bytes 524288 | tf_op jit(solution)/shard_map/all_to_all | solution.py:45
  64.0 3.0 %index_forward.1.prob_ref = f32[16,2048]{1,0:T(8,128)S(1)} custom-call(s32[5]{0:T(128)S(1)} %stack.27.at_ref, s32[2,16]{1,0:T(2,128)S(1)} %copy-done, bf16[16,80,128]{2,1,0:T(8,128)(2,1)S(1)} %all-to-all-done.q_ref, bf16[2048,128]{1,0:T(8,128)(2,1)S(1)} %get-tuple-element.16.keys), custom_call_target="tpu_custom_call" | custom-call | tf_op jit(solution)/shard_map/index_forward/pallas_call | solution.py:225
  67.0 6.8 %all-to-all-done.1.sums = bf16[4,16,2048]{2,1,0:T(8,128)(2,1)S(1)} async-done(((bf16[4,16,2048]{2,1,0:T(8,128)(2,1)}), bf16[4,16,2048]{2,1,0:T(8,128)(2,1)S(1)}, u32[]{:S(2)}, u32[]{:S(2)}) %all-to-all-start.1) | async-done | bytes 262176 | tf_op jit(solution)/shard_map/all_to_all | solution.py:45
  73.7 4.6 %index_backward.1 = (f32[8,128,128]{2,1,0:T(8,128)S(1)}, bf16[8,128,128]{2,1,0:T(8,128)(2,1)S(1)}, bf16[16,64,128]{2,1,0:T(8,128)(2,1)S(1)}) custom-call(s32[5]{0:T(128)S(1)} %stack.27.at_ref, s32[2,16]{1,0:T(2,128)S(1)} %copy-done, f32[16,2048]{1,0:T(8,128)S(1)} %index_forward.1.prob_ref, bf16[16,80,128]{2,1,0:T(8,128)(2,1)S(1)} %all-to-all-done.q_ref, ...), custom_call_target="tpu_custom_call" | custom-call | tf_op jit(solution)/shard_map/index_backward/pallas_call | solution.py:278
  78.4 0.1 collective-permute-start.18
  78.5 1.5 %collective-permute-done.18 = bf16[8,128,128]{2,1,0:T(8,128)(2,1)S(1)} collective-permute-done((bf16[8,128,128]{2,1,0:T(8,128)(2,1)S(1)}, bf16[8,128,128]{2,1,0:T(8,128)(2,1)S(1)}, u32[]{:S(2)}, u32[]{:S(2)}) %collective-permute-start.18) | collective-permute-done | bytes 262176 | tf_op jit(solution)/shard_map/ppermute | solution.py:37
  80.0 0.1 add_convert_fusion
  80.1 21.0 %all_to_all.20 = bf16[32,32,128]{2,1,0:T(8,128)(2,1)S(1)} all-to-all(bf16[32,32,128]{2,1,0:T(8,128)(2,1)S(1)} %bitcast.13), channel_id=1, replica_groups={{0,1,2,3,32,33,34,35,64,65,66,67,96,97,98,99,128,129,130,131,160,161,16..., dimensions={0} | all-to-all | bytes 524288 | tf_op jit(solution)/shard_map/all_to_all | solution.py:45
  101.1 0.1 reduce_sum.12
  101.2 18.0 %all_to_all.21.both_ref = bf16[16,96,128]{2,1,0:T(8,128)(2,1)S(1)} all-to-all(bf16[16,96,128]{2,1,0:T(8,128)(2,1)S(1)} %pad_maximum_fusion), channel_id=1, replica_groups=mesh['seq'=16,'head'=16] {'head'}, dimensions={0} | all-to-all | bytes 786432 | tf_op jit(solution)/shard_map/all_to_all | solution.py:45
  119.2 0.9 last.1
  (7 shorter events, 0.1 us)
Async XLA Ops:
  0.6 28.8 %copy-start.2 = (bf16[256,4,128]{2,1,0:T(4,128)(2,1)S(1)}, bf16[256,4,128]{2,1,0:T(4,128)(2,1)}, u32[]{:S(2)}) copy-start(bf16[256,4,128]{2,1,0:T(4,128)(2,1)} %param.10) | copy-start | bytes 786436
  1.6 7.2 %collective-permute-start.9 = (bf16[704,128]{1,0:T(8,128)(2,1)S(1)}, bf16[704,128]{1,0:T(8,128)(2,1)S(1)}, u32[]{:S(2)}, u32[]{:S(2)}) collective-permute-start(bf16[704,128]{1,0:T(8,128)(2,1)S(1)} %pad_maximum_fusion.2.refs_3_.refs_1_), channel_id=1, source_target_pairs={{0,32},{16,48},{32,0},{48,16},{64,96},{80,112},{96,64},{112,80},{1... | collective-permute-start | bytes 540680 | tf_op jit(solution)/shard_map/ppermute | solution.py:33
  3.6 10.4 %collective-permute-start.3 = (bf16[704,128]{1,0:T(8,128)(2,1)S(1)}, bf16[704,128]{1,0:T(8,128)(2,1)S(1)}, u32[]{:S(2)}, u32[]{:S(2)}) collective-permute-start(bf16[704,128]{1,0:T(8,128)(2,1)S(1)} %pad_maximum_fusion.2.refs_3_.refs_1_), channel_id=1, source_target_pairs={{0,192},{16,208},{32,224},{48,240},{64,0},{80,16},{96,32},{112,48}... | collective-permute-start | bytes 540680 | tf_op jit(solution)/shard_map/ppermute | solution.py:29
  6.6 12.9 %collective-permute-start.5 = (bf16[704,128]{1,0:T(8,128)(2,1)S(1)}, bf16[704,128]{1,0:T(8,128)(2,1)S(1)}, u32[]{:S(2)}, u32[]{:S(2)}) collective-permute-start(bf16[704,128]{1,0:T(8,128)(2,1)S(1)} %pad_maximum_fusion.2.refs_3_.refs_1_), channel_id=1, source_target_pairs={{0,64},{16,80},{32,96},{48,112},{64,128},{80,144},{96,160},{112,17... | collective-permute-start | bytes 540680 | tf_op jit(solution)/shard_map/ppermute | solution.py:29
  6.6 14.4 %collective-permute-start.7 = (bf16[704,128]{1,0:T(8,128)(2,1)S(1)}, bf16[704,128]{1,0:T(8,128)(2,1)S(1)}, u32[]{:S(2)}, u32[]{:S(2)}) collective-permute-start(bf16[704,128]{1,0:T(8,128)(2,1)S(1)} %pad_maximum_fusion.2.refs_3_.refs_1_), channel_id=1, source_target_pairs={{0,128},{16,144},{32,160},{48,176},{64,192},{80,208},{96,224},{112... | collective-permute-start | bytes 540680 | tf_op jit(solution)/shard_map/ppermute | solution.py:29
  8.8 12.8 %collective-permute-start.2 = (bf16[704,128]{1,0:T(8,128)(2,1)S(1)}, bf16[704,128]{1,0:T(8,128)(2,1)S(1)}, u32[]{:S(2)}, u32[]{:S(2)}) collective-permute-start(bf16[704,128]{1,0:T(8,128)(2,1)S(1)} %pad_maximum_fusion.2.refs_3_.refs_1_), channel_id=1, source_target_pairs={{0,16},{16,0},{32,48},{48,32},{64,80},{80,64},{96,112},{112,96},{1... | collective-permute-start | bytes 540680 | tf_op jit(solution)/shard_map/ppermute | solution.py:37
  8.8 14.9 %collective-permute-start.11 = (bf16[704,128]{1,0:T(8,128)(2,1)S(1)}, bf16[704,128]{1,0:T(8,128)(2,1)S(1)}, u32[]{:S(2)}, u32[]{:S(2)}) collective-permute-start(bf16[704,128]{1,0:T(8,128)(2,1)S(1)} %collective-permute-done.9.refs_11_.refs_9_), channel_id=1, source_target_pairs={{0,192},{16,208},{32,224},{48,240},{64,0},{80,16},{96,32},{112,48}... | collective-permute-start | bytes 540680 | tf_op jit(solution)/shard_map/ppermute | solution.py:29
  14.0 15.4 %collective-permute-start.13 = (bf16[704,128]{1,0:T(8,128)(2,1)S(1)}, bf16[704,128]{1,0:T(8,128)(2,1)S(1)}, u32[]{:S(2)}, u32[]{:S(2)}) collective-permute-start(bf16[704,128]{1,0:T(8,128)(2,1)S(1)} %collective-permute-done.9.refs_11_.refs_9_), channel_id=1, source_target_pairs={{0,64},{16,80},{32,96},{48,112},{64,128},{80,144},{96,160},{112,17... | collective-permute-start | bytes 540680 | tf_op jit(solution)/shard_map/ppermute | solution.py:29
  19.5 25.4 %collective-permute-start = (bf16[8,64,640]{2,1,0:T(8,128)(2,1)}, bf16[8,64,640]{2,1,0:T(8,128)(2,1)S(1)}, u32[]{:S(2)}, u32[]{:S(2)}) collective-permute-start(bf16[8,64,640]{2,1,0:T(8,128)(2,1)} %get-tuple-element.14), channel_id=1, source_target_pairs={{0,1},{1,2},{2,3},{3,0},{4,5},{5,6},{6,7},{7,4},{8,9},{9,10},{10,1... | collective-permute-start | bytes 1966088 | tf_op jit(solution)/shard_map/ppermute | solution.py:41
  21.1 23.9 %collective-permute-start.1 = (bf16[8,64,640]{2,1,0:T(8,128)(2,1)}, bf16[8,64,640]{2,1,0:T(8,128)(2,1)}, u32[]{:S(2)}, u32[]{:S(2)}) collective-permute-start(bf16[8,64,640]{2,1,0:T(8,128)(2,1)} %get-tuple-element.15), channel_id=1, source_target_pairs={{0,3},{1,0},{2,1},{3,2},{4,7},{5,4},{6,5},{7,6},{8,11},{9,8},{10,9... | collective-permute-start | bytes 1966088 | tf_op jit(solution)/shard_map/ppermute | solution.py:41
  21.6 30.7 %collective-permute-start.17 = (bf16[8,64,640]{2,1,0:T(8,128)(2,1)}, bf16[8,64,640]{2,1,0:T(8,128)(2,1)}, u32[]{:S(2)}, u32[]{:S(2)}) collective-permute-start(bf16[8,64,640]{2,1,0:T(8,128)(2,1)} %get-tuple-element.17), channel_id=1, source_target_pairs={{0,2},{1,3},{2,0},{3,1},{4,6},{5,7},{6,4},{7,5},{8,10},{9,11},{10,... | collective-permute-start | bytes 1966088 | tf_op jit(solution)/shard_map/ppermute | solution.py:41
  23.7 16.6 %collective-permute-start.15 = (bf16[704,128]{1,0:T(8,128)(2,1)S(1)}, bf16[704,128]{1,0:T(8,128)(2,1)S(1)}, u32[]{:S(2)}, u32[]{:S(2)}) collective-permute-start(bf16[704,128]{1,0:T(8,128)(2,1)S(1)} %collective-permute-done.9.refs_11_.refs_9_), channel_id=1, source_target_pairs={{0,128},{16,144},{32,160},{48,176},{64,192},{80,208},{96,224},{112... | collective-permute-start | bytes 540680 | tf_op jit(solution)/shard_map/ppermute | solution.py:29
  29.4 11.0 %collective-permute-start.10 = (bf16[704,128]{1,0:T(8,128)(2,1)S(1)}, bf16[704,128]{1,0:T(8,128)(2,1)S(1)}, u32[]{:S(2)}, u32[]{:S(2)}) collective-permute-start(bf16[704,128]{1,0:T(8,128)(2,1)S(1)} %collective-permute-done.9.refs_11_.refs_9_), channel_id=1, source_target_pairs={{0,16},{16,0},{32,48},{48,32},{64,80},{80,64},{96,112},{112,96},{1... | collective-permute-start | bytes 540680 | tf_op jit(solution)/shard_map/ppermute | solution.py:37
  30.1 25.8 %all-to-all-start = ((bf16[16,80,128]{2,1,0:T(8,128)(2,1)}), bf16[16,80,128]{2,1,0:T(8,128)(2,1)S(1)}, u32[]{:S(2)}, u32[]{:S(2)}) async-start(bf16[16,80,128]{2,1,0:T(8,128)(2,1)} %pad_maximum_fusion.1), calls=%async_computation | async-start | bytes 655360 | tf_op jit(solution)/shard_map/all_to_all | solution.py:45
  40.3 1.5 %collective-permute-start.4 = (bf16[704,128]{1,0:T(8,128)(2,1)S(1)}, bf16[704,128]{1,0:T(8,128)(2,1)S(1)}, u32[]{:S(2)}, u32[]{:S(2)}) collective-permute-start(bf16[704,128]{1,0:T(8,128)(2,1)S(1)} %collective-permute-done.3.refs_5_.refs_3_), channel_id=1, source_target_pairs={{0,16},{16,0},{32,48},{48,32},{64,80},{80,64},{96,112},{112,96},{1... | collective-permute-start | bytes 540680 | tf_op jit(solution)/shard_map/ppermute | solution.py:37
  40.4 1.7 %collective-permute-start.6 = (bf16[704,128]{1,0:T(8,128)(2,1)S(1)}, bf16[704,128]{1,0:T(8,128)(2,1)S(1)}, u32[]{:S(2)}, u32[]{:S(2)}) collective-permute-start(bf16[704,128]{1,0:T(8,128)(2,1)S(1)} %collective-permute-done.5.refs_7_.refs_5_), channel_id=1, source_target_pairs={{0,16},{16,0},{32,48},{48,32},{64,80},{80,64},{96,112},{112,96},{1... | collective-permute-start | bytes 540680 | tf_op jit(solution)/shard_map/ppermute | solution.py:37
  41.8 1.4 %collective-permute-start.8 = (bf16[704,128]{1,0:T(8,128)(2,1)S(1)}, bf16[704,128]{1,0:T(8,128)(2,1)S(1)}, u32[]{:S(2)}, u32[]{:S(2)}) collective-permute-start(bf16[704,128]{1,0:T(8,128)(2,1)S(1)} %collective-permute-done.7.refs_9_.refs_7_), channel_id=1, source_target_pairs={{0,16},{16,0},{32,48},{48,32},{64,80},{80,64},{96,112},{112,96},{1... | collective-permute-start | bytes 540680 | tf_op jit(solution)/shard_map/ppermute | solution.py:37
  42.1 1.4 %collective-permute-start.12 = (bf16[704,128]{1,0:T(8,128)(2,1)S(1)}, bf16[704,128]{1,0:T(8,128)(2,1)S(1)}, u32[]{:S(2)}, u32[]{:S(2)}) collective-permute-start(bf16[704,128]{1,0:T(8,128)(2,1)S(1)} %collective-permute-done.11.refs_13_.refs_11_), channel_id=1, source_target_pairs={{0,16},{16,0},{32,48},{48,32},{64,80},{80,64},{96,112},{112,96},{1... | collective-permute-start | bytes 540680 | tf_op jit(solution)/shard_map/ppermute | solution.py:37
  43.2 1.4 %collective-permute-start.14 = (bf16[704,128]{1,0:T(8,128)(2,1)S(1)}, bf16[704,128]{1,0:T(8,128)(2,1)S(1)}, u32[]{:S(2)}, u32[]{:S(2)}) collective-permute-start(bf16[704,128]{1,0:T(8,128)(2,1)S(1)} %collective-permute-done.13.refs_15_.refs_13_), channel_id=1, source_target_pairs={{0,16},{16,0},{32,48},{48,32},{64,80},{80,64},{96,112},{112,96},{1... | collective-permute-start | bytes 540680 | tf_op jit(solution)/shard_map/ppermute | solution.py:37
  43.5 1.4 %collective-permute-start.16 = (bf16[704,128]{1,0:T(8,128)(2,1)S(1)}, bf16[704,128]{1,0:T(8,128)(2,1)S(1)}, u32[]{:S(2)}, u32[]{:S(2)}) collective-permute-start(bf16[704,128]{1,0:T(8,128)(2,1)S(1)} %collective-permute-done.15.refs_17_.refs_15_), channel_id=1, source_target_pairs={{0,16},{16,0},{32,48},{48,32},{64,80},{80,64},{96,112},{112,96},{1... | collective-permute-start | bytes 540680 | tf_op jit(solution)/shard_map/ppermute | solution.py:37
  44.9 0.8 copy-start.1
  52.3 11.6 %copy-start = (s32[2,16]{1,0:T(2,128)S(1)}, s32[2,16]{1,0:T(2,128)}, u32[]{:S(2)}) copy-start(s32[2,16]{1,0:T(2,128)} %kept_ref.3) | copy-start | bytes 388
  56.0 17.7 %all-to-all-start.1 = ((bf16[4,16,2048]{2,1,0:T(8,128)(2,1)}), bf16[4,16,2048]{2,1,0:T(8,128)(2,1)S(1)}, u32[]{:S(2)}, u32[]{:S(2)}) async-start(bf16[4,16,2048]{2,1,0:T(8,128)(2,1)} %bitcast.9), calls=%async_computation.1 | async-start | bytes 524288 | tf_op jit(solution)/shard_map/all_to_all | solution.py:45
  78.4 1.6 %collective-permute-start.18 = (bf16[8,128,128]{2,1,0:T(8,128)(2,1)S(1)}, bf16[8,128,128]{2,1,0:T(8,128)(2,1)S(1)}, u32[]{:S(2)}, u32[]{:S(2)}) collective-permute-start(bf16[8,128,128]{2,1,0:T(8,128)(2,1)S(1)} %get-tuple-element.21), channel_id=1, source_target_pairs={{0,16},{16,0},{32,48},{48,32},{64,80},{80,64},{96,112},{112,96},{1... | collective-permute-start | bytes 786440 | tf_op jit(solution)/shard_map/ppermute | solution.py:37

commit v5 on v4

--- a/solution.py
+++ b/solution.py
@@ -129,15 +129,16 @@
     row = lax.broadcasted_iota(jnp.int32, (depth - width, 512), 0)
     for n in range(4):
         keys[n, width:, :] = jnp.where(row < 3, 1.0, 0.0).astype(bf16)
-    for i, tile in enumerate(tiles):
-        keys[i // 4, 0:width, i % 4 * 128 : i % 4 * 128 + 128] = tile[128 : 128 + width, :]
-        for index_ref in index:
+    for index_ref in index:
+        for i, tile in enumerate(tiles):
             index_ref[i * 128 : i * 128 + 128, :] = tile[0:128, :]
     for a in range(groups):
         q_loads[a].wait()
         some = q_ref[a].reshape(heads * rows, depth)
         for n in range(4):
             at = n * 512
+            for i in range(4) if a == 0 else ():
+                keys[n, 0:width, i * 128 : i * 128 + 128] = tiles[4 * n + i][128 : 128 + width, :]
             s = jnp.dot(some, keys[n], preferred_element_type=f32)
             p = jnp.exp2(s * (attn_scale * LOG2E))
             total = acc[:, at : at + 512] if a else None
@@ -170,10 +171,25 @@
     )(*in_hbm(*queries), *tiles, *before)
 
 
-def weight_column(q_ref, j):
-    row = jnp.sum(q_ref[j, 64:80, :].astype(f32), axis=0, keepdims=True)[:, 0:64]
-    eye = lax.broadcasted_iota(jnp.int32, (64, 64), 0) == lax.broadcasted_iota(jnp.int32, (64, 64), 1)
-    return jnp.sum(jnp.where(eye, row, 0.0), axis=1, keepdims=True)
+def pack_body(q_ref, w_ref, out_ref):
+    value = w_ref[...]
+    p0 = value.astype(bf16).astype(f32)
+    p1 = (value - p0).astype(bf16).astype(f32)
+    p2 = value - p0 - p1
+    rows = jnp.concatenate([p0, p1, p2, jnp.zeros_like(p0)], axis=0).astype(bf16)
+    for j in range(16):
+        out_ref[j, 0:64, :] = q_ref[j]
+        out_ref[j, 64:80, :] = rows[:, j // 8 * 128 : j // 8 * 128 + 128]
+
+
+def weight_column(at_ref, q_ref, j):
+    block = lax.rem(at_ref[0] * 4 + at_ref[1], 8) * 16
+    rows = q_ref[j, 64:80, :].astype(f32)
+    rows = rows[0:4] + rows[4:8] + rows[8:12]
+    rows = jnp.concatenate([rows] * 16, axis=0)
+    lane = lax.broadcasted_iota(jnp.int32, (64, 128), 1)
+    query = lax.broadcasted_iota(jnp.int32, (64, 128), 0) // 4
+    return jnp.sum(jnp.where(lane == query + block, rows, 0.0), axis=1, keepdims=True)
 
 
 def slot_tile(at_ref, slot):
@@ -205,7 +221,7 @@
         z = lax.dot_general(rows, keys[...], NT, preferred_element_type=f32)
         part = None
         for a in range(4):
-            weight = weight_column(q_ref, 4 * g + a) * scale
+            weight = weight_column(at_ref, q_ref, 4 * g + a) * scale
             term = jnp.maximum(z[a * 64 : a * 64 + 64], 0.0) * weight
             part = term if part is None else part + term
         acc[...] += part
@@ -241,19 +257,17 @@
     grad = prob_ref[...] - head_sum / jnp.sum(head_sum, axis=1, keepdims=True)
     for t in range(16):
         wide[4 * t : 4 * t + 4, :] = jnp.broadcast_to(grad[t : t + 1], (4, 2048))
-    dk[...] = jnp.zeros_like(dk)
-
-    @pl.loop(0, 4)
-    def _(g):
-        rows = q_ref[pl.ds(4 * g, 4), 0:64, :].reshape(256, 128)
+    for g in range(4):
+        rows = q_ref[4 * g : 4 * g + 4, 0:64, :].reshape(256, 128)
         z = lax.dot_general(rows, keys[...], NT, preferred_element_type=f32)
         for a in range(4):
             at = a * 64
-            value = wide[...] * weight_column(q_ref, 4 * g + a)
-            dz[at : at + 64, :] = jnp.where(z[at : at + 64] > 0.0, value, 0.0).astype(bf16)
-        dk[...] += lax.dot_general(rows, dz[...], TN, preferred_element_type=f32)
-        dq = jnp.dot(dz[...], keys[...], preferred_element_type=f32) * scale
-        dq_ref[pl.ds(4 * g, 4)] = dq.astype(bf16).reshape(4, 64, 128)
+            value = wide[...] * weight_column(at_ref, q_ref, 4 * g + a)
+            dz[g % 2, at : at + 64, :] = jnp.where(z[at : at + 64] > 0.0, value, 0.0).astype(bf16)
+        part = lax.dot_general(rows, dz[g % 2], TN, preferred_element_type=f32)
+        dk[...] = part if g == 0 else dk[...] + part
+        dq = jnp.dot(dz[g % 2], keys[...], preferred_element_type=f32) * scale
+        dq_ref[4 * g : 4 * g + 4] = dq.astype(bf16).reshape(4, 64, 128)
 
     for slot in range(16):
         tile = dk[:, slot * 128 : slot * 128 + 128] * scale
@@ -281,7 +295,7 @@
         [SM, SM] + [VM] * 4,
         16,
         scratch_shapes=[
-            pltpu.VMEM((256, 2048), bf16),
+            pltpu.VMEM((2, 256, 2048), bf16),
             pltpu.VMEM((128, 2048), f32),
             pltpu.VMEM((64, 2048), f32),
         ],
@@ -304,12 +318,9 @@
             there = along_y(tile, -d) if d else tile
             tiles += [there, other_core(there)]
 
-    w0 = lax.reduce_precision(index_weight, 8, 7)
-    w1 = lax.reduce_precision(index_weight - w0, 8, 7)
-    w2 = index_weight - w0 - w1
-    weight = jnp.stack([w.reshape(16, 64) for w in (w0, w1, w2)], axis=1).astype(bf16)
-    weight = jnp.pad(weight, ((0, 0), (0, 13), (0, 64)))
-    queries = jnp.concatenate([index_query.reshape(16, 64, 128), weight], axis=1)
+    queries = call(
+        pack_body, pltpu.HBM((16, 80, 128), bf16), [VM, VM], 6, out_specs=VM, name="pack"
+    )(index_query.reshape(16, 64, 128), index_weight.T)
     queries = exchanged(queries, "head")
 
     parts = wide_queries(at, jnp.transpose(query_latent, (1, 2, 0)), normalizer.T)

time: 121 us -> 129 us (1.066)
  the two profiles are of different devices: /device:TPU:2 before, /device:TPU:32 now
where the time goes in v5:
time: 129 us; the launch traced here: 127 us
  starting transfers between devices  36 us (28%)
  blocking collectives  34.3 us (27%)
  waiting for transfers between devices  31.6 us (24%)
  Pallas kernels  22.9 us (18%)
    all_to_all x2, blocking collectives, exchanged(): lax.all_to_all(value, axis, 0, 0, tiled=True, axis_index_groups=groups)  34.3 us
    all_to_all x2, starting transfers between devices, exchanged(): lax.all_to_all(value, axis, 0, 0, tiled=True, axis_index_groups=groups)  19.5 us
    ppermute x3, waiting for transfers between devices, along_x(): lax.ppermute(value, 'head', [(i, i // 4 * 4 + (i + d) % 4) for i in range...  13.8 us
    pallas_call x2, Pallas kernels, scores(): call(functools.partial(score_body, groups, last), (sds((rows, 2048), bf16...  10.6 us
    ppermute x6, starting transfers between devices, along_y(): lax.ppermute(value, 'seq', [(i, (i + 4 * d) % 16) for i in range(16)])  7.56 us
    all_to_all x2, waiting for transfers between devices, exchanged(): lax.all_to_all(value, axis, 0, 0, tiled=True, axis_index_groups=groups)  6.3 us
    ppermute x6, waiting for transfers between devices, along_y(): lax.ppermute(value, 'seq', [(i, (i + 4 * d) % 16) for i in range(16)])  5.82 us
    ppermute x3, starting transfers between devices, along_x(): lax.ppermute(value, 'head', [(i, i // 4 * 4 + (i + d) % 4) for i in range...  5.63 us
  transfers between devices with their start and end apart: 21, of which 12 were waited for; matrix products, arithmetic and copies ran while one was open for 0% of the time, Pallas kernels for 14%

profile of v5, /device:TPU:32, one launch (start us, length us, event | category | flops | bytes accessed | tf_op | source)
XLA Modules:
  0.0 126.8 jit_solution(11362580820601686104)
XLA Ops:
  0.6 0.0 copy-start
  0.6 0.0 copy-start.1
  0.7 1.0 pad_maximum_fusion.1.refs_3_.refs_1_
  1.6 1.9 %collective-permute-start.9 = (bf16[704,128]{1,0:T(8,128)(2,1)S(1)}, bf16[704,128]{1,0:T(8,128)(2,1)S(1)}, u32[]{:S(2)}, u32[]{:S(2)}) collective-permute-start(bf16[704,128]{1,0:T(8,128)(2,1)S(1)} %pad_maximum_fusion.1.refs_3_.refs_1_), channel_id=1, source_target_pairs={{0,32},{16,48},{32,0},{48,16},{64,96},{80,112},{96,64},{112,80},{1... | collective-permute-start | bytes 540680 | tf_op jit(solution)/shard_map/ppermute | solution.py:33
  3.5 1.3 %collective-permute-start.3 = (bf16[704,128]{1,0:T(8,128)(2,1)S(1)}, bf16[704,128]{1,0:T(8,128)(2,1)S(1)}, u32[]{:S(2)}, u32[]{:S(2)}) collective-permute-start(bf16[704,128]{1,0:T(8,128)(2,1)S(1)} %pad_maximum_fusion.1.refs_3_.refs_1_), channel_id=1, source_target_pairs={{0,192},{16,208},{32,224},{48,240},{64,0},{80,16},{96,32},{112,48}... | collective-permute-start | bytes 540680 | tf_op jit(solution)/shard_map/ppermute | solution.py:29
  4.8 0.7 collective-permute-start.5
  5.5 1.5 %collective-permute-start.7 = (bf16[704,128]{1,0:T(8,128)(2,1)S(1)}, bf16[704,128]{1,0:T(8,128)(2,1)S(1)}, u32[]{:S(2)}, u32[]{:S(2)}) collective-permute-start(bf16[704,128]{1,0:T(8,128)(2,1)S(1)} %pad_maximum_fusion.1.refs_3_.refs_1_), channel_id=1, source_target_pairs={{0,128},{16,144},{32,160},{48,176},{64,192},{80,208},{96,224},{112... | collective-permute-start | bytes 540680 | tf_op jit(solution)/shard_map/ppermute | solution.py:29
  7.0 0.0 collective-permute-start.2
  7.0 1.0 collective-permute-done.9.refs_11_.refs_9_
  8.0 3.0 %collective-permute-start.11 = (bf16[704,128]{1,0:T(8,128)(2,1)S(1)}, bf16[704,128]{1,0:T(8,128)(2,1)S(1)}, u32[]{:S(2)}, u32[]{:S(2)}) collective-permute-start(bf16[704,128]{1,0:T(8,128)(2,1)S(1)} %collective-permute-done.9.refs_11_.refs_9_), channel_id=1, source_target_pairs={{0,192},{16,208},{32,224},{48,240},{64,0},{80,16},{96,32},{112,48}... | collective-permute-start | bytes 540680 | tf_op jit(solution)/shard_map/ppermute | solution.py:29
  11.0 1.2 collective-permute-done.3.refs_5_.refs_3_
  12.2 0.0 collective-permute-start.13
  12.2 4.6 %collective-permute-done.5.refs_7_.refs_5_ = bf16[704,128]{1,0:T(8,128)(2,1)S(1)} collective-permute-done((bf16[704,128]{1,0:T(8,128)(2,1)S(1)}, bf16[704,128]{1,0:T(8,128)(2,1)S(1)}, u32[]{:S(2)}, u32[]{:S(2)}) %collective-permute-start.5) | collective-permute-done | bytes 180256 | tf_op jit(solution)/shard_map/ppermute | solution.py:29
  16.8 1.0 collective-permute-start.15
  17.9 0.0 collective-permute-done.7.refs_9_.refs_7_
  17.9 0.0 collective-permute-start.10
  17.9 0.1 stack.23.at_ref
  17.9 3.8 %wide_queries.1 = (bf16[8,64,640]{2,1,0:T(8,128)(2,1)}, bf16[8,64,640]{2,1,0:T(8,128)(2,1)}, bf16[8,64,640]{2,1,0:T(8,128)(2,1)}, bf16[8,64,640]{2,1,0:T(8,128)(2,1)}) custom-call(s32[5]{0:T(128)S(1)} %stack.23.at_ref, bf16[8,576,256]{2,1,0:T(8,128)(2,1)} %bitcast.15, f32[8,256]{1,0:T(8,128)} %bitcast.18), custom_call_target="tpu_custom_call" | custom-call | tf_op jit(solution)/shard_map/wide_queries/pallas_call | solution.py:102
  21.7 0.0 collective-permute-done.2.refs_4_.refs_2_
  21.7 2.1 %collective-permute-start = (bf16[8,64,640]{2,1,0:T(8,128)(2,1)}, bf16[8,64,640]{2,1,0:T(8,128)(2,1)S(1)}, u32[]{:S(2)}, u32[]{:S(2)}) collective-permute-start(bf16[8,64,640]{2,1,0:T(8,128)(2,1)} %get-tuple-element.14), channel_id=1, source_target_pairs={{0,1},{1,2},{2,3},{3,0},{4,5},{5,6},{6,7},{7,4},{8,9},{9,10},{10,1... | collective-permute-start | bytes 1966088 | tf_op jit(solution)/shard_map/ppermute | solution.py:41
  23.8 0.0 collective-permute-done.11.refs_13_.refs_11_
  23.8 1.4 %collective-permute-start.1 = (bf16[8,64,640]{2,1,0:T(8,128)(2,1)}, bf16[8,64,640]{2,1,0:T(8,128)(2,1)}, u32[]{:S(2)}, u32[]{:S(2)}) collective-permute-start(bf16[8,64,640]{2,1,0:T(8,128)(2,1)} %get-tuple-element.15), channel_id=1, source_target_pairs={{0,3},{1,0},{2,1},{3,2},{4,7},{5,4},{6,5},{7,6},{8,11},{9,8},{10,9... | collective-permute-start | bytes 1966088 | tf_op jit(solution)/shard_map/ppermute | solution.py:41
  25.2 0.0 collective-permute-done.13.refs_15_.refs_13_
  25.2 2.2 %collective-permute-start.17 = (bf16[8,64,640]{2,1,0:T(8,128)(2,1)}, bf16[8,64,640]{2,1,0:T(8,128)(2,1)}, u32[]{:S(2)}, u32[]{:S(2)}) collective-permute-start(bf16[8,64,640]{2,1,0:T(8,128)(2,1)} %get-tuple-element.17), channel_id=1, source_target_pairs={{0,2},{1,3},{2,0},{3,1},{4,6},{5,7},{6,4},{7,5},{8,10},{9,11},{10,... | collective-permute-start | bytes 1966088 | tf_op jit(solution)/shard_map/ppermute | solution.py:41
  27.4 0.0 copy-done
  27.4 0.0 copy-done.1
  27.4 0.8 pack.1
  28.1 9.9 %all-to-all-start = ((bf16[16,80,128]{2,1,0:T(8,128)(2,1)}), bf16[16,80,128]{2,1,0:T(8,128)(2,1)S(1)}, u32[]{:S(2)}, u32[]{:S(2)}) async-start(bf16[16,80,128]{2,1,0:T(8,128)(2,1)} %pack.1), calls=%async_computation | async-start | bytes 655360 | tf_op jit(solution)/shard_map/all_to_all | solution.py:45
  38.1 0.0 collective-permute-done.15.refs_17_.refs_15_
  38.1 0.1 collective-permute-start.4
  38.2 0.0 collective-permute-done.10.refs_12_.refs_10_
  38.2 0.5 collective-permute-start.6
  38.7 0.9 collective-permute-done.4.refs_6_.refs_4_
  39.6 0.1 collective-permute-start.8
  39.7 0.1 collective-permute-done.6.refs_8_.refs_6_
  39.8 0.3 collective-permute-start.12
  40.1 0.9 collective-permute-done.8.refs_10_.refs_8_
  41.0 0.1 collective-permute-start.14
  41.1 0.1 collective-permute-done.12.refs_14_.refs_12_
  41.3 0.3 collective-permute-start.16
  41.5 0.9 collective-permute-done.14.refs_16_.refs_14_
  42.4 0.3 collective-permute-done.16.refs_18_.refs_16_
  42.7 0.0 collective-permute-done.refs_1_
  42.7 0.0 copy-start.3
  42.7 13.8 %collective-permute-done.1.refs_2_ = bf16[8,64,640]{2,1,0:T(8,128)(2,1)} collective-permute-done((bf16[8,64,640]{2,1,0:T(8,128)(2,1)}, bf16[8,64,640]{2,1,0:T(8,128)(2,1)}, u32[]{:S(2)}, u32[]{:S(2)}) %collective-permute-start.1) | collective-permute-done | bytes 655392 | tf_op jit(solution)/shard_map/ppermute | solution.py:41
  56.5 0.0 copy-done.3
  56.5 6.8 %scores.2 = (f32[64,2048]{1,0:T(8,128)S(1)}, bf16[2048,128]{1,0:T(8,128)(2,1)S(1)}) custom-call(bf16[8,64,640]{2,1,0:T(8,128)(2,1)} %get-tuple-element.13.refs_0_, bf16[8,64,640]{2,1,0:T(8,128)(2,1)} %copy-done.3, bf16[8,64,640]{2,1,0:T(8,128)(2,1)} %collective-permute-done.1.refs_2_, bf16[704,128]{1,0:T(8,128)(2,1)S(1)} %pad_maximum_fusion.1.refs_3_.refs_1_, ...), custom_call_target="tpu_custom_call" | custom-call | tf_op jit(solution)/shard_map/scores/pallas_call | solution.py:159
  63.2 0.0 collective-permute-done.17.refs_0_
  63.2 0.0 copy-start.2
  63.2 3.8 %scores.3 = bf16[64,2048]{1,0:T(8,128)(2,1)} custom-call(bf16[8,64,640]{2,1,0:T(8,128)(2,1)} %collective-permute-done.17.refs_0_, bf16[704,128]{1,0:T(8,128)(2,1)S(1)} %pad_maximum_fusion.1.refs_3_.refs_1_, bf16[704,128]{1,0:T(8,128)(2,1)S(1)} %collective-permute-done.2.refs_4_.refs_2_, bf16[704,128]{1,0:T(8,128)(2,1)S(1)} %collective-permute-done.3.refs_5_.refs_3_, ...), custom_call_target="tpu_custom_call" | custom-call | tf_op jit(solution)/shard_map/scores/pallas_call | solution.py:159
  67.1 0.0 all-to-all-done.q_ref
  67.1 9.5 %all-to-all-start.1 = ((bf16[4,16,2048]{2,1,0:T(8,128)(2,1)}), bf16[4,16,2048]{2,1,0:T(8,128)(2,1)S(1)}, u32[]{:S(2)}, u32[]{:S(2)}) async-start(bf16[4,16,2048]{2,1,0:T(8,128)(2,1)} %bitcast.10), calls=%async_computation.1 | async-start | bytes 524288 | tf_op jit(solution)/shard_map/all_to_all | solution.py:45
  76.6 0.0 copy-done.2
  76.7 3.0 %index_forward.1.prob_ref = f32[16,2048]{1,0:T(8,128)S(1)} custom-call(s32[5]{0:T(128)S(1)} %stack.23.at_ref, s32[2,16]{1,0:T(2,128)S(1)} %copy-done.2, bf16[16,80,128]{2,1,0:T(8,128)(2,1)S(1)} %all-to-all-done.q_ref, bf16[2048,128]{1,0:T(8,128)(2,1)S(1)} %get-tuple-element.16.keys), custom_call_target="tpu_custom_call" | custom-call | tf_op jit(solution)/shard_map/index_forward/pallas_call | solution.py:241
  79.6 6.3 %all-to-all-done.1.sums = bf16[4,16,2048]{2,1,0:T(8,128)(2,1)S(1)} async-done(((bf16[4,16,2048]{2,1,0:T(8,128)(2,1)}), bf16[4,16,2048]{2,1,0:T(8,128)(2,1)S(1)}, u32[]{:S(2)}, u32[]{:S(2)}) %all-to-all-start.1) | async-done | bytes 262176 | tf_op jit(solution)/shard_map/all_to_all | solution.py:45
  85.9 3.9 %index_backward.1 = (f32[8,128,128]{2,1,0:T(8,128)S(1)}, bf16[8,128,128]{2,1,0:T(8,128)(2,1)S(1)}, bf16[16,64,128]{2,1,0:T(8,128)(2,1)S(1)}) custom-call(s32[5]{0:T(128)S(1)} %stack.23.at_ref, s32[2,16]{1,0:T(2,128)S(1)} %copy-done.2, f32[16,2048]{1,0:T(8,128)S(1)} %index_forward.1.prob_ref, bf16[16,80,128]{2,1,0:T(8,128)(2,1)S(1)} %all-to-all-done.q_ref, ...), custom_call_target="tpu_custom_call" | custom-call | tf_op jit(solution)/shard_map/index_backward/pallas_call | solution.py:292
  89.8 0.1 collective-permute-start.18
  90.0 1.5 %collective-permute-done.18 = bf16[8,128,128]{2,1,0:T(8,128)(2,1)S(1)} collective-permute-done((bf16[8,128,128]{2,1,0:T(8,128)(2,1)S(1)}, bf16[8,128,128]{2,1,0:T(8,128)(2,1)S(1)}, u32[]{:S(2)}, u32[]{:S(2)}) %collective-permute-start.18) | collective-permute-done | bytes 262176 | tf_op jit(solution)/shard_map/ppermute | solution.py:37
  91.5 0.1 add_convert_fusion
  91.5 17.9 %all_to_all.20 = bf16[32,32,128]{2,1,0:T(8,128)(2,1)S(1)} all-to-all(bf16[32,32,128]{2,1,0:T(8,128)(2,1)S(1)} %bitcast.16), channel_id=1, replica_groups={{0,1,2,3,32,33,34,35,64,65,66,67,96,97,98,99,128,129,130,131,160,161,16..., dimensions={0} | all-to-all | bytes 524288 | tf_op jit(solution)/shard_map/all_to_all | solution.py:45
  109.4 0.1 reduce_sum.12
  109.5 16.4 %all_to_all.21.both_ref = bf16[16,96,128]{2,1,0:T(8,128)(2,1)S(1)} all-to-all(bf16[16,96,128]{2,1,0:T(8,128)(2,1)S(1)} %pad_maximum_fusion), channel_id=1, replica_groups=mesh['seq'=16,'head'=16] {'head'}, dimensions={0} | all-to-all | bytes 786432 | tf_op jit(solution)/shard_map/all_to_all | solution.py:45
  125.9 0.9 last.1
  (2 shorter events, 0.0 us)
Async XLA Ops:
  0.6 26.7 %copy-start = (bf16[256,4,128]{2,1,0:T(4,128)(2,1)S(1)}, bf16[256,4,128]{2,1,0:T(4,128)(2,1)}, u32[]{:S(2)}) copy-start(bf16[256,4,128]{2,1,0:T(4,128)(2,1)} %param.10) | copy-start | bytes 786436
  0.6 26.7 %copy-start.1 = (f32[256,4]{0,1:T(4,128)S(1)}, f32[256,4]{0,1:T(4,128)}, u32[]{:S(2)}) copy-start(f32[256,4]{0,1:T(4,128)} %param.12) | copy-start | bytes 12292
  1.6 6.4 %collective-permute-start.9 = (bf16[704,128]{1,0:T(8,128)(2,1)S(1)}, bf16[704,128]{1,0:T(8,128)(2,1)S(1)}, u32[]{:S(2)}, u32[]{:S(2)}) collective-permute-start(bf16[704,128]{1,0:T(8,128)(2,1)S(1)} %pad_maximum_fusion.1.refs_3_.refs_1_), channel_id=1, source_target_pairs={{0,32},{16,48},{32,0},{48,16},{64,96},{80,112},{96,64},{112,80},{1... | collective-permute-start | bytes 540680 | tf_op jit(solution)/shard_map/ppermute | solution.py:33
  3.5 8.7 %collective-permute-start.3 = (bf16[704,128]{1,0:T(8,128)(2,1)S(1)}, bf16[704,128]{1,0:T(8,128)(2,1)S(1)}, u32[]{:S(2)}, u32[]{:S(2)}) collective-permute-start(bf16[704,128]{1,0:T(8,128)(2,1)S(1)} %pad_maximum_fusion.1.refs_3_.refs_1_), channel_id=1, source_target_pairs={{0,192},{16,208},{32,224},{48,240},{64,0},{80,16},{96,32},{112,48}... | collective-permute-start | bytes 540680 | tf_op jit(solution)/shard_map/ppermute | solution.py:29
  4.8 12.0 %collective-permute-start.5 = (bf16[704,128]{1,0:T(8,128)(2,1)S(1)}, bf16[704,128]{1,0:T(8,128)(2,1)S(1)}, u32[]{:S(2)}, u32[]{:S(2)}) collective-permute-start(bf16[704,128]{1,0:T(8,128)(2,1)S(1)} %pad_maximum_fusion.1.refs_3_.refs_1_), channel_id=1, source_target_pairs={{0,64},{16,80},{32,96},{48,112},{64,128},{80,144},{96,160},{112,17... | collective-permute-start | bytes 540680 | tf_op jit(solution)/shard_map/ppermute | solution.py:29
  5.5 12.3 %collective-permute-start.7 = (bf16[704,128]{1,0:T(8,128)(2,1)S(1)}, bf16[704,128]{1,0:T(8,128)(2,1)S(1)}, u32[]{:S(2)}, u32[]{:S(2)}) collective-permute-start(bf16[704,128]{1,0:T(8,128)(2,1)S(1)} %pad_maximum_fusion.1.refs_3_.refs_1_), channel_id=1, source_target_pairs={{0,128},{16,144},{32,160},{48,176},{64,192},{80,208},{96,224},{112... | collective-permute-start | bytes 540680 | tf_op jit(solution)/shard_map/ppermute | solution.py:29
  7.0 14.7 %collective-permute-start.2 = (bf16[704,128]{1,0:T(8,128)(2,1)S(1)}, bf16[704,128]{1,0:T(8,128)(2,1)S(1)}, u32[]{:S(2)}, u32[]{:S(2)}) collective-permute-start(bf16[704,128]{1,0:T(8,128)(2,1)S(1)} %pad_maximum_fusion.1.refs_3_.refs_1_), channel_id=1, source_target_pairs={{0,16},{16,0},{32,48},{48,32},{64,80},{80,64},{96,112},{112,96},{1... | collective-permute-start | bytes 540680 | tf_op jit(solution)/shard_map/ppermute | solution.py:37
  8.0 15.8 %collective-permute-start.11 = (bf16[704,128]{1,0:T(8,128)(2,1)S(1)}, bf16[704,128]{1,0:T(8,128)(2,1)S(1)}, u32[]{:S(2)}, u32[]{:S(2)}) collective-permute-start(bf16[704,128]{1,0:T(8,128)(2,1)S(1)} %collective-permute-done.9.refs_11_.refs_9_), channel_id=1, source_target_pairs={{0,192},{16,208},{32,224},{48,240},{64,0},{80,16},{96,32},{112,48}... | collective-permute-start | bytes 540680 | tf_op jit(solution)/shard_map/ppermute | solution.py:29
  12.2 13.0 %collective-permute-start.13 = (bf16[704,128]{1,0:T(8,128)(2,1)S(1)}, bf16[704,128]{1,0:T(8,128)(2,1)S(1)}, u32[]{:S(2)}, u32[]{:S(2)}) collective-permute-start(bf16[704,128]{1,0:T(8,128)(2,1)S(1)} %collective-permute-done.9.refs_11_.refs_9_), channel_id=1, source_target_pairs={{0,64},{16,80},{32,96},{48,112},{64,128},{80,144},{96,160},{112,17... | collective-permute-start | bytes 540680 | tf_op jit(solution)/shard_map/ppermute | solution.py:29
  16.8 21.2 %collective-permute-start.15 = (bf16[704,128]{1,0:T(8,128)(2,1)S(1)}, bf16[704,128]{1,0:T(8,128)(2,1)S(1)}, u32[]{:S(2)}, u32[]{:S(2)}) collective-permute-start(bf16[704,128]{1,0:T(8,128)(2,1)S(1)} %collective-permute-done.9.refs_11_.refs_9_), channel_id=1, source_target_pairs={{0,128},{16,144},{32,160},{48,176},{64,192},{80,208},{96,224},{112... | collective-permute-start | bytes 540680 | tf_op jit(solution)/shard_map/ppermute | solution.py:29
  17.9 20.3 %collective-permute-start.10 = (bf16[704,128]{1,0:T(8,128)(2,1)S(1)}, bf16[704,128]{1,0:T(8,128)(2,1)S(1)}, u32[]{:S(2)}, u32[]{:S(2)}) collective-permute-start(bf16[704,128]{1,0:T(8,128)(2,1)S(1)} %collective-permute-done.9.refs_11_.refs_9_), channel_id=1, source_target_pairs={{0,16},{16,0},{32,48},{48,32},{64,80},{80,64},{96,112},{112,96},{1... | collective-permute-start | bytes 540680 | tf_op jit(solution)/shard_map/ppermute | solution.py:37
  21.7 20.9 %collective-permute-start = (bf16[8,64,640]{2,1,0:T(8,128)(2,1)}, bf16[8,64,640]{2,1,0:T(8,128)(2,1)S(1)}, u32[]{:S(2)}, u32[]{:S(2)}) collective-permute-start(bf16[8,64,640]{2,1,0:T(8,128)(2,1)} %get-tuple-element.14), channel_id=1, source_target_pairs={{0,1},{1,2},{2,3},{3,0},{4,5},{5,6},{6,7},{7,4},{8,9},{9,10},{10,1... | collective-permute-start | bytes 1966088 | tf_op jit(solution)/shard_map/ppermute | solution.py:41
  23.8 32.6 %collective-permute-start.1 = (bf16[8,64,640]{2,1,0:T(8,128)(2,1)}, bf16[8,64,640]{2,1,0:T(8,128)(2,1)}, u32[]{:S(2)}, u32[]{:S(2)}) collective-permute-start(bf16[8,64,640]{2,1,0:T(8,128)(2,1)} %get-tuple-element.15), channel_id=1, source_target_pairs={{0,3},{1,0},{2,1},{3,2},{4,7},{5,4},{6,5},{7,6},{8,11},{9,8},{10,9... | collective-permute-start | bytes 1966088 | tf_op jit(solution)/shard_map/ppermute | solution.py:41
  25.2 38.0 %collective-permute-start.17 = (bf16[8,64,640]{2,1,0:T(8,128)(2,1)}, bf16[8,64,640]{2,1,0:T(8,128)(2,1)}, u32[]{:S(2)}, u32[]{:S(2)}) collective-permute-start(bf16[8,64,640]{2,1,0:T(8,128)(2,1)} %get-tuple-element.17), channel_id=1, source_target_pairs={{0,2},{1,3},{2,0},{3,1},{4,6},{5,7},{6,4},{7,5},{8,10},{9,11},{10,... | collective-permute-start | bytes 1966088 | tf_op jit(solution)/shard_map/ppermute | solution.py:41
  28.1 39.0 %all-to-all-start = ((bf16[16,80,128]{2,1,0:T(8,128)(2,1)}), bf16[16,80,128]{2,1,0:T(8,128)(2,1)S(1)}, u32[]{:S(2)}, u32[]{:S(2)}) async-start(bf16[16,80,128]{2,1,0:T(8,128)(2,1)} %pack.1), calls=%async_computation | async-start | bytes 655360 | tf_op jit(solution)/shard_map/all_to_all | solution.py:45
  38.1 1.5 %collective-permute-start.4 = (bf16[704,128]{1,0:T(8,128)(2,1)S(1)}, bf16[704,128]{1,0:T(8,128)(2,1)S(1)}, u32[]{:S(2)}, u32[]{:S(2)}) collective-permute-start(bf16[704,128]{1,0:T(8,128)(2,1)S(1)} %collective-permute-done.3.refs_5_.refs_3_), channel_id=1, source_target_pairs={{0,16},{16,0},{32,48},{48,32},{64,80},{80,64},{96,112},{112,96},{1... | collective-permute-start | bytes 540680 | tf_op jit(solution)/shard_map/ppermute | solution.py:37
  38.2 1.7 %collective-permute-start.6 = (bf16[704,128]{1,0:T(8,128)(2,1)S(1)}, bf16[704,128]{1,0:T(8,128)(2,1)S(1)}, u32[]{:S(2)}, u32[]{:S(2)}) collective-permute-start(bf16[704,128]{1,0:T(8,128)(2,1)S(1)} %collective-permute-done.5.refs_7_.refs_5_), channel_id=1, source_target_pairs={{0,16},{16,0},{32,48},{48,32},{64,80},{80,64},{96,112},{112,96},{1... | collective-permute-start | bytes 540680 | tf_op jit(solution)/shard_map/ppermute | solution.py:37
  39.6 1.4 %collective-permute-start.8 = (bf16[704,128]{1,0:T(8,128)(2,1)S(1)}, bf16[704,128]{1,0:T(8,128)(2,1)S(1)}, u32[]{:S(2)}, u32[]{:S(2)}) collective-permute-start(bf16[704,128]{1,0:T(8,128)(2,1)S(1)} %collective-permute-done.7.refs_9_.refs_7_), channel_id=1, source_target_pairs={{0,16},{16,0},{32,48},{48,32},{64,80},{80,64},{96,112},{112,96},{1... | collective-permute-start | bytes 540680 | tf_op jit(solution)/shard_map/ppermute | solution.py:37
  39.8 1.4 %collective-permute-start.12 = (bf16[704,128]{1,0:T(8,128)(2,1)S(1)}, bf16[704,128]{1,0:T(8,128)(2,1)S(1)}, u32[]{:S(2)}, u32[]{:S(2)}) collective-permute-start(bf16[704,128]{1,0:T(8,128)(2,1)S(1)} %collective-permute-done.11.refs_13_.refs_11_), channel_id=1, source_target_pairs={{0,16},{16,0},{32,48},{48,32},{64,80},{80,64},{96,112},{112,96},{1... | collective-permute-start | bytes 540680 | tf_op jit(solution)/shard_map/ppermute | solution.py:37
  41.0 1.4 %collective-permute-start.14 = (bf16[704,128]{1,0:T(8,128)(2,1)S(1)}, bf16[704,128]{1,0:T(8,128)(2,1)S(1)}, u32[]{:S(2)}, u32[]{:S(2)}) collective-permute-start(bf16[704,128]{1,0:T(8,128)(2,1)S(1)} %collective-permute-done.13.refs_15_.refs_13_), channel_id=1, source_target_pairs={{0,16},{16,0},{32,48},{48,32},{64,80},{80,64},{96,112},{112,96},{1... | collective-permute-start | bytes 540680 | tf_op jit(solution)/shard_map/ppermute | solution.py:37
  41.3 1.4 %collective-permute-start.16 = (bf16[704,128]{1,0:T(8,128)(2,1)S(1)}, bf16[704,128]{1,0:T(8,128)(2,1)S(1)}, u32[]{:S(2)}, u32[]{:S(2)}) collective-permute-start(bf16[704,128]{1,0:T(8,128)(2,1)S(1)} %collective-permute-done.15.refs_17_.refs_15_), channel_id=1, source_target_pairs={{0,16},{16,0},{32,48},{48,32},{64,80},{80,64},{96,112},{112,96},{1... | collective-permute-start | bytes 540680 | tf_op jit(solution)/shard_map/ppermute | solution.py:37
  42.7 13.8 %copy-start.3 = (bf16[8,64,640]{2,1,0:T(8,128)(2,1)}, bf16[8,64,640]{2,1,0:T(8,128)(2,1)S(1)}, u32[]{:S(2)}) copy-start(bf16[8,64,640]{2,1,0:T(8,128)(2,1)S(1)} %collective-permute-done.refs_1_) | copy-start | bytes 1966084
  63.2 13.4 %copy-start.2 = (s32[2,16]{1,0:T(2,128)S(1)}, s32[2,16]{1,0:T(2,128)}, u32[]{:S(2)}) copy-start(s32[2,16]{1,0:T(2,128)} %kept_ref.3) | copy-start | bytes 388
  67.1 18.8 %all-to-all-start.1 = ((bf16[4,16,2048]{2,1,0:T(8,128)(2,1)}), bf16[4,16,2048]{2,1,0:T(8,128)(2,1)S(1)}, u32[]{:S(2)}, u32[]{:S(2)}) async-start(bf16[4,16,2048]{2,1,0:T(8,128)(2,1)} %bitcast.10), calls=%async_computation.1 | async-start | bytes 524288 | tf_op jit(solution)/shard_map/all_to_all | solution.py:45
  89.8 1.6 %collective-permute-start.18 = (bf16[8,128,128]{2,1,0:T(8,128)(2,1)S(1)}, bf16[8,128,128]{2,1,0:T(8,128)(2,1)S(1)}, u32[]{:S(2)}, u32[]{:S(2)}) collective-permute-start(bf16[8,128,128]{2,1,0:T(8,128)(2,1)S(1)} %get-tuple-element.21), channel_id=1, source_target_pairs={{0,16},{16,0},{32,48},{48,32},{64,80},{80,64},{96,112},{112,96},{1... | collective-permute-start | bytes 786440 | tf_op jit(solution)/shard_map/ppermute | solution.py:37

commit v6 on v5

--- a/solution.py
+++ b/solution.py
@@ -18,11 +18,7 @@
 HB = pl.BlockSpec(memory_space=pltpu.HBM)
 
 ROW_ZH = [[zh * 4 + x for zh in range(4)] for x in range(4)]
-YZX = [
-    [(y * 4 + z * 2 + c) * 16 + zh * 4 + x for y in range(4) for z in range(2) for x in range(4)]
-    for zh in range(4)
-    for c in range(2)
-]
+SAME_ZH = [[seq * 16 + zh * 4 + x for seq in range(16) for x in range(4)] for zh in range(4)]
 
 
 def along_y(value, d):
@@ -249,7 +245,7 @@
 
 
 def back_body(scale, at_ref, kept_ref, prob_ref, q_ref, keys, sums, *refs):
-    own_ref, send_ref, dq_ref, dz, dk, wide = refs
+    dk_ref, dq_ref, dz, dk, wide = refs
     total = sums[0].astype(f32)
     for j in range(1, sums.shape[0]):
         total += sums[j].astype(f32)
@@ -271,11 +267,7 @@
 
     for slot in range(16):
         tile = dk[:, slot * 128 : slot * 128 + 128] * scale
-        place = lax.div(slot_tile(at_ref, slot), 2)
-        if slot % 2 == 0:
-            own_ref[place] = tile
-        else:
-            send_ref[place] = tile.astype(bf16)
+        dk_ref[slot_tile(at_ref, slot)] = tile.astype(bf16)
 
 
 def last_body(both_ref, dq_ref, dk_ref):
@@ -291,7 +283,7 @@
 def index_backward(at, kept, prob, queries, keys, sums, scale):
     return call(
         functools.partial(back_body, scale),
-        (sds((8, 128, 128), f32), sds((8, 128, 128), bf16), sds((16, 64, 128), bf16)),
+        (sds((16, 128, 128), bf16), sds((16, 64, 128), bf16)),
         [SM, SM] + [VM] * 4,
         16,
         scratch_shapes=[
@@ -327,16 +319,14 @@
     query = [parts[0]]
     for part, d in zip(parts[1:], STEPS):
         query.append(along_x(part, d))
-    part, index_keys = scores(query[:3], tiles)
-    (part,) = scores(query[3:], tiles, part)
+    part, index_keys = scores(query[:1], tiles)
+    (part,) = scores(query[1:], tiles, part)
     sums = exchanged(part.reshape(4, 16, 2048), "head", ROW_ZH)
 
     prob = index_forward(at, kept, queries, index_keys, index_scale)
-    own, send, dq = index_backward(at, kept, prob, queries, index_keys, sums, index_scale)
-
-    got = other_core(send)
-    dkey = (own + got.astype(f32)).astype(bf16)
-    dkey = exchanged(dkey.reshape(32, 32, 128), ("seq", "head"), YZX)
+    dkey, dq = index_backward(at, kept, prob, queries, index_keys, sums, index_scale)
+
+    dkey = exchanged(dkey.reshape(64, 32, 128), ("seq", "head"), SAME_ZH)
     dkey = jnp.sum(dkey.astype(f32), axis=0).astype(bf16)
     dkey = jnp.broadcast_to(dkey, (16, 32, 128))
     both = exchanged(jnp.concatenate([dq, dkey], axis=1), "head")

time: 129 us -> 129 us (level); the launches traced: 127 us -> 128 us
  blocking collectives: 34.3 us -> 37.8 us
    all_to_all x2, blocking collectives: 34.3 us -> 37.8 us  [exchanged(): lax.all_to_all(value, axis, 0, 0, tiled=True, axis_index_groups=groups)]
    ppermute x9 -> x8, waiting for transfers between devices: 4.73 us -> 3.2 us  [other_core(): return lax.ppermute(value, 'seq', [(i, i ^ 1) for i in range(16)])]
  transfers between devices with their start and end apart: 21 -> 20, of which waited for: 12 -> 12; matrix products, arithmetic and copies ran while one was open for 0% -> 0% of each run, Pallas kernels for 14% -> 14%
where the time goes in v6:
time: 129 us; the launch traced here: 128 us
  blocking collectives  37.8 us (29%)
  starting transfers between devices  34.8 us (27%)
  waiting for transfers between devices  30.6 us (24%)
  Pallas kernels  22.9 us (18%)
    all_to_all x2, blocking collectives, exchanged(): lax.all_to_all(value, axis, 0, 0, tiled=True, axis_index_groups=groups)  37.8 us
    all_to_all x2, starting transfers between devices, exchanged(): lax.all_to_all(value, axis, 0, 0, tiled=True, axis_index_groups=groups)  18.4 us
    ppermute x3, waiting for transfers between devices, along_x(): lax.ppermute(value, 'head', [(i, i // 4 * 4 + (i + d) % 4) for i in range...  13.5 us
    pallas_call x2, Pallas kernels, scores(): call(functools.partial(score_body, groups, last), (sds((rows, 2048), bf16...  10.6 us
    ppermute x6, starting transfers between devices, along_y(): lax.ppermute(value, 'seq', [(i, (i + 4 * d) % 16) for i in range(16)])  7.56 us
    all_to_all x2, waiting for transfers between devices, exchanged(): lax.all_to_all(value, axis, 0, 0, tiled=True, axis_index_groups=groups)  7.19 us
    ppermute x6, waiting for transfers between devices, along_y(): lax.ppermute(value, 'seq', [(i, (i + 4 * d) % 16) for i in range(16)])  5.82 us
    ppermute x3, starting transfers between devices, along_x(): lax.ppermute(value, 'head', [(i, i // 4 * 4 + (i + d) % 4) for i in range...  5.63 us
  transfers between devices with their start and end apart: 20, of which 12 were waited for; matrix products, arithmetic and copies ran while one was open for 0% of the time, Pallas kernels for 14%

profile of v6, /device:TPU:32, one launch (start us, length us, event | category | flops | bytes accessed | tf_op | source)
XLA Modules:
  0.0 128.2 jit_solution(11216463586687855149)
XLA Ops:
  0.6 0.0 copy-start
  0.6 0.0 copy-start.1
  0.7 1.0 pad_maximum_fusion.1.refs_1_.refs_3_
  1.6 1.9 %collective-permute-start.7 = (bf16[704,128]{1,0:T(8,128)(2,1)S(1)}, bf16[704,128]{1,0:T(8,128)(2,1)S(1)}, u32[]{:S(2)}, u32[]{:S(2)}) collective-permute-start(bf16[704,128]{1,0:T(8,128)(2,1)S(1)} %pad_maximum_fusion.1.refs_1_.refs_3_), channel_id=1, source_target_pairs={{0,32},{16,48},{32,0},{48,16},{64,96},{80,112},{96,64},{112,80},{1... | collective-permute-start | bytes 540680 | tf_op jit(solution)/shard_map/ppermute | solution.py:29
  3.5 1.3 %collective-permute-start.1 = (bf16[704,128]{1,0:T(8,128)(2,1)S(1)}, bf16[704,128]{1,0:T(8,128)(2,1)S(1)}, u32[]{:S(2)}, u32[]{:S(2)}) collective-permute-start(bf16[704,128]{1,0:T(8,128)(2,1)S(1)} %pad_maximum_fusion.1.refs_1_.refs_3_), channel_id=1, source_target_pairs={{0,192},{16,208},{32,224},{48,240},{64,0},{80,16},{96,32},{112,48}... | collective-permute-start | bytes 540680 | tf_op jit(solution)/shard_map/ppermute | solution.py:25
  4.8 0.7 collective-permute-start.3
  5.5 1.5 %collective-permute-start.5 = (bf16[704,128]{1,0:T(8,128)(2,1)S(1)}, bf16[704,128]{1,0:T(8,128)(2,1)S(1)}, u32[]{:S(2)}, u32[]{:S(2)}) collective-permute-start(bf16[704,128]{1,0:T(8,128)(2,1)S(1)} %pad_maximum_fusion.1.refs_1_.refs_3_), channel_id=1, source_target_pairs={{0,128},{16,144},{32,160},{48,176},{64,192},{80,208},{96,224},{112... | collective-permute-start | bytes 540680 | tf_op jit(solution)/shard_map/ppermute | solution.py:25
  7.0 0.0 collective-permute-start
  7.0 1.0 collective-permute-done.7.refs_9_.refs_11_
  8.0 3.0 %collective-permute-start.9 = (bf16[704,128]{1,0:T(8,128)(2,1)S(1)}, bf16[704,128]{1,0:T(8,128)(2,1)S(1)}, u32[]{:S(2)}, u32[]{:S(2)}) collective-permute-start(bf16[704,128]{1,0:T(8,128)(2,1)S(1)} %collective-permute-done.7.refs_9_.refs_11_), channel_id=1, source_target_pairs={{0,192},{16,208},{32,224},{48,240},{64,0},{80,16},{96,32},{112,48}... | collective-permute-start | bytes 540680 | tf_op jit(solution)/shard_map/ppermute | solution.py:25
  11.0 1.2 collective-permute-done.1.refs_3_.refs_5_
  12.2 0.0 collective-permute-start.11
  12.2 4.6 %collective-permute-done.3.refs_5_.refs_7_ = bf16[704,128]{1,0:T(8,128)(2,1)S(1)} collective-permute-done((bf16[704,128]{1,0:T(8,128)(2,1)S(1)}, bf16[704,128]{1,0:T(8,128)(2,1)S(1)}, u32[]{:S(2)}, u32[]{:S(2)}) %collective-permute-start.3) | collective-permute-done | bytes 180256 | tf_op jit(solution)/shard_map/ppermute | solution.py:25
  16.8 1.0 collective-permute-start.13
  17.9 0.0 collective-permute-done.5.refs_7_.refs_9_
  17.9 0.0 collective-permute-start.8
  17.9 0.1 stack.23.at_ref
  17.9 3.7 %wide_queries.1 = (bf16[8,64,640]{2,1,0:T(8,128)(2,1)}, bf16[8,64,640]{2,1,0:T(8,128)(2,1)}, bf16[8,64,640]{2,1,0:T(8,128)(2,1)}, bf16[8,64,640]{2,1,0:T(8,128)(2,1)}) custom-call(s32[5]{0:T(128)S(1)} %stack.23.at_ref, bf16[8,576,256]{2,1,0:T(8,128)(2,1)} %bitcast.16, f32[8,256]{1,0:T(8,128)} %bitcast.18), custom_call_target="tpu_custom_call" | custom-call | tf_op jit(solution)/shard_map/wide_queries/pallas_call | solution.py:98
  21.7 0.0 collective-permute-done.refs_2_.refs_4_
  21.7 2.1 %collective-permute-start.15 = (bf16[8,64,640]{2,1,0:T(8,128)(2,1)}, bf16[8,64,640]{2,1,0:T(8,128)(2,1)}, u32[]{:S(2)}, u32[]{:S(2)}) collective-permute-start(bf16[8,64,640]{2,1,0:T(8,128)(2,1)} %get-tuple-element.14), channel_id=1, source_target_pairs={{0,1},{1,2},{2,3},{3,0},{4,5},{5,6},{6,7},{7,4},{8,9},{9,10},{10,1... | collective-permute-start | bytes 1966088 | tf_op jit(solution)/shard_map/ppermute | solution.py:37
  23.8 0.0 collective-permute-done.9.refs_11_.refs_13_
  23.8 1.4 %collective-permute-start.16 = (bf16[8,64,640]{2,1,0:T(8,128)(2,1)}, bf16[8,64,640]{2,1,0:T(8,128)(2,1)}, u32[]{:S(2)}, u32[]{:S(2)}) collective-permute-start(bf16[8,64,640]{2,1,0:T(8,128)(2,1)} %get-tuple-element.15), channel_id=1, source_target_pairs={{0,3},{1,0},{2,1},{3,2},{4,7},{5,4},{6,5},{7,6},{8,11},{9,8},{10,9... | collective-permute-start | bytes 1966088 | tf_op jit(solution)/shard_map/ppermute | solution.py:37
  25.2 0.0 collective-permute-done.11.refs_13_.refs_15_
  25.2 2.2 %collective-permute-start.17 = (bf16[8,64,640]{2,1,0:T(8,128)(2,1)}, bf16[8,64,640]{2,1,0:T(8,128)(2,1)}, u32[]{:S(2)}, u32[]{:S(2)}) collective-permute-start(bf16[8,64,640]{2,1,0:T(8,128)(2,1)} %get-tuple-element.16), channel_id=1, source_target_pairs={{0,2},{1,3},{2,0},{3,1},{4,6},{5,7},{6,4},{7,5},{8,10},{9,11},{10,... | collective-permute-start | bytes 1966088 | tf_op jit(solution)/shard_map/ppermute | solution.py:37
  27.4 0.0 copy-done
  27.4 0.0 copy-done.1
  27.4 0.8 pack.1
  28.1 9.9 %all-to-all-start = ((bf16[16,80,128]{2,1,0:T(8,128)(2,1)}), bf16[16,80,128]{2,1,0:T(8,128)(2,1)S(1)}, u32[]{:S(2)}, u32[]{:S(2)}) async-start(bf16[16,80,128]{2,1,0:T(8,128)(2,1)} %pack.1), calls=%async_computation | async-start | bytes 655360 | tf_op jit(solution)/shard_map/all_to_all | solution.py:41
  38.0 0.0 collective-permute-done.13.refs_15_.refs_17_
  38.1 0.1 collective-permute-start.2
  38.2 0.0 collective-permute-done.8.refs_10_.refs_12_
  38.2 0.5 collective-permute-start.4
  38.7 0.9 collective-permute-done.2.refs_4_.refs_6_
  39.6 0.1 collective-permute-start.6
  39.7 0.1 collective-permute-done.4.refs_6_.refs_8_
  39.8 0.3 collective-permute-start.10
  40.1 0.9 collective-permute-done.6.refs_8_.refs_10_
  41.0 0.1 collective-permute-start.12
  41.1 0.1 collective-permute-done.10.refs_12_.refs_14_
  41.2 0.3 collective-permute-start.14
  41.5 0.9 collective-permute-done.12.refs_14_.refs_16_
  42.4 0.3 collective-permute-done.14.refs_16_.refs_18_
  42.7 3.1 %scores.2 = (f32[64,2048]{1,0:T(8,128)S(1)}, bf16[2048,128]{1,0:T(8,128)(2,1)S(1)}) custom-call(bf16[8,64,640]{2,1,0:T(8,128)(2,1)} %get-tuple-element.12.refs_0_, bf16[704,128]{1,0:T(8,128)(2,1)S(1)} %pad_maximum_fusion.1.refs_1_.refs_3_, bf16[704,128]{1,0:T(8,128)(2,1)S(1)} %collective-permute-done.refs_2_.refs_4_, ...), custom_call_target="tpu_custom_call" | custom-call | tf_op jit(solution)/shard_map/scores/pallas_call | solution.py:155
  45.8 0.0 collective-permute-done.15.refs_0_
  45.8 10.7 %collective-permute-done.16.refs_1_ = bf16[8,64,640]{2,1,0:T(8,128)(2,1)} collective-permute-done((bf16[8,64,640]{2,1,0:T(8,128)(2,1)}, bf16[8,64,640]{2,1,0:T(8,128)(2,1)}, u32[]{:S(2)}, u32[]{:S(2)}) %collective-permute-start.16) | collective-permute-done | bytes 655392 | tf_op jit(solution)/shard_map/ppermute | solution.py:37
  56.4 2.8 %collective-permute-done.17.refs_2_ = bf16[8,64,640]{2,1,0:T(8,128)(2,1)} collective-permute-done((bf16[8,64,640]{2,1,0:T(8,128)(2,1)}, bf16[8,64,640]{2,1,0:T(8,128)(2,1)}, u32[]{:S(2)}, u32[]{:S(2)}) %collective-permute-start.17) | collective-permute-done | bytes 655392 | tf_op jit(solution)/shard_map/ppermute | solution.py:37
  59.2 0.0 copy-start.2
  59.2 7.5 %scores.3 = bf16[64,2048]{1,0:T(8,128)(2,1)} custom-call(bf16[8,64,640]{2,1,0:T(8,128)(2,1)} %collective-permute-done.15.refs_0_, bf16[8,64,640]{2,1,0:T(8,128)(2,1)} %collective-permute-done.16.refs_1_, bf16[8,64,640]{2,1,0:T(8,128)(2,1)} %collective-permute-done.17.refs_2_, bf16[704,128]{1,0:T(8,128)(2,1)S(1)} %pad_maximum_fusion.1.refs_1_.refs_3_, ...), custom_call_target="tpu_custom_call" | custom-call | tf_op jit(solution)/shard_map/scores/pallas_call | solution.py:155
  66.7 0.0 all-to-all-done.q_ref
  66.7 8.4 %all-to-all-start.1 = ((bf16[4,16,2048]{2,1,0:T(8,128)(2,1)}), bf16[4,16,2048]{2,1,0:T(8,128)(2,1)S(1)}, u32[]{:S(2)}, u32[]{:S(2)}) async-start(bf16[4,16,2048]{2,1,0:T(8,128)(2,1)} %bitcast.10), calls=%async_computation.1 | async-start | bytes 524288 | tf_op jit(solution)/shard_map/all_to_all | solution.py:41
  75.2 0.0 copy-done.2
  75.2 3.0 %index_forward.1.prob_ref = f32[16,2048]{1,0:T(8,128)S(1)} custom-call(s32[5]{0:T(128)S(1)} %stack.23.at_ref, s32[2,16]{1,0:T(2,128)S(1)} %copy-done.2, bf16[16,80,128]{2,1,0:T(8,128)(2,1)S(1)} %all-to-all-done.q_ref, bf16[2048,128]{1,0:T(8,128)(2,1)S(1)} %get-tuple-element.13.keys), custom_call_target="tpu_custom_call" | custom-call | tf_op jit(solution)/shard_map/index_forward/pallas_call | solution.py:237
  78.2 7.2 %all-to-all-done.1.sums = bf16[4,16,2048]{2,1,0:T(8,128)(2,1)S(1)} async-done(((bf16[4,16,2048]{2,1,0:T(8,128)(2,1)}), bf16[4,16,2048]{2,1,0:T(8,128)(2,1)S(1)}, u32[]{:S(2)}, u32[]{:S(2)}) %all-to-all-start.1) | async-done | bytes 262176 | tf_op jit(solution)/shard_map/all_to_all | solution.py:41
  85.4 3.9 %index_backward.1 = (bf16[16,128,128]{2,1,0:T(8,128)(2,1)S(1)}, bf16[16,64,128]{2,1,0:T(8,128)(2,1)S(1)}) custom-call(s32[5]{0:T(128)S(1)} %stack.23.at_ref, s32[2,16]{1,0:T(2,128)S(1)} %copy-done.2, f32[16,2048]{1,0:T(8,128)S(1)} %index_forward.1.prob_ref, bf16[16,80,128]{2,1,0:T(8,128)(2,1)S(1)} %all-to-all-done.q_ref, ...), custom_call_target="tpu_custom_call" | custom-call | tf_op jit(solution)/shard_map/index_backward/pallas_call | solution.py:284
  89.3 19.9 %all_to_all.20 = bf16[64,32,128]{2,1,0:T(8,128)(2,1)S(1)} all-to-all(bf16[64,32,128]{2,1,0:T(8,128)(2,1)S(1)} %bitcast.13), channel_id=1, replica_groups={{0,1,2,3,16,17,18,19,32,33,34,35,48,49,50,51,64,65,66,67,80,81,82,83,96..., dimensions={0} | all-to-all | bytes 1048576 | tf_op jit(solution)/shard_map/all_to_all | solution.py:41
  109.2 0.1 reduce_sum.12
  109.4 17.9 %all_to_all.21.both_ref = bf16[16,96,128]{2,1,0:T(8,128)(2,1)S(1)} all-to-all(bf16[16,96,128]{2,1,0:T(8,128)(2,1)S(1)} %pad_maximum_fusion), channel_id=1, replica_groups=mesh['seq'=16,'head'=16] {'head'}, dimensions={0} | all-to-all | bytes 786432 | tf_op jit(solution)/shard_map/all_to_all | solution.py:41
  127.3 0.9 last.1
  (2 shorter events, 0.0 us)
Async XLA Ops:
  0.6 26.7 %copy-start = (bf16[256,4,128]{2,1,0:T(4,128)(2,1)S(1)}, bf16[256,4,128]{2,1,0:T(4,128)(2,1)}, u32[]{:S(2)}) copy-start(bf16[256,4,128]{2,1,0:T(4,128)(2,1)} %param.10) | copy-start | bytes 786436
  0.6 26.7 %copy-start.1 = (f32[256,4]{0,1:T(4,128)S(1)}, f32[256,4]{0,1:T(4,128)}, u32[]{:S(2)}) copy-start(f32[256,4]{0,1:T(4,128)} %param.12) | copy-start | bytes 12292
  1.6 6.4 %collective-permute-start.7 = (bf16[704,128]{1,0:T(8,128)(2,1)S(1)}, bf16[704,128]{1,0:T(8,128)(2,1)S(1)}, u32[]{:S(2)}, u32[]{:S(2)}) collective-permute-start(bf16[704,128]{1,0:T(8,128)(2,1)S(1)} %pad_maximum_fusion.1.refs_1_.refs_3_), channel_id=1, source_target_pairs={{0,32},{16,48},{32,0},{48,16},{64,96},{80,112},{96,64},{112,80},{1... | collective-permute-start | bytes 540680 | tf_op jit(solution)/shard_map/ppermute | solution.py:29
  3.5 8.7 %collective-permute-start.1 = (bf16[704,128]{1,0:T(8,128)(2,1)S(1)}, bf16[704,128]{1,0:T(8,128)(2,1)S(1)}, u32[]{:S(2)}, u32[]{:S(2)}) collective-permute-start(bf16[704,128]{1,0:T(8,128)(2,1)S(1)} %pad_maximum_fusion.1.refs_1_.refs_3_), channel_id=1, source_target_pairs={{0,192},{16,208},{32,224},{48,240},{64,0},{80,16},{96,32},{112,48}... | collective-permute-start | bytes 540680 | tf_op jit(solution)/shard_map/ppermute | solution.py:25
  4.8 12.0 %collective-permute-start.3 = (bf16[704,128]{1,0:T(8,128)(2,1)S(1)}, bf16[704,128]{1,0:T(8,128)(2,1)S(1)}, u32[]{:S(2)}, u32[]{:S(2)}) collective-permute-start(bf16[704,128]{1,0:T(8,128)(2,1)S(1)} %pad_maximum_fusion.1.refs_1_.refs_3_), channel_id=1, source_target_pairs={{0,64},{16,80},{32,96},{48,112},{64,128},{80,144},{96,160},{112,17... | collective-permute-start | bytes 540680 | tf_op jit(solution)/shard_map/ppermute | solution.py:25
  5.5 12.3 %collective-permute-start.5 = (bf16[704,128]{1,0:T(8,128)(2,1)S(1)}, bf16[704,128]{1,0:T(8,128)(2,1)S(1)}, u32[]{:S(2)}, u32[]{:S(2)}) collective-permute-start(bf16[704,128]{1,0:T(8,128)(2,1)S(1)} %pad_maximum_fusion.1.refs_1_.refs_3_), channel_id=1, source_target_pairs={{0,128},{16,144},{32,160},{48,176},{64,192},{80,208},{96,224},{112... | collective-permute-start | bytes 540680 | tf_op jit(solution)/shard_map/ppermute | solution.py:25
  7.0 14.7 %collective-permute-start = (bf16[704,128]{1,0:T(8,128)(2,1)S(1)}, bf16[704,128]{1,0:T(8,128)(2,1)S(1)}, u32[]{:S(2)}, u32[]{:S(2)}) collective-permute-start(bf16[704,128]{1,0:T(8,128)(2,1)S(1)} %pad_maximum_fusion.1.refs_1_.refs_3_), channel_id=1, source_target_pairs={{0,16},{16,0},{32,48},{48,32},{64,80},{80,64},{96,112},{112,96},{1... | collective-permute-start | bytes 540680 | tf_op jit(solution)/shard_map/ppermute | solution.py:33
  8.0 15.8 %collective-permute-start.9 = (bf16[704,128]{1,0:T(8,128)(2,1)S(1)}, bf16[704,128]{1,0:T(8,128)(2,1)S(1)}, u32[]{:S(2)}, u32[]{:S(2)}) collective-permute-start(bf16[704,128]{1,0:T(8,128)(2,1)S(1)} %collective-permute-done.7.refs_9_.refs_11_), channel_id=1, source_target_pairs={{0,192},{16,208},{32,224},{48,240},{64,0},{80,16},{96,32},{112,48}... | collective-permute-start | bytes 540680 | tf_op jit(solution)/shard_map/ppermute | solution.py:25
  12.2 13.0 %collective-permute-start.11 = (bf16[704,128]{1,0:T(8,128)(2,1)S(1)}, bf16[704,128]{1,0:T(8,128)(2,1)S(1)}, u32[]{:S(2)}, u32[]{:S(2)}) collective-permute-start(bf16[704,128]{1,0:T(8,128)(2,1)S(1)} %collective-permute-done.7.refs_9_.refs_11_), channel_id=1, source_target_pairs={{0,64},{16,80},{32,96},{48,112},{64,128},{80,144},{96,160},{112,17... | collective-permute-start | bytes 540680 | tf_op jit(solution)/shard_map/ppermute | solution.py:25
  16.8 21.2 %collective-permute-start.13 = (bf16[704,128]{1,0:T(8,128)(2,1)S(1)}, bf16[704,128]{1,0:T(8,128)(2,1)S(1)}, u32[]{:S(2)}, u32[]{:S(2)}) collective-permute-start(bf16[704,128]{1,0:T(8,128)(2,1)S(1)} %collective-permute-done.7.refs_9_.refs_11_), channel_id=1, source_target_pairs={{0,128},{16,144},{32,160},{48,176},{64,192},{80,208},{96,224},{112... | collective-permute-start | bytes 540680 | tf_op jit(solution)/shard_map/ppermute | solution.py:25
  17.9 20.3 %collective-permute-start.8 = (bf16[704,128]{1,0:T(8,128)(2,1)S(1)}, bf16[704,128]{1,0:T(8,128)(2,1)S(1)}, u32[]{:S(2)}, u32[]{:S(2)}) collective-permute-start(bf16[704,128]{1,0:T(8,128)(2,1)S(1)} %collective-permute-done.7.refs_9_.refs_11_), channel_id=1, source_target_pairs={{0,16},{16,0},{32,48},{48,32},{64,80},{80,64},{96,112},{112,96},{1... | collective-permute-start | bytes 540680 | tf_op jit(solution)/shard_map/ppermute | solution.py:33
  21.7 24.1 %collective-permute-start.15 = (bf16[8,64,640]{2,1,0:T(8,128)(2,1)}, bf16[8,64,640]{2,1,0:T(8,128)(2,1)}, u32[]{:S(2)}, u32[]{:S(2)}) collective-permute-start(bf16[8,64,640]{2,1,0:T(8,128)(2,1)} %get-tuple-element.14), channel_id=1, source_target_pairs={{0,1},{1,2},{2,3},{3,0},{4,5},{5,6},{6,7},{7,4},{8,9},{9,10},{10,1... | collective-permute-start | bytes 1966088 | tf_op jit(solution)/shard_map/ppermute | solution.py:37
  23.8 32.6 %collective-permute-start.16 = (bf16[8,64,640]{2,1,0:T(8,128)(2,1)}, bf16[8,64,640]{2,1,0:T(8,128)(2,1)}, u32[]{:S(2)}, u32[]{:S(2)}) collective-permute-start(bf16[8,64,640]{2,1,0:T(8,128)(2,1)} %get-tuple-element.15), channel_id=1, source_target_pairs={{0,3},{1,0},{2,1},{3,2},{4,7},{5,4},{6,5},{7,6},{8,11},{9,8},{10,9... | collective-permute-start | bytes 1966088 | tf_op jit(solution)/shard_map/ppermute | solution.py:37
  25.2 34.1 %collective-permute-start.17 = (bf16[8,64,640]{2,1,0:T(8,128)(2,1)}, bf16[8,64,640]{2,1,0:T(8,128)(2,1)}, u32[]{:S(2)}, u32[]{:S(2)}) collective-permute-start(bf16[8,64,640]{2,1,0:T(8,128)(2,1)} %get-tuple-element.16), channel_id=1, source_target_pairs={{0,2},{1,3},{2,0},{3,1},{4,6},{5,7},{6,4},{7,5},{8,10},{9,11},{10,... | collective-permute-start | bytes 1966088 | tf_op jit(solution)/shard_map/ppermute | solution.py:37
  28.1 38.6 %all-to-all-start = ((bf16[16,80,128]{2,1,0:T(8,128)(2,1)}), bf16[16,80,128]{2,1,0:T(8,128)(2,1)S(1)}, u32[]{:S(2)}, u32[]{:S(2)}) async-start(bf16[16,80,128]{2,1,0:T(8,128)(2,1)} %pack.1), calls=%async_computation | async-start | bytes 655360 | tf_op jit(solution)/shard_map/all_to_all | solution.py:41
  38.1 1.5 %collective-permute-start.2 = (bf16[704,128]{1,0:T(8,128)(2,1)S(1)}, bf16[704,128]{1,0:T(8,128)(2,1)S(1)}, u32[]{:S(2)}, u32[]{:S(2)}) collective-permute-start(bf16[704,128]{1,0:T(8,128)(2,1)S(1)} %collective-permute-done.1.refs_3_.refs_5_), channel_id=1, source_target_pairs={{0,16},{16,0},{32,48},{48,32},{64,80},{80,64},{96,112},{112,96},{1... | collective-permute-start | bytes 540680 | tf_op jit(solution)/shard_map/ppermute | solution.py:33
  38.2 1.7 %collective-permute-start.4 = (bf16[704,128]{1,0:T(8,128)(2,1)S(1)}, bf16[704,128]{1,0:T(8,128)(2,1)S(1)}, u32[]{:S(2)}, u32[]{:S(2)}) collective-permute-start(bf16[704,128]{1,0:T(8,128)(2,1)S(1)} %collective-permute-done.3.refs_5_.refs_7_), channel_id=1, source_target_pairs={{0,16},{16,0},{32,48},{48,32},{64,80},{80,64},{96,112},{112,96},{1... | collective-permute-start | bytes 540680 | tf_op jit(solution)/shard_map/ppermute | solution.py:33
  39.6 1.4 %collective-permute-start.6 = (bf16[704,128]{1,0:T(8,128)(2,1)S(1)}, bf16[704,128]{1,0:T(8,128)(2,1)S(1)}, u32[]{:S(2)}, u32[]{:S(2)}) collective-permute-start(bf16[704,128]{1,0:T(8,128)(2,1)S(1)} %collective-permute-done.5.refs_7_.refs_9_), channel_id=1, source_target_pairs={{0,16},{16,0},{32,48},{48,32},{64,80},{80,64},{96,112},{112,96},{1... | collective-permute-start | bytes 540680 | tf_op jit(solution)/shard_map/ppermute | solution.py:33
  39.8 1.4 %collective-permute-start.10 = (bf16[704,128]{1,0:T(8,128)(2,1)S(1)}, bf16[704,128]{1,0:T(8,128)(2,1)S(1)}, u32[]{:S(2)}, u32[]{:S(2)}) collective-permute-start(bf16[704,128]{1,0:T(8,128)(2,1)S(1)} %collective-permute-done.9.refs_11_.refs_13_), channel_id=1, source_target_pairs={{0,16},{16,0},{32,48},{48,32},{64,80},{80,64},{96,112},{112,96},{1... | collective-permute-start | bytes 540680 | tf_op jit(solution)/shard_map/ppermute | solution.py:33
  41.0 1.4 %collective-permute-start.12 = (bf16[704,128]{1,0:T(8,128)(2,1)S(1)}, bf16[704,128]{1,0:T(8,128)(2,1)S(1)}, u32[]{:S(2)}, u32[]{:S(2)}) collective-permute-start(bf16[704,128]{1,0:T(8,128)(2,1)S(1)} %collective-permute-done.11.refs_13_.refs_15_), channel_id=1, source_target_pairs={{0,16},{16,0},{32,48},{48,32},{64,80},{80,64},{96,112},{112,96},{1... | collective-permute-start | bytes 540680 | tf_op jit(solution)/shard_map/ppermute | solution.py:33
  41.2 1.4 %collective-permute-start.14 = (bf16[704,128]{1,0:T(8,128)(2,1)S(1)}, bf16[704,128]{1,0:T(8,128)(2,1)S(1)}, u32[]{:S(2)}, u32[]{:S(2)}) collective-permute-start(bf16[704,128]{1,0:T(8,128)(2,1)S(1)} %collective-permute-done.13.refs_15_.refs_17_), channel_id=1, source_target_pairs={{0,16},{16,0},{32,48},{48,32},{64,80},{80,64},{96,112},{112,96},{1... | collective-permute-start | bytes 540680 | tf_op jit(solution)/shard_map/ppermute | solution.py:33
  59.2 16.0 %copy-start.2 = (s32[2,16]{1,0:T(2,128)S(1)}, s32[2,16]{1,0:T(2,128)}, u32[]{:S(2)}) copy-start(s32[2,16]{1,0:T(2,128)} %kept_ref.3) | copy-start | bytes 388
  66.7 18.6 %all-to-all-start.1 = ((bf16[4,16,2048]{2,1,0:T(8,128)(2,1)}), bf16[4,16,2048]{2,1,0:T(8,128)(2,1)S(1)}, u32[]{:S(2)}, u32[]{:S(2)}) async-start(bf16[4,16,2048]{2,1,0:T(8,128)(2,1)} %bitcast.10), calls=%async_computation.1 | async-start | bytes 524288 | tf_op jit(solution)/shard_map/all_to_all | solution.py:41

commit v7 on v5

--- a/solution.py
+++ b/solution.py
@@ -159,7 +159,7 @@
     return call(
         functools.partial(score_body, groups, last),
         (sds((rows, 2048), bf16),) if last else (sds((rows, 2048), f32), sds((2048, 128), bf16)),
-        [HB] * groups + [VM] * (16 + last),
+        [pl.BlockSpec(memory_space=pl.ANY) if last else HB] * groups + [VM] * (16 + last),
         16,
         scratch_shapes=[
             pltpu.VMEM((groups, heads, rows, depth), bf16),
@@ -168,7 +168,7 @@
             pltpu.SemaphoreType.DMA((groups,)),
         ],
         name="scores",
-    )(*in_hbm(*queries), *tiles, *before)
+    )(*(queries if last else in_hbm(*queries)), *tiles, *before)
 
 
 def pack_body(q_ref, w_ref, out_ref):
@@ -327,8 +327,8 @@
     query = [parts[0]]
     for part, d in zip(parts[1:], STEPS):
         query.append(along_x(part, d))
-    part, index_keys = scores(query[:3], tiles)
-    (part,) = scores(query[3:], tiles, part)
+    part, index_keys = scores(query[:1], tiles)
+    (part,) = scores(query[1:], tiles, part)
     sums = exchanged(part.reshape(4, 16, 2048), "head", ROW_ZH)
 
     prob = index_forward(at, kept, queries, index_keys, index_scale)

time: 129 us -> 126 us (0.977)
  blocking collectives: 34.3 us -> 32.2 us
    all_to_all x2, blocking collectives: 34.3 us -> 32.2 us  [exchanged(): lax.all_to_all(value, axis, 0, 0, tiled=True, axis_index_groups=groups)]
  transfers between devices with their start and end apart: 21 -> 21, of which waited for: 12 -> 13; matrix products, arithmetic and copies ran while one was open for 0% -> 0% of each run, Pallas kernels for 14% -> 14%
where the time goes in v7:
time: 126 us; the launch traced here: 123 us
  starting transfers between devices  34.9 us (28%)
  waiting for transfers between devices  32.2 us (26%)
  blocking collectives  32.2 us (26%)
  Pallas kernels  21.9 us (17%)
    all_to_all x2, blocking collectives, exchanged(): lax.all_to_all(value, axis, 0, 0, tiled=True, axis_index_groups=groups)  32.2 us
    all_to_all x2, starting transfers between devices, exchanged(): lax.all_to_all(value, axis, 0, 0, tiled=True, axis_index_groups=groups)  18.4 us
    ppermute x3, waiting for transfers between devices, along_x(): lax.ppermute(value, 'head', [(i, i // 4 * 4 + (i + d) % 4) for i in range...  13.5 us
    pallas_call x2, Pallas kernels, scores(): call(functools.partial(score_body, groups, last), (sds((rows, 2048), bf16...  9.72 us
    ppermute x6, starting transfers between devices, along_y(): lax.ppermute(value, 'seq', [(i, (i + 4 * d) % 16) for i in range(16)])  7.56 us
    all_to_all x2, waiting for transfers between devices, exchanged(): lax.all_to_all(value, axis, 0, 0, tiled=True, axis_index_groups=groups)  7.19 us
    ppermute x6, waiting for transfers between devices, along_y(): lax.ppermute(value, 'seq', [(i, (i + 4 * d) % 16) for i in range(16)])  5.82 us
    ppermute x3, starting transfers between devices, along_x(): lax.ppermute(value, 'head', [(i, i // 4 * 4 + (i + d) % 4) for i in range...  5.63 us
  transfers between devices with their start and end apart: 21, of which 13 were waited for; matrix products, arithmetic and copies ran while one was open for 0% of the time, Pallas kernels for 14%

profile of v7, /device:TPU:32, one launch (start us, length us, event | category | flops | bytes accessed | tf_op | source)
XLA Modules:
  0.0 123.2 jit_solution(1530644631891421374)
XLA Ops:
  0.6 0.0 copy-start
  0.6 0.0 copy-start.1
  0.7 1.0 pad_maximum_fusion.1.refs_1_.refs_3_
  1.6 1.9 %collective-permute-start.7 = (bf16[704,128]{1,0:T(8,128)(2,1)S(1)}, bf16[704,128]{1,0:T(8,128)(2,1)S(1)}, u32[]{:S(2)}, u32[]{:S(2)}) collective-permute-start(bf16[704,128]{1,0:T(8,128)(2,1)S(1)} %pad_maximum_fusion.1.refs_1_.refs_3_), channel_id=1, source_target_pairs={{0,32},{16,48},{32,0},{48,16},{64,96},{80,112},{96,64},{112,80},{1... | collective-permute-start | bytes 540680 | tf_op jit(solution)/shard_map/ppermute | solution.py:33
  3.5 1.3 %collective-permute-start.1 = (bf16[704,128]{1,0:T(8,128)(2,1)S(1)}, bf16[704,128]{1,0:T(8,128)(2,1)S(1)}, u32[]{:S(2)}, u32[]{:S(2)}) collective-permute-start(bf16[704,128]{1,0:T(8,128)(2,1)S(1)} %pad_maximum_fusion.1.refs_1_.refs_3_), channel_id=1, source_target_pairs={{0,192},{16,208},{32,224},{48,240},{64,0},{80,16},{96,32},{112,48}... | collective-permute-start | bytes 540680 | tf_op jit(solution)/shard_map/ppermute | solution.py:29
  4.8 0.7 collective-permute-start.3
  5.5 1.5 %collective-permute-start.5 = (bf16[704,128]{1,0:T(8,128)(2,1)S(1)}, bf16[704,128]{1,0:T(8,128)(2,1)S(1)}, u32[]{:S(2)}, u32[]{:S(2)}) collective-permute-start(bf16[704,128]{1,0:T(8,128)(2,1)S(1)} %pad_maximum_fusion.1.refs_1_.refs_3_), channel_id=1, source_target_pairs={{0,128},{16,144},{32,160},{48,176},{64,192},{80,208},{96,224},{112... | collective-permute-start | bytes 540680 | tf_op jit(solution)/shard_map/ppermute | solution.py:29
  7.0 0.0 collective-permute-start
  7.0 1.0 collective-permute-done.7.refs_9_.refs_11_
  8.0 3.0 %collective-permute-start.9 = (bf16[704,128]{1,0:T(8,128)(2,1)S(1)}, bf16[704,128]{1,0:T(8,128)(2,1)S(1)}, u32[]{:S(2)}, u32[]{:S(2)}) collective-permute-start(bf16[704,128]{1,0:T(8,128)(2,1)S(1)} %collective-permute-done.7.refs_9_.refs_11_), channel_id=1, source_target_pairs={{0,192},{16,208},{32,224},{48,240},{64,0},{80,16},{96,32},{112,48}... | collective-permute-start | bytes 540680 | tf_op jit(solution)/shard_map/ppermute | solution.py:29
  11.0 1.2 collective-permute-done.1.refs_3_.refs_5_
  12.2 0.0 collective-permute-start.11
  12.2 4.6 %collective-permute-done.3.refs_5_.refs_7_ = bf16[704,128]{1,0:T(8,128)(2,1)S(1)} collective-permute-done((bf16[704,128]{1,0:T(8,128)(2,1)S(1)}, bf16[704,128]{1,0:T(8,128)(2,1)S(1)}, u32[]{:S(2)}, u32[]{:S(2)}) %collective-permute-start.3) | collective-permute-done | bytes 180256 | tf_op jit(solution)/shard_map/ppermute | solution.py:29
  16.8 1.0 collective-permute-start.13
  17.9 0.0 collective-permute-done.5.refs_7_.refs_9_
  17.9 0.0 collective-permute-start.8
  17.9 0.1 stack.23.at_ref
  17.9 3.8 %wide_queries.1 = (bf16[8,64,640]{2,1,0:T(8,128)(2,1)}, bf16[8,64,640]{2,1,0:T(8,128)(2,1)}, bf16[8,64,640]{2,1,0:T(8,128)(2,1)}, bf16[8,64,640]{2,1,0:T(8,128)(2,1)}) custom-call(s32[5]{0:T(128)S(1)} %stack.23.at_ref, bf16[8,576,256]{2,1,0:T(8,128)(2,1)} %bitcast.15, f32[8,256]{1,0:T(8,128)} %bitcast.18), custom_call_target="tpu_custom_call" | custom-call | tf_op jit(solution)/shard_map/wide_queries/pallas_call | solution.py:102
  21.7 0.0 collective-permute-done.refs_2_.refs_4_
  21.7 2.1 %collective-permute-start.15 = (bf16[8,64,640]{2,1,0:T(8,128)(2,1)}, bf16[8,64,640]{2,1,0:T(8,128)(2,1)S(1)}, u32[]{:S(2)}, u32[]{:S(2)}) collective-permute-start(bf16[8,64,640]{2,1,0:T(8,128)(2,1)} %get-tuple-element.15), channel_id=1, source_target_pairs={{0,1},{1,2},{2,3},{3,0},{4,5},{5,6},{6,7},{7,4},{8,9},{9,10},{10,1... | collective-permute-start | bytes 1966088 | tf_op jit(solution)/shard_map/ppermute | solution.py:41
  23.8 0.0 collective-permute-done.9.refs_11_.refs_13_
  23.8 1.4 %collective-permute-start.16 = (bf16[8,64,640]{2,1,0:T(8,128)(2,1)}, bf16[8,64,640]{2,1,0:T(8,128)(2,1)}, u32[]{:S(2)}, u32[]{:S(2)}) collective-permute-start(bf16[8,64,640]{2,1,0:T(8,128)(2,1)} %get-tuple-element.16), channel_id=1, source_target_pairs={{0,3},{1,0},{2,1},{3,2},{4,7},{5,4},{6,5},{7,6},{8,11},{9,8},{10,9... | collective-permute-start | bytes 1966088 | tf_op jit(solution)/shard_map/ppermute | solution.py:41
  25.2 0.0 collective-permute-done.11.refs_13_.refs_15_
  25.2 2.2 %collective-permute-start.17 = (bf16[8,64,640]{2,1,0:T(8,128)(2,1)}, bf16[8,64,640]{2,1,0:T(8,128)(2,1)}, u32[]{:S(2)}, u32[]{:S(2)}) collective-permute-start(bf16[8,64,640]{2,1,0:T(8,128)(2,1)} %get-tuple-element.17), channel_id=1, source_target_pairs={{0,2},{1,3},{2,0},{3,1},{4,6},{5,7},{6,4},{7,5},{8,10},{9,11},{10,... | collective-permute-start | bytes 1966088 | tf_op jit(solution)/shard_map/ppermute | solution.py:41
  27.4 0.0 copy-done
  27.4 0.0 copy-done.1
  27.4 0.7 pack.1
  28.1 9.9 %all-to-all-start = ((bf16[16,80,128]{2,1,0:T(8,128)(2,1)}), bf16[16,80,128]{2,1,0:T(8,128)(2,1)S(1)}, u32[]{:S(2)}, u32[]{:S(2)}) async-start(bf16[16,80,128]{2,1,0:T(8,128)(2,1)} %pack.1), calls=%async_computation | async-start | bytes 655360 | tf_op jit(solution)/shard_map/all_to_all | solution.py:45
  38.0 0.0 collective-permute-done.13.refs_15_.refs_17_
  38.1 0.1 collective-permute-start.2
  38.2 0.0 collective-permute-done.8.refs_10_.refs_12_
  38.2 0.5 collective-permute-start.4
  38.7 0.9 collective-permute-done.2.refs_4_.refs_6_
  39.6 0.1 collective-permute-start.6
  39.7 0.1 collective-permute-done.4.refs_6_.refs_8_
  39.8 0.3 collective-permute-start.10
  40.1 0.9 collective-permute-done.6.refs_8_.refs_10_
  41.0 0.1 collective-permute-start.12
  41.1 0.1 collective-permute-done.10.refs_12_.refs_14_
  41.2 0.3 collective-permute-start.14
  41.5 0.9 collective-permute-done.12.refs_14_.refs_16_
  42.4 0.3 collective-permute-done.14.refs_16_.refs_18_
  42.7 3.1 %scores.2 = (f32[64,2048]{1,0:T(8,128)S(1)}, bf16[2048,128]{1,0:T(8,128)(2,1)S(1)}) custom-call(bf16[8,64,640]{2,1,0:T(8,128)(2,1)} %get-tuple-element.13.refs_0_, bf16[704,128]{1,0:T(8,128)(2,1)S(1)} %pad_maximum_fusion.1.refs_1_.refs_3_, bf16[704,128]{1,0:T(8,128)(2,1)S(1)} %collective-permute-done.refs_2_.refs_4_, ...), custom_call_target="tpu_custom_call" | custom-call | tf_op jit(solution)/shard_map/scores/pallas_call | solution.py:159
  45.8 0.0 collective-permute-done.15.refs_0_
  45.8 10.7 %collective-permute-done.16.refs_1_ = bf16[8,64,640]{2,1,0:T(8,128)(2,1)} collective-permute-done((bf16[8,64,640]{2,1,0:T(8,128)(2,1)}, bf16[8,64,640]{2,1,0:T(8,128)(2,1)}, u32[]{:S(2)}, u32[]{:S(2)}) %collective-permute-start.16) | collective-permute-done | bytes 655392 | tf_op jit(solution)/shard_map/ppermute | solution.py:41
  56.4 2.8 %collective-permute-done.17.refs_2_ = bf16[8,64,640]{2,1,0:T(8,128)(2,1)} collective-permute-done((bf16[8,64,640]{2,1,0:T(8,128)(2,1)}, bf16[8,64,640]{2,1,0:T(8,128)(2,1)}, u32[]{:S(2)}, u32[]{:S(2)}) %collective-permute-start.17) | collective-permute-done | bytes 655392 | tf_op jit(solution)/shard_map/ppermute | solution.py:41
  59.2 0.0 copy-start.2
  59.2 6.6 %scores.3 = bf16[64,2048]{1,0:T(8,128)(2,1)} custom-call(bf16[8,64,640]{2,1,0:T(8,128)(2,1)S(1)} %collective-permute-done.15.refs_0_, bf16[8,64,640]{2,1,0:T(8,128)(2,1)} %collective-permute-done.16.refs_1_, bf16[8,64,640]{2,1,0:T(8,128)(2,1)} %collective-permute-done.17.refs_2_, bf16[704,128]{1,0:T(8,128)(2,1)S(1)} %pad_maximum_fusion.1.refs_1_.refs_3_, ...), custom_call_target="tpu_custom_call" | custom-call | tf_op jit(solution)/shard_map/scores/pallas_call | solution.py:159
  65.9 0.0 all-to-all-done.q_ref
  65.9 8.4 %all-to-all-start.1 = ((bf16[4,16,2048]{2,1,0:T(8,128)(2,1)}), bf16[4,16,2048]{2,1,0:T(8,128)(2,1)S(1)}, u32[]{:S(2)}, u32[]{:S(2)}) async-start(bf16[4,16,2048]{2,1,0:T(8,128)(2,1)} %bitcast.10), calls=%async_computation.1 | async-start | bytes 524288 | tf_op jit(solution)/shard_map/all_to_all | solution.py:45
  74.3 0.0 copy-done.2
  74.3 3.0 %index_forward.1.prob_ref = f32[16,2048]{1,0:T(8,128)S(1)} custom-call(s32[5]{0:T(128)S(1)} %stack.23.at_ref, s32[2,16]{1,0:T(2,128)S(1)} %copy-done.2, bf16[16,80,128]{2,1,0:T(8,128)(2,1)S(1)} %all-to-all-done.q_ref, bf16[2048,128]{1,0:T(8,128)(2,1)S(1)} %get-tuple-element.14.keys), custom_call_target="tpu_custom_call" | custom-call | tf_op jit(solution)/shard_map/index_forward/pallas_call | solution.py:241
  77.3 7.2 %all-to-all-done.1.sums = bf16[4,16,2048]{2,1,0:T(8,128)(2,1)S(1)} async-done(((bf16[4,16,2048]{2,1,0:T(8,128)(2,1)}), bf16[4,16,2048]{2,1,0:T(8,128)(2,1)S(1)}, u32[]{:S(2)}, u32[]{:S(2)}) %all-to-all-start.1) | async-done | bytes 262176 | tf_op jit(solution)/shard_map/all_to_all | solution.py:45
  84.5 3.8 %index_backward.1 = (f32[8,128,128]{2,1,0:T(8,128)S(1)}, bf16[8,128,128]{2,1,0:T(8,128)(2,1)S(1)}, bf16[16,64,128]{2,1,0:T(8,128)(2,1)S(1)}) custom-call(s32[5]{0:T(128)S(1)} %stack.23.at_ref, s32[2,16]{1,0:T(2,128)S(1)} %copy-done.2, f32[16,2048]{1,0:T(8,128)S(1)} %index_forward.1.prob_ref, bf16[16,80,128]{2,1,0:T(8,128)(2,1)S(1)} %all-to-all-done.q_ref, ...), custom_call_target="tpu_custom_call" | custom-call | tf_op jit(solution)/shard_map/index_backward/pallas_call | solution.py:292
  88.3 0.1 collective-permute-start.18
  88.4 1.5 %collective-permute-done.18 = bf16[8,128,128]{2,1,0:T(8,128)(2,1)S(1)} collective-permute-done((bf16[8,128,128]{2,1,0:T(8,128)(2,1)S(1)}, bf16[8,128,128]{2,1,0:T(8,128)(2,1)S(1)}, u32[]{:S(2)}, u32[]{:S(2)}) %collective-permute-start.18) | collective-permute-done | bytes 262176 | tf_op jit(solution)/shard_map/ppermute | solution.py:37
  90.0 0.1 add_convert_fusion
  90.0 16.2 %all_to_all.20 = bf16[32,32,128]{2,1,0:T(8,128)(2,1)S(1)} all-to-all(bf16[32,32,128]{2,1,0:T(8,128)(2,1)S(1)} %bitcast.16), channel_id=1, replica_groups={{0,1,2,3,32,33,34,35,64,65,66,67,96,97,98,99,128,129,130,131,160,161,16..., dimensions={0} | all-to-all | bytes 524288 | tf_op jit(solution)/shard_map/all_to_all | solution.py:45
  106.2 0.1 reduce_sum.12
  106.3 16.0 %all_to_all.21.both_ref = bf16[16,96,128]{2,1,0:T(8,128)(2,1)S(1)} all-to-all(bf16[16,96,128]{2,1,0:T(8,128)(2,1)S(1)} %pad_maximum_fusion), channel_id=1, replica_groups=mesh['seq'=16,'head'=16] {'head'}, dimensions={0} | all-to-all | bytes 786432 | tf_op jit(solution)/shard_map/all_to_all | solution.py:45
  122.3 0.9 last.1
  (2 shorter events, 0.0 us)
Async XLA Ops:
  0.6 26.7 %copy-start = (bf16[256,4,128]{2,1,0:T(4,128)(2,1)S(1)}, bf16[256,4,128]{2,1,0:T(4,128)(2,1)}, u32[]{:S(2)}) copy-start(bf16[256,4,128]{2,1,0:T(4,128)(2,1)} %param.10) | copy-start | bytes 786436
  0.6 26.7 %copy-start.1 = (f32[256,4]{0,1:T(4,128)S(1)}, f32[256,4]{0,1:T(4,128)}, u32[]{:S(2)}) copy-start(f32[256,4]{0,1:T(4,128)} %param.12) | copy-start | bytes 12292
  1.6 6.4 %collective-permute-start.7 = (bf16[704,128]{1,0:T(8,128)(2,1)S(1)}, bf16[704,128]{1,0:T(8,128)(2,1)S(1)}, u32[]{:S(2)}, u32[]{:S(2)}) collective-permute-start(bf16[704,128]{1,0:T(8,128)(2,1)S(1)} %pad_maximum_fusion.1.refs_1_.refs_3_), channel_id=1, source_target_pairs={{0,32},{16,48},{32,0},{48,16},{64,96},{80,112},{96,64},{112,80},{1... | collective-permute-start | bytes 540680 | tf_op jit(solution)/shard_map/ppermute | solution.py:33
  3.5 8.7 %collective-permute-start.1 = (bf16[704,128]{1,0:T(8,128)(2,1)S(1)}, bf16[704,128]{1,0:T(8,128)(2,1)S(1)}, u32[]{:S(2)}, u32[]{:S(2)}) collective-permute-start(bf16[704,128]{1,0:T(8,128)(2,1)S(1)} %pad_maximum_fusion.1.refs_1_.refs_3_), channel_id=1, source_target_pairs={{0,192},{16,208},{32,224},{48,240},{64,0},{80,16},{96,32},{112,48}... | collective-permute-start | bytes 540680 | tf_op jit(solution)/shard_map/ppermute | solution.py:29
  4.8 12.0 %collective-permute-start.3 = (bf16[704,128]{1,0:T(8,128)(2,1)S(1)}, bf16[704,128]{1,0:T(8,128)(2,1)S(1)}, u32[]{:S(2)}, u32[]{:S(2)}) collective-permute-start(bf16[704,128]{1,0:T(8,128)(2,1)S(1)} %pad_maximum_fusion.1.refs_1_.refs_3_), channel_id=1, source_target_pairs={{0,64},{16,80},{32,96},{48,112},{64,128},{80,144},{96,160},{112,17... | collective-permute-start | bytes 540680 | tf_op jit(solution)/shard_map/ppermute | solution.py:29
  5.5 12.3 %collective-permute-start.5 = (bf16[704,128]{1,0:T(8,128)(2,1)S(1)}, bf16[704,128]{1,0:T(8,128)(2,1)S(1)}, u32[]{:S(2)}, u32[]{:S(2)}) collective-permute-start(bf16[704,128]{1,0:T(8,128)(2,1)S(1)} %pad_maximum_fusion.1.refs_1_.refs_3_), channel_id=1, source_target_pairs={{0,128},{16,144},{32,160},{48,176},{64,192},{80,208},{96,224},{112... | collective-permute-start | bytes 540680 | tf_op jit(solution)/shard_map/ppermute | solution.py:29
  7.0 14.7 %collective-permute-start = (bf16[704,128]{1,0:T(8,128)(2,1)S(1)}, bf16[704,128]{1,0:T(8,128)(2,1)S(1)}, u32[]{:S(2)}, u32[]{:S(2)}) collective-permute-start(bf16[704,128]{1,0:T(8,128)(2,1)S(1)} %pad_maximum_fusion.1.refs_1_.refs_3_), channel_id=1, source_target_pairs={{0,16},{16,0},{32,48},{48,32},{64,80},{80,64},{96,112},{112,96},{1... | collective-permute-start | bytes 540680 | tf_op jit(solution)/shard_map/ppermute | solution.py:37
  8.0 15.8 %collective-permute-start.9 = (bf16[704,128]{1,0:T(8,128)(2,1)S(1)}, bf16[704,128]{1,0:T(8,128)(2,1)S(1)}, u32[]{:S(2)}, u32[]{:S(2)}) collective-permute-start(bf16[704,128]{1,0:T(8,128)(2,1)S(1)} %collective-permute-done.7.refs_9_.refs_11_), channel_id=1, source_target_pairs={{0,192},{16,208},{32,224},{48,240},{64,0},{80,16},{96,32},{112,48}... | collective-permute-start | bytes 540680 | tf_op jit(solution)/shard_map/ppermute | solution.py:29
  12.2 13.0 %collective-permute-start.11 = (bf16[704,128]{1,0:T(8,128)(2,1)S(1)}, bf16[704,128]{1,0:T(8,128)(2,1)S(1)}, u32[]{:S(2)}, u32[]{:S(2)}) collective-permute-start(bf16[704,128]{1,0:T(8,128)(2,1)S(1)} %collective-permute-done.7.refs_9_.refs_11_), channel_id=1, source_target_pairs={{0,64},{16,80},{32,96},{48,112},{64,128},{80,144},{96,160},{112,17... | collective-permute-start | bytes 540680 | tf_op jit(solution)/shard_map/ppermute | solution.py:29
  16.8 21.2 %collective-permute-start.13 = (bf16[704,128]{1,0:T(8,128)(2,1)S(1)}, bf16[704,128]{1,0:T(8,128)(2,1)S(1)}, u32[]{:S(2)}, u32[]{:S(2)}) collective-permute-start(bf16[704,128]{1,0:T(8,128)(2,1)S(1)} %collective-permute-done.7.refs_9_.refs_11_), channel_id=1, source_target_pairs={{0,128},{16,144},{32,160},{48,176},{64,192},{80,208},{96,224},{112... | collective-permute-start | bytes 540680 | tf_op jit(solution)/shard_map/ppermute | solution.py:29
  17.9 20.3 %collective-permute-start.8 = (bf16[704,128]{1,0:T(8,128)(2,1)S(1)}, bf16[704,128]{1,0:T(8,128)(2,1)S(1)}, u32[]{:S(2)}, u32[]{:S(2)}) collective-permute-start(bf16[704,128]{1,0:T(8,128)(2,1)S(1)} %collective-permute-done.7.refs_9_.refs_11_), channel_id=1, source_target_pairs={{0,16},{16,0},{32,48},{48,32},{64,80},{80,64},{96,112},{112,96},{1... | collective-permute-start | bytes 540680 | tf_op jit(solution)/shard_map/ppermute | solution.py:37
  21.7 24.0 %collective-permute-start.15 = (bf16[8,64,640]{2,1,0:T(8,128)(2,1)}, bf16[8,64,640]{2,1,0:T(8,128)(2,1)S(1)}, u32[]{:S(2)}, u32[]{:S(2)}) collective-permute-start(bf16[8,64,640]{2,1,0:T(8,128)(2,1)} %get-tuple-element.15), channel_id=1, source_target_pairs={{0,1},{1,2},{2,3},{3,0},{4,5},{5,6},{6,7},{7,4},{8,9},{9,10},{10,1... | collective-permute-start | bytes 1966088 | tf_op jit(solution)/shard_map/ppermute | solution.py:41
  23.8 32.6 %collective-permute-start.16 = (bf16[8,64,640]{2,1,0:T(8,128)(2,1)}, bf16[8,64,640]{2,1,0:T(8,128)(2,1)}, u32[]{:S(2)}, u32[]{:S(2)}) collective-permute-start(bf16[8,64,640]{2,1,0:T(8,128)(2,1)} %get-tuple-element.16), channel_id=1, source_target_pairs={{0,3},{1,0},{2,1},{3,2},{4,7},{5,4},{6,5},{7,6},{8,11},{9,8},{10,9... | collective-permute-start | bytes 1966088 | tf_op jit(solution)/shard_map/ppermute | solution.py:41
  25.2 34.1 %collective-permute-start.17 = (bf16[8,64,640]{2,1,0:T(8,128)(2,1)}, bf16[8,64,640]{2,1,0:T(8,128)(2,1)}, u32[]{:S(2)}, u32[]{:S(2)}) collective-permute-start(bf16[8,64,640]{2,1,0:T(8,128)(2,1)} %get-tuple-element.17), channel_id=1, source_target_pairs={{0,2},{1,3},{2,0},{3,1},{4,6},{5,7},{6,4},{7,5},{8,10},{9,11},{10,... | collective-permute-start | bytes 1966088 | tf_op jit(solution)/shard_map/ppermute | solution.py:41
  28.1 37.8 %all-to-all-start = ((bf16[16,80,128]{2,1,0:T(8,128)(2,1)}), bf16[16,80,128]{2,1,0:T(8,128)(2,1)S(1)}, u32[]{:S(2)}, u32[]{:S(2)}) async-start(bf16[16,80,128]{2,1,0:T(8,128)(2,1)} %pack.1), calls=%async_computation | async-start | bytes 655360 | tf_op jit(solution)/shard_map/all_to_all | solution.py:45
  38.1 1.5 %collective-permute-start.2 = (bf16[704,128]{1,0:T(8,128)(2,1)S(1)}, bf16[704,128]{1,0:T(8,128)(2,1)S(1)}, u32[]{:S(2)}, u32[]{:S(2)}) collective-permute-start(bf16[704,128]{1,0:T(8,128)(2,1)S(1)} %collective-permute-done.1.refs_3_.refs_5_), channel_id=1, source_target_pairs={{0,16},{16,0},{32,48},{48,32},{64,80},{80,64},{96,112},{112,96},{1... | collective-permute-start | bytes 540680 | tf_op jit(solution)/shard_map/ppermute | solution.py:37
  38.2 1.7 %collective-permute-start.4 = (bf16[704,128]{1,0:T(8,128)(2,1)S(1)}, bf16[704,128]{1,0:T(8,128)(2,1)S(1)}, u32[]{:S(2)}, u32[]{:S(2)}) collective-permute-start(bf16[704,128]{1,0:T(8,128)(2,1)S(1)} %collective-permute-done.3.refs_5_.refs_7_), channel_id=1, source_target_pairs={{0,16},{16,0},{32,48},{48,32},{64,80},{80,64},{96,112},{112,96},{1... | collective-permute-start | bytes 540680 | tf_op jit(solution)/shard_map/ppermute | solution.py:37
  39.6 1.4 %collective-permute-start.6 = (bf16[704,128]{1,0:T(8,128)(2,1)S(1)}, bf16[704,128]{1,0:T(8,128)(2,1)S(1)}, u32[]{:S(2)}, u32[]{:S(2)}) collective-permute-start(bf16[704,128]{1,0:T(8,128)(2,1)S(1)} %collective-permute-done.5.refs_7_.refs_9_), channel_id=1, source_target_pairs={{0,16},{16,0},{32,48},{48,32},{64,80},{80,64},{96,112},{112,96},{1... | collective-permute-start | bytes 540680 | tf_op jit(solution)/shard_map/ppermute | solution.py:37
  39.8 1.4 %collective-permute-start.10 = (bf16[704,128]{1,0:T(8,128)(2,1)S(1)}, bf16[704,128]{1,0:T(8,128)(2,1)S(1)}, u32[]{:S(2)}, u32[]{:S(2)}) collective-permute-start(bf16[704,128]{1,0:T(8,128)(2,1)S(1)} %collective-permute-done.9.refs_11_.refs_13_), channel_id=1, source_target_pairs={{0,16},{16,0},{32,48},{48,32},{64,80},{80,64},{96,112},{112,96},{1... | collective-permute-start | bytes 540680 | tf_op jit(solution)/shard_map/ppermute | solution.py:37
  41.0 1.4 %collective-permute-start.12 = (bf16[704,128]{1,0:T(8,128)(2,1)S(1)}, bf16[704,128]{1,0:T(8,128)(2,1)S(1)}, u32[]{:S(2)}, u32[]{:S(2)}) collective-permute-start(bf16[704,128]{1,0:T(8,128)(2,1)S(1)} %collective-permute-done.11.refs_13_.refs_15_), channel_id=1, source_target_pairs={{0,16},{16,0},{32,48},{48,32},{64,80},{80,64},{96,112},{112,96},{1... | collective-permute-start | bytes 540680 | tf_op jit(solution)/shard_map/ppermute | solution.py:37
  41.2 1.4 %collective-permute-start.14 = (bf16[704,128]{1,0:T(8,128)(2,1)S(1)}, bf16[704,128]{1,0:T(8,128)(2,1)S(1)}, u32[]{:S(2)}, u32[]{:S(2)}) collective-permute-start(bf16[704,128]{1,0:T(8,128)(2,1)S(1)} %collective-permute-done.13.refs_15_.refs_17_), channel_id=1, source_target_pairs={{0,16},{16,0},{32,48},{48,32},{64,80},{80,64},{96,112},{112,96},{1... | collective-permute-start | bytes 540680 | tf_op jit(solution)/shard_map/ppermute | solution.py:37
  59.2 15.1 %copy-start.2 = (s32[2,16]{1,0:T(2,128)S(1)}, s32[2,16]{1,0:T(2,128)}, u32[]{:S(2)}) copy-start(s32[2,16]{1,0:T(2,128)} %kept_ref.3) | copy-start | bytes 388
  65.9 18.6 %all-to-all-start.1 = ((bf16[4,16,2048]{2,1,0:T(8,128)(2,1)}), bf16[4,16,2048]{2,1,0:T(8,128)(2,1)S(1)}, u32[]{:S(2)}, u32[]{:S(2)}) async-start(bf16[4,16,2048]{2,1,0:T(8,128)(2,1)} %bitcast.10), calls=%async_computation.1 | async-start | bytes 524288 | tf_op jit(solution)/shard_map/all_to_all | solution.py:45
  88.3 1.6 %collective-permute-start.18 = (bf16[8,128,128]{2,1,0:T(8,128)(2,1)S(1)}, bf16[8,128,128]{2,1,0:T(8,128)(2,1)S(1)}, u32[]{:S(2)}, u32[]{:S(2)}) collective-permute-start(bf16[8,128,128]{2,1,0:T(8,128)(2,1)S(1)} %get-tuple-element.21), channel_id=1, source_target_pairs={{0,16},{16,0},{32,48},{48,32},{64,80},{80,64},{96,112},{112,96},{1... | collective-permute-start | bytes 786440 | tf_op jit(solution)/shard_map/ppermute | solution.py:37
